TPU v7x, 256 devices: a whole 4x4x8 slice. The times are simulated.
256 devices in a mesh: gx: 16 (over y, z_lo), gy: 16 (over x, z_hi, core).
Axes of the slice: x: 4, y: 4, z: 8 (z_hi: 2, z_lo: 4; z = z_hi * 4 + z_lo), core: 2. Of those that a mesh axis runs over, the one named last changes fastest.
Arguments:
- densities: bfloat16 [16, 16, 64, 8192], P('gx', 'gy'), may hold values from -6 to 6
- trials: bfloat16 [16, 16, 64, 256], P('gx', 'gy'), may hold values from -6 to 6
- energies: float32 [16, 16, 64, 8], P('gx', 'gy'), may hold values from 1 to 4
- metric: bfloat16 [1024, 1024], replicated, may hold values from -0.1875 to 0.1875
- pair_local: int32 [16, 16, 6912], P('gx', 'gy'), may hold values from 0 to 63
- pair_remote: int32 [16, 16, 6912], P('gx', 'gy'), may hold values from 0 to 63, as said below
- pair_scale: float32 [16, 16, 6912], P('gx', 'gy'), may hold values from 0.2 to 2
Outputs:
- sigma_first: float32 [16, 16, 64, 256], P('gx', 'gy')
- corrections: bfloat16 [16, 16, 64, 256], P('gx', 'gy')
- sigma_second: float32 [16, 16, 64, 256], P('gx', 'gy')
- theta: float32 [32], replicated
Inputs may be any that keep to these rules, and one draw needn't show every extreme that they name: pair_remote is below 63 in the slots of the bin's own block (p // 768 = 4); in the other slots it takes every value up to 63.
All inputs are finite; a program needn't handle non-finite values.
Results may differ from a plain program's by a relative error of at most 0.0057.
Values may be sent and summed in bfloat16 or wider, within the bound.
No kernel may reach another device: no remote copies, remote signals or barrier semaphores. Data moves between devices by JAX's collectives and lax.ppermute only.
A program may use at most 128 MiB of HBM per device.

v0:
```python
import jax
import jax.numpy as jnp
from jax import lax
from jax.sharding import PartitionSpec as P


def extended(block, sides, width):
    for axis, dim in sides:
        count = lax.axis_size(axis)
        forward = [(i, i + 1) for i in range(count - 1)]
        forward.append((count - 1, 0))
        backward = [(target, source) for source, target in forward]
        low = lax.ppermute(
            lax.slice_in_dim(block, block.shape[dim] - width, None, axis=dim), axis, forward
        )
        high = lax.ppermute(lax.slice_in_dim(block, 0, width, axis=dim), axis, backward)
        block = jnp.concatenate([low, block, high], axis=dim)
    return block


def shards(densities, trials, energies, metric, pair_local, pair_remote, pair_scale):
    mols = densities.shape[2]
    states = energies.shape[3]
    aux = metric.shape[0]
    vecs = trials.shape[3] // states
    pairs = pair_local.shape[2]
    cap = pairs // 9
    width = mols * states
    halo_rho, halo_trial = (
        extended(densities, (("gx", 0), ("gy", 1)), 1),
        extended(trials, (("gx", 0), ("gy", 1)), 1),
    )
    local = pair_local[0, 0]
    owner = jnp.arange(pairs, dtype=jnp.int32) // cap
    inner = jnp.where(owner == 4, (local + 1 + pair_remote[0, 0]) % mols, pair_remote[0, 0])
    molecule_ids = jnp.arange(mols, dtype=jnp.int32)
    own_onehot = (local[:, None] == molecule_ids[None, :]).astype(jnp.float32)
    far_onehot = (inner[:, None] == molecule_ids[None, :]).astype(jnp.float32)
    scaled_own = own_onehot * pair_scale[0, 0][:, None]
    weights = jnp.einsum(
        "opi,opj->oij",
        scaled_own.reshape(9, cap, mols),
        far_onehot.reshape(9, cap, mols),
        precision=lax.Precision.HIGHEST,
    )
    weights = weights / jnp.sqrt(jnp.float32(aux))
    proj = jnp.dot(densities.reshape(width, aux), metric, preferred_element_type=jnp.float32)
    proj = proj.astype(jnp.bfloat16)
    near_rho = halo_rho.reshape(9, width, aux)

    def couple(items):
        far_block, weight = items
        dense = lax.dot_general(
            proj, far_block, (((1,), (1,)), ((), ())), preferred_element_type=jnp.float32
        )
        dense = dense.reshape(mols, states, mols, states) * weight[:, None, :, None]
        return dense.reshape(width, width)

    coupled = lax.map(couple, (near_rho, weights))
    energy = energies[0, 0]

    def matvec(halo_field, own):
        near = halo_field.reshape(9, width, vecs).astype(jnp.float32)
        summed = jnp.einsum("oxy,oyv->xv", coupled, near, precision=lax.Precision.HIGHEST)
        return summed.reshape(mols, states, vecs) + energy[:, :, None] * own

    start_vecs = trials[0, 0].astype(jnp.float32).reshape(mols, states, vecs)
    sigma_first = matvec(halo_trial, start_vecs)
    numer, denom = lax.psum(
        (
            jnp.sum(start_vecs * sigma_first, axis=(0, 1)),
            jnp.sum(start_vecs * start_vecs, axis=(0, 1)),
        ),
        ("gx", "gy"),
    )
    theta = numer / denom
    resid = (sigma_first - theta * start_vecs) / jnp.maximum(
        jnp.abs(energy[:, :, None] - theta), 1.0
    )
    total_sq = lax.psum(jnp.sum(resid * resid, axis=(0, 1)), ("gx", "gy"))
    count = mols * states * lax.axis_size("gx") * lax.axis_size("gy")
    corrections = (resid / jnp.sqrt(total_sq / count + 1e-06)).astype(jnp.bfloat16)
    shaped = corrections.reshape(1, 1, mols, states * vecs)
    halo_corr = extended(shaped, (("gx", 0), ("gy", 1)), 1)
    sigma_second = matvec(halo_corr, corrections.astype(jnp.float32))
    out_shape = (1, 1, mols, states * vecs)
    return (sigma_first.reshape(out_shape), shaped, sigma_second.reshape(out_shape), theta)


def solution(mesh):
    return jax.shard_map(
        shards,
        mesh=mesh,
        in_specs=(
            P("gx", "gy", None, None),
            P("gx", "gy", None, None),
            P("gx", "gy", None, None),
            P(),
            P("gx", "gy", None),
            P("gx", "gy", None),
            P("gx", "gy", None),
        ),
        out_specs=(
            P("gx", "gy", None, None),
            P("gx", "gy", None, None),
            P("gx", "gy", None, None),
            P(),
        ),
        check_vma=False,
    )
```

profile of v0, /device:TPU:24, one launch (start us, length us, event | category | flops | bytes accessed | tf_op | source)
XLA Modules:
  0.0 647.2 jit_solution(13449455259553608656)
XLA Ops:
  5.6 24.2 %collective-permute-done = bf16[1,1,64,8192]{3,2,1,0:T(8,128)(2,1)S(1)} collective-permute-done((bf16[1,1,64,8192]{3,2,1,0:T(8,128)(2,1)}, bf16[1,1,64,8192]{3,2,1,0:T(8,128)(2,1)S(1)}, u32[]{:S(2)}, u32[]{:S(2)}) %collective-permute-start) | collective-permute-done | bytes 1048608 | tf_op jit(solution)/shard_map/ppermute | solution.py:13
  33.1 17.0 %collective-permute-done.1 = bf16[1,1,64,8192]{3,2,1,0:T(8,128)(2,1)S(1)} collective-permute-done((bf16[1,1,64,8192]{3,2,1,0:T(8,128)(2,1)}, bf16[1,1,64,8192]{3,2,1,0:T(8,128)(2,1)S(1)}, u32[]{:S(2)}, u32[]{:S(2)}) %collective-permute-start.1) | collective-permute-done | bytes 1048608 | tf_op jit(solution)/shard_map/ppermute | solution.py:16
  71.5 125.9 %collective-permute-done.4 = bf16[1,1,64,256]{3,2,1,0:T(8,128)(2,1)} collective-permute-done((bf16[1,1,64,256]{3,2,1,0:T(8,128)(2,1)S(1)}, bf16[1,1,64,256]{3,2,1,0:T(8,128)(2,1)}, u32[]{:S(2)}, u32[]{:S(2)}) %collective-permute-start.4) | collective-permute-done | bytes 32800 | tf_op jit(solution)/shard_map/ppermute | solution.py:13
  211.8 9.3 %pad_maximum_fusion = bf16[3,3,64,8192]{3,2,1,0:T(8,128)(2,1)} fusion(bf16[3,1,64,8192]{3,2,1,0:T(8,128)(2,1)} %collective-permute-done.3, bf16[3,1,64,8192]{3,2,1,0:T(8,128)(2,1)} %constant_dynamic-update-slice_fusion.1, bf16[3,1,64,8192]{3,2,1,0:T(8,128)(2,1)} %collective-permute-done.2), kind=kLoop, calls=%fused_computation.8 | loop fusion | flops 9437184 | bytes 18874368 | tf_op jit(solution)/shard_map/concatenate | solution.py:17
  221.1 15.0 %reshape.118 = bf16[9,512,1024]{2,1,0:T(8,128)(2,1)} reshape(bf16[3,3,64,8192]{3,2,1,0:T(8,128)(2,1)} %pad_maximum_fusion) | data formatting | bytes 18874368 | tf_op jit(solution)/shard_map/reshape | solution.py:49
  236.1 218.5 %while.10 = (s32[]{:T(128)}, f32[9,512,512]{2,1,0:T(8,128)}, bf16[9,512,1024]{2,1,0:T(8,128)(2,1)}, bf16[512,1024]{1,0:T(8,128)(2,1)S(1)}, f32[9,64,64]{2,1,0:T(8,128)S(1)}, /*index=5*/s32[]{:T(128)}) while((s32[]{:T(128)}, f32[9,512,512]{2,1,0:T(8,128)}, bf16[9,512,1024]{2,1,0:T(8,128)(2,1)}, bf16[512,1024]{1,0:T(8,128)(2,1)S(1)}, ...), condition=%wide.region_1.2_spmd, body=%wide.region_0.1_spmd.sunk | while | flops 537133056 | bytes 13681737 | solution.py:59
  236.1 7.9 %mul.110 = f32[64,8,64,8]{3,2,1,0:T(8,128)} broadcast(f32[64,64]{1,0:T(8,128)S(1)} %dynamic-slice_bitcast_fusion.2), dimensions={0,2} | broadcast | bytes 1064960 | tf_op jit(solution)/shard_map/while/body/eval_jaxpr/mul | solution.py:56
  244.0 12.6 %mul.111 = f32[512,512]{1,0:T(8,128)S(1)} reshape(f32[64,8,64,8]{3,2,1,0:T(8,128)} %mul.110) | data formatting | bytes 2097152 | tf_op jit(solution)/shard_map/while/body/eval_jaxpr/mul | solution.py:56
  260.4 7.9 %mul.110 = f32[64,8,64,8]{3,2,1,0:T(8,128)} broadcast(f32[64,64]{1,0:T(8,128)S(1)} %dynamic-slice_bitcast_fusion.2), dimensions={0,2} | broadcast | bytes 1064960 | tf_op jit(solution)/shard_map/while/body/eval_jaxpr/mul | solution.py:56
  268.3 12.6 %mul.111 = f32[512,512]{1,0:T(8,128)S(1)} reshape(f32[64,8,64,8]{3,2,1,0:T(8,128)} %mul.110) | data formatting | bytes 2097152 | tf_op jit(solution)/shard_map/while/body/eval_jaxpr/mul | solution.py:56
  284.7 7.9 %mul.110 = f32[64,8,64,8]{3,2,1,0:T(8,128)} broadcast(f32[64,64]{1,0:T(8,128)S(1)} %dynamic-slice_bitcast_fusion.2), dimensions={0,2} | broadcast | bytes 1064960 | tf_op jit(solution)/shard_map/while/body/eval_jaxpr/mul | solution.py:56
  292.6 12.6 %mul.111 = f32[512,512]{1,0:T(8,128)S(1)} reshape(f32[64,8,64,8]{3,2,1,0:T(8,128)} %mul.110) | data formatting | bytes 2097152 | tf_op jit(solution)/shard_map/while/body/eval_jaxpr/mul | solution.py:56
  308.9 7.9 %mul.110 = f32[64,8,64,8]{3,2,1,0:T(8,128)} broadcast(f32[64,64]{1,0:T(8,128)S(1)} %dynamic-slice_bitcast_fusion.2), dimensions={0,2} | broadcast | bytes 1064960 | tf_op jit(solution)/shard_map/while/body/eval_jaxpr/mul | solution.py:56
  316.9 12.6 %mul.111 = f32[512,512]{1,0:T(8,128)S(1)} reshape(f32[64,8,64,8]{3,2,1,0:T(8,128)} %mul.110) | data formatting | bytes 2097152 | tf_op jit(solution)/shard_map/while/body/eval_jaxpr/mul | solution.py:56
  333.2 7.9 %mul.110 = f32[64,8,64,8]{3,2,1,0:T(8,128)} broadcast(f32[64,64]{1,0:T(8,128)S(1)} %dynamic-slice_bitcast_fusion.2), dimensions={0,2} | broadcast | bytes 1064960 | tf_op jit(solution)/shard_map/while/body/eval_jaxpr/mul | solution.py:56
  341.1 12.6 %mul.111 = f32[512,512]{1,0:T(8,128)S(1)} reshape(f32[64,8,64,8]{3,2,1,0:T(8,128)} %mul.110) | data formatting | bytes 2097152 | tf_op jit(solution)/shard_map/while/body/eval_jaxpr/mul | solution.py:56
  365.4 12.6 %mul.111 = f32[512,512]{1,0:T(8,128)S(1)} reshape(f32[64,8,64,8]{3,2,1,0:T(8,128)} %mul.110) | data formatting | bytes 2097152 | tf_op jit(solution)/shard_map/while/body/eval_jaxpr/mul | solution.py:56
  389.6 12.6 %mul.111 = f32[512,512]{1,0:T(8,128)S(1)} reshape(f32[64,8,64,8]{3,2,1,0:T(8,128)} %mul.110) | data formatting | bytes 2097152 | tf_op jit(solution)/shard_map/while/body/eval_jaxpr/mul | solution.py:56
  413.9 12.6 %mul.111 = f32[512,512]{1,0:T(8,128)S(1)} reshape(f32[64,8,64,8]{3,2,1,0:T(8,128)} %mul.110) | data formatting | bytes 2097152 | tf_op jit(solution)/shard_map/while/body/eval_jaxpr/mul | solution.py:56
  438.2 12.6 %mul.111 = f32[512,512]{1,0:T(8,128)S(1)} reshape(f32[64,8,64,8]{3,2,1,0:T(8,128)} %mul.110) | data formatting | bytes 2097152 | tf_op jit(solution)/shard_map/while/body/eval_jaxpr/mul | solution.py:56
  454.6 8.1 %fusion.16 = f32[64,8,32]{2,1,0:T(8,128)S(1)} fusion(bf16[9,512,32]{2,1,0:T(8,128)(2,1)} %reshape.120, f32[9,512,512]{2,1,0:T(8,128)} %get-tuple-element.31), kind=kOutput, calls=%fused_computation.21 | convolution fusion | flops 905969664 | bytes 9797632 | tf_op jit(solution)/shard_map/oxy,oyv->xv/dot_general | solution.py:64
  463.0 75.8 %all-reduce = (f32[32]{0:T(128)S(1)}, f32[32]{0:T(128)S(1)}) all-reduce(f32[32]{0:T(128)S(1)} %get-tuple-element.61, f32[32]{0:T(128)S(1)} %reduce_sum.37), channel_id=1, replica_groups=mesh['gx'=16,'gy'=16] {'gx','gy'}, use_global_device_ids=true, to_apply=%region_3.4 | all-reduce | flops 64 | bytes 512 | tf_op jit(solution)/shard_map/psum | solution.py:69
  539.0 74.5 %psum.23 = f32[32]{0:T(128)S(1)} all-reduce(f32[32]{0:T(128)S(1)} %multiply_reduce_fusion), channel_id=1, replica_groups=mesh['gx'=16,'gy'=16] {'gx','gy'}, use_global_device_ids=true, to_apply=%region_8.9 | all-reduce | flops 32 | bytes 256 | tf_op jit(solution)/shard_map/psum | solution.py:80
  636.7 8.7 %fusion.21 = f32[64,8,32]{2,1,0:T(8,128)} fusion(bf16[9,512,32]{2,1,0:T(8,128)(2,1)S(1)} %reshape.123, f32[9,512,512]{2,1,0:T(8,128)} %get-tuple-element.31), kind=kOutput, calls=%fused_computation.22 | convolution fusion | flops 905969664 | bytes 9797632 | tf_op jit(solution)/shard_map/oxy,oyv->xv/dot_general | solution.py:64
  (128 shorter events, 134.4 us)
Async XLA Ops:
  0.6 66.9 %copy-start = (bf16[1024,1024]{1,0:T(8,128)(2,1)S(1)}, bf16[1024,1024]{1,0:T(8,128)(2,1)}, u32[]{:S(2)}) copy-start(bf16[1024,1024]{1,0:T(8,128)(2,1)} %param.12) | copy-start | bytes 6291460
  0.6 64.6 %copy-start.2 = (bf16[1,1,64,8192]{3,2,1,0:T(8,128)(2,1)S(1)}, bf16[1,1,64,8192]{3,2,1,0:T(8,128)(2,1)}, u32[]{:S(2)}) copy-start(bf16[1,1,64,8192]{3,2,1,0:T(8,128)(2,1)} %param.9) | copy-start | bytes 3145732
  0.7 58.3 %copy-start.3 = (bf16[1,1,64,256]{3,2,1,0:T(8,128)(2,1)S(1)}, bf16[1,1,64,256]{3,2,1,0:T(8,128)(2,1)}, u32[]{:S(2)}) copy-start(bf16[1,1,64,256]{3,2,1,0:T(8,128)(2,1)} %param.10) | copy-start | bytes 98308
  0.7 29.1 %collective-permute-start = (bf16[1,1,64,8192]{3,2,1,0:T(8,128)(2,1)}, bf16[1,1,64,8192]{3,2,1,0:T(8,128)(2,1)S(1)}, u32[]{:S(2)}, u32[]{:S(2)}) collective-permute-start(bf16[1,1,64,8192]{3,2,1,0:T(8,128)(2,1)} %param.9), channel_id=1, source_target_pairs={{0,16},{16,32},{32,48},{48,64},{64,80},{80,96},{96,112},{112,128},... | collective-permute-start | bytes 3145736 | tf_op jit(solution)/shard_map/ppermute | solution.py:13
  2.7 47.5 %collective-permute-start.1 = (bf16[1,1,64,8192]{3,2,1,0:T(8,128)(2,1)}, bf16[1,1,64,8192]{3,2,1,0:T(8,128)(2,1)S(1)}, u32[]{:S(2)}, u32[]{:S(2)}) collective-permute-start(bf16[1,1,64,8192]{3,2,1,0:T(8,128)(2,1)} %param.9), channel_id=1, source_target_pairs={{16,0},{32,16},{48,32},{64,48},{80,64},{96,80},{112,96},{128,112},... | collective-permute-start | bytes 3145736 | tf_op jit(solution)/shard_map/ppermute | solution.py:16
  30.9 35.7 %copy-start.6 = (s32[1,1,6912]{2,1,0:T(1,128)S(1)}, s32[1,1,6912]{2,1,0:T(1,128)}, u32[]{:S(2)}) copy-start(s32[1,1,6912]{2,1,0:T(1,128)} %param.13) | copy-start | bytes 82948
  30.9 35.8 %copy-start.7 = (s32[1,1,6912]{2,1,0:T(1,128)S(1)}, s32[1,1,6912]{2,1,0:T(1,128)}, u32[]{:S(2)}) copy-start(s32[1,1,6912]{2,1,0:T(1,128)} %param.14) | copy-start | bytes 82948
  30.9 35.9 %copy-start.8 = (f32[1,1,6912]{2,1,0:T(1,128)S(1)}, f32[1,1,6912]{2,1,0:T(1,128)}, u32[]{:S(2)}) copy-start(f32[1,1,6912]{2,1,0:T(1,128)} %param.15) | copy-start | bytes 82948
  51.2 160.6 %collective-permute-start.2 = (bf16[3,1,64,8192]{3,2,1,0:T(8,128)(2,1)}, bf16[3,1,64,8192]{3,2,1,0:T(8,128)(2,1)}, u32[]{:S(2)}, u32[]{:S(2)}) collective-permute-start(bf16[3,1,64,8192]{3,2,1,0:T(8,128)(2,1)} %constant_dynamic-update-slice_fusion.1), channel_id=1, source_target_pairs={{0,1},{1,2},{2,3},{3,4},{4,5},{5,6},{6,7},{7,8},{8,9},{9,10},{10,1... | collective-permute-start | bytes 9437192 | tf_op jit(solution)/shard_map/ppermute | solution.py:13
  51.2 160.6 %collective-permute-start.3 = (bf16[3,1,64,8192]{3,2,1,0:T(8,128)(2,1)}, bf16[3,1,64,8192]{3,2,1,0:T(8,128)(2,1)}, u32[]{:S(2)}, u32[]{:S(2)}) collective-permute-start(bf16[3,1,64,8192]{3,2,1,0:T(8,128)(2,1)} %constant_dynamic-update-slice_fusion.1), channel_id=1, source_target_pairs={{1,0},{2,1},{3,2},{4,3},{5,4},{6,5},{7,6},{8,7},{9,8},{10,9},{11,1... | collective-permute-start | bytes 9437192 | tf_op jit(solution)/shard_map/ppermute | solution.py:16
  59.0 138.5 %collective-permute-start.4 = (bf16[1,1,64,256]{3,2,1,0:T(8,128)(2,1)S(1)}, bf16[1,1,64,256]{3,2,1,0:T(8,128)(2,1)}, u32[]{:S(2)}, u32[]{:S(2)}) collective-permute-start(bf16[1,1,64,256]{3,2,1,0:T(8,128)(2,1)S(1)} %copy-done.3), channel_id=1, source_target_pairs={{0,16},{16,32},{32,48},{48,64},{64,80},{80,96},{96,112},{112,128},... | collective-permute-start | bytes 98312 | tf_op jit(solution)/shard_map/ppermute | solution.py:13
  62.0 136.3 %collective-permute-start.5 = (bf16[1,1,64,256]{3,2,1,0:T(8,128)(2,1)S(1)}, bf16[1,1,64,256]{3,2,1,0:T(8,128)(2,1)}, u32[]{:S(2)}, u32[]{:S(2)}) collective-permute-start(bf16[1,1,64,256]{3,2,1,0:T(8,128)(2,1)S(1)} %copy-done.3), channel_id=1, source_target_pairs={{16,0},{32,16},{48,32},{64,48},{80,64},{96,80},{112,96},{128,112},... | collective-permute-start | bytes 98312 | tf_op jit(solution)/shard_map/ppermute | solution.py:16
  67.6 2.5 copy-start.5
  199.0 11.2 %collective-permute-start.6 = (bf16[3,1,64,256]{3,2,1,0:T(8,128)(2,1)S(1)}, bf16[3,1,64,256]{3,2,1,0:T(8,128)(2,1)S(1)}, u32[]{:S(2)}, u32[]{:S(2)}) collective-permute-start(bf16[3,1,64,256]{3,2,1,0:T(8,128)(2,1)S(1)} %constant_dynamic-update-slice_fusion.4), channel_id=1, source_target_pairs={{0,1},{1,2},{2,3},{3,4},{4,5},{5,6},{6,7},{7,8},{8,9},{9,10},{10,1... | collective-permute-start | bytes 294920 | tf_op jit(solution)/shard_map/ppermute | solution.py:13
  199.0 11.2 %collective-permute-start.7 = (bf16[3,1,64,256]{3,2,1,0:T(8,128)(2,1)S(1)}, bf16[3,1,64,256]{3,2,1,0:T(8,128)(2,1)S(1)}, u32[]{:S(2)}, u32[]{:S(2)}) collective-permute-start(bf16[3,1,64,256]{3,2,1,0:T(8,128)(2,1)S(1)} %constant_dynamic-update-slice_fusion.4), channel_id=1, source_target_pairs={{1,0},{2,1},{3,2},{4,3},{5,4},{6,5},{7,6},{8,7},{9,8},{10,9},{11,1... | collective-permute-start | bytes 294920 | tf_op jit(solution)/shard_map/ppermute | solution.py:16
  454.6 8.3 %copy-start.4 = (f32[1,1,64,8]{2,3,1,0:T(8,128)S(1)}, f32[1,1,64,8]{2,3,1,0:T(8,128)}, u32[]{:S(2)}) copy-start(f32[1,1,64,8]{2,3,1,0:T(8,128)} %param.11) | copy-start | bytes 6148
  538.8 106.6 %copy-start.9 = (f32[32]{0:T(128)}, f32[32]{0:T(128)S(1)}, u32[]{:S(2)}) copy-start(f32[32]{0:T(128)S(1)} %div.39) | copy-start | bytes 388
  613.7 7.5 %collective-permute-start.8 = (bf16[1,1,64,256]{2,3,1,0:T(8,128)(2,1)S(1)}, bf16[1,1,64,256]{2,3,1,0:T(8,128)(2,1)S(1)}, u32[]{:S(2)}, u32[]{:S(2)}) collective-permute-start(bf16[1,1,64,256]{2,3,1,0:T(8,128)(2,1)S(1)} %bitcast.72), channel_id=1, source_target_pairs={{0,16},{16,32},{32,48},{48,64},{64,80},{80,96},{96,112},{112,128},... | collective-permute-start | bytes 98312 | tf_op jit(solution)/shard_map/ppermute | solution.py:13
  614.9 6.4 collective-permute-start.9
  621.3 14.5 %collective-permute-start.10 = (bf16[3,1,64,256]{2,3,1,0:T(8,128)(2,1)S(1)}, bf16[3,1,64,256]{2,3,1,0:T(8,128)(2,1)S(1)}, u32[]{:S(2)}, u32[]{:S(2)}) collective-permute-start(bf16[3,1,64,256]{2,3,1,0:T(8,128)(2,1)S(1)} %pad_maximum_fusion.3), channel_id=1, source_target_pairs={{0,1},{1,2},{2,3},{3,4},{4,5},{5,6},{6,7},{7,8},{8,9},{9,10},{10,1... | collective-permute-start | bytes 294920 | tf_op jit(solution)/shard_map/ppermute | solution.py:13
  621.4 14.4 %collective-permute-start.11 = (bf16[3,1,64,256]{2,3,1,0:T(8,128)(2,1)S(1)}, bf16[3,1,64,256]{2,3,1,0:T(8,128)(2,1)S(1)}, u32[]{:S(2)}, u32[]{:S(2)}) collective-permute-start(bf16[3,1,64,256]{2,3,1,0:T(8,128)(2,1)S(1)} %pad_maximum_fusion.3), channel_id=1, source_target_pairs={{1,0},{2,1},{3,2},{4,3},{5,4},{6,5},{7,6},{8,7},{9,8},{10,9},{11,1... | collective-permute-start | bytes 294920 | tf_op jit(solution)/shard_map/ppermute | solution.py:16
  636.7 10.5 %copy-start.1 = (bf16[1024,1024]{1,0:T(8,128)(2,1)S(1)}, bf16[1024,1024]{1,0:T(8,128)(2,1)}, u32[]{:S(2)}) copy-start(bf16[1024,1024]{1,0:T(8,128)(2,1)} %param.12) | copy-start | bytes 6291460
where the time goes:
time: 654 us; the launch traced here: 647 us
  local copies, waits for them, and re-layouts  229 us (35%)
  waiting for transfers between devices  178 us (27%)
  blocking collectives  150 us (23%)
  starting transfers between devices  39.6 us (6%)
  matrix products  38.4 us (6%)
  other arithmetic  10.5 us (2%)
    mul x36, local copies, waits for them, and re-layouts, couple(): dense = dense.reshape(mols, states, mols, states) * weight[:, None, :, None]  188 us
    ppermute x6, waiting for transfers between devices, extended(): lax.ppermute(lax.slice_in_dim(block, block.shape[dim] - width, None, axis...  161 us
    psum x1, blocking collectives, shards(): lax.psum((jnp.sum(start_vecs * sigma_first, axis=(0, 1)), jnp.sum(start_v...  75.8 us
    psum x1, blocking collectives, shards(): total_sq = lax.psum(jnp.sum(resid * resid, axis=(0, 1)), ('gx', 'gy'))  74.5 us
    ppermute x6, starting transfers between devices, extended(): lax.ppermute(lax.slice_in_dim(block, 0, width, axis=dim), axis, backward)  33.4 us
    dot_general x9, matrix products, couple(): lax.dot_general(proj, far_block, (((1,), (1,)), ((), ())), preferred_elem...  17.7 us
    ppermute x6, waiting for transfers between devices, extended(): lax.ppermute(lax.slice_in_dim(block, 0, width, axis=dim), axis, backward)  17 us
    dot_general x2, matrix products, matvec(): jnp.einsum('oxy,oyv->xv', coupled, near, precision=lax.Precision.HIGHEST)  16.8 us
  transfers between devices with their start and end apart: 12, of which 6 were waited for; matrix products, arithmetic and copies ran while one was open for 2% of the time, Pallas kernels for 0%

commit v1 on v0

v1 whole, which is shorter than its diff:
```python
import functools

import jax
import jax.numpy as jnp
from jax import lax
from jax.experimental import pallas as pl
from jax.experimental.pallas import tpu as pltpu
from jax.sharding import PartitionSpec as P

BF = jnp.bfloat16
F32 = jnp.float32
AXES = ("gx", "gy")
SELF, TO_R, TO_U, TO_UR = 4, 7, 5, 8
R_TO_A, R_TO_U, U_TO_A, U_TO_R, UR_TO_A = 1, 2, 3, 6, 0


def vmem(count):
    return [pl.BlockSpec(memory_space=pltpu.VMEM)] * count


def call(body, outs, flops, moved):
    return lambda *args: pl.pallas_call(
        body,
        out_shape=outs,
        in_specs=vmem(len(args)),
        out_specs=jax.tree.map(lambda _: pl.BlockSpec(memory_space=pltpu.VMEM), outs),
        compiler_params=pltpu.CompilerParams(vmem_limit_bytes=60 * 2**20),
        cost_estimate=pl.CostEstimate(flops=flops, bytes_accessed=moved, transcendentals=0),
    )(*args)


def shape(*dims, dtype=F32):
    return jax.ShapeDtypeStruct(dims, dtype)


def stack(ref, states):
    width = ref.shape[1] // states
    return jnp.concatenate([ref[:, a * width : (a + 1) * width] for a in range(states)], axis=0)


def unstack(value, states):
    mols = value.shape[0] // states
    return jnp.concatenate([value[a * mols : (a + 1) * mols] for a in range(states)], axis=1)


def dot_nt(a, b):
    return lax.dot_general(a, b, (((1,), (1,)), ((), ())), preferred_element_type=F32)


def dot(a, b):
    return jnp.dot(a, b, preferred_element_type=F32)


def twice(w):
    return jnp.concatenate([w, w], axis=1)


def couple(proj, rho, pair):
    dense = dot_nt(proj, rho)
    tiles = (dense.shape[0] // pair.shape[0], dense.shape[1] // pair.shape[1])
    return (dense * jnp.tile(pair, tiles)).astype(BF)


def spread(e, width):
    mols, states = e.shape
    lane = lax.broadcasted_iota(jnp.int32, (mols, states * width), 1) // width
    out = jnp.zeros((mols, states * width), F32)
    for a in range(states):
        out = jnp.where(lane == a, e[:, a : a + 1], out)
    return out


def weights_body(scale, loc, rem, sc, y, e, own, msg):
    mols = y.shape[0]
    cap = loc.shape[1] // 9
    mol = lax.broadcasted_iota(jnp.int32, (mols, cap), 0)

    def weight(o):
        part = slice(o * cap, (o + 1) * cap)
        left, right, factor = loc[:, part], rem[:, part], sc[:, part] * scale
        if o == 4:
            right = left + 1 + right
            right = jnp.where(right >= mols, right - mols, right)
        mine = jnp.where(mol == left, factor, 0.0)
        far = jnp.where(mol == right, 1.0, 0.0).astype(BF)
        high = mine.astype(BF)
        rest = mine - high.astype(F32)
        mid = rest.astype(BF)
        low = (rest - mid.astype(F32)).astype(BF)
        three = dot_nt(
            jnp.concatenate([high, mid, low], axis=0), jnp.concatenate([far, far], axis=0)
        )
        return three[:mols] + (three[mols : 2 * mols] + three[2 * mols :])

    for k, o in enumerate((SELF, TO_R, TO_U, TO_UR)):
        own[k] = weight(o)
    field = y.shape[1]
    for k, (o, q) in enumerate(((R_TO_A, R_TO_U), (U_TO_A, U_TO_R), (UR_TO_A, None))):
        first = weight(o)
        if q is not None:
            lane = lax.broadcasted_iota(jnp.int32, first.shape, 1)
            first = jnp.where(lane < mols, first, weight(q))
        msg[k, :, :field] = y[...].astype(F32)
        msg[k, :, field : field + 2 * mols] = first
        msg[k, :, field + 2 * mols :] = jnp.concatenate(
            [e[...], jnp.zeros((mols, 2 * mols - e.shape[1]), F32)], axis=1
        )


def self_body(states, rho, metric, own, proj, c_aa):
    rows = stack(rho, states)
    proj[...] = dot(rows, metric[...]).astype(BF)
    c_aa[...] = couple(proj[...], rows, own[0])


def right_body(states, rho_a, rho_r, metric, proj_a, own, msg_r, proj_r, c):
    mols = rho_a.shape[0]
    rows_a, rows_r = stack(rho_a, states), stack(rho_r, states)
    field = msg_r.shape[1] - 4 * mols
    c[0] = couple(proj_a[...], rows_r, own[1])
    proj_r[...] = dot(rows_r, metric[...]).astype(BF)
    c[1] = couple(proj_r[...], rows_a, twice(msg_r[:, field : field + mols]))


def up_body(
    states, rho_a, rho_r, rho_u, metric, proj_a, proj_r, own, msg_r, msg_u, c_aa, c_r, y_a, c, sig
):
    mols = rho_a.shape[0]
    field = msg_r.shape[1] - 4 * mols
    rows_u = stack(rho_u, states)
    c[0] = couple(proj_a[...], rows_u, own[2])
    c[1] = couple(proj_r[...], rows_u, twice(msg_r[:, field + mols : field + 2 * mols]))
    proj_u = dot(rows_u, metric[...]).astype(BF)
    c[2] = couple(proj_u, stack(rho_a, states), twice(msg_u[:, field : field + mols]))
    c[3] = couple(
        proj_u, stack(rho_r, states), twice(msg_u[:, field + mols : field + 2 * mols])
    )
    f_a = stack(y_a, states)
    f_r = stack(msg_r[:, :field], states).astype(BF)
    f_u = stack(msg_u[:, :field], states).astype(BF)
    sig[0] = dot(c_aa[...], f_a) + (dot(c_r[0], f_r) + dot(c[0], f_u))
    sig[1] = dot(c_r[1], f_a) + dot(c[1], f_u)
    sig[2] = dot(c[2], f_a) + dot(c[3], f_r)


def corner_body(
    states, rho_a, rho_c, metric, proj_a, own, msg_r, msg_u, msg_c, y_a, e_a, sig, c, parts, sums
):
    mols = rho_a.shape[0]
    field = msg_r.shape[1] - 4 * mols
    rows_c = stack(rho_c, states)
    c[0] = couple(proj_a[...], rows_c, own[3])
    proj_c = dot(rows_c, metric[...]).astype(BF)
    c[1] = couple(proj_c, stack(rho_a, states), twice(msg_c[:, field : field + mols]))
    f_a = stack(y_a, states)
    f_c = stack(msg_c[:, :field], states).astype(BF)
    own_y = y_a[...].astype(F32)
    part_a = unstack(sig[0] + dot(c[0], f_c), states)
    part_a = part_a + spread(e_a[...], field // states) * own_y
    part_r = unstack(sig[1], states)
    part_u = unstack(sig[2], states)
    part_c = unstack(dot(c[1], f_a), states)
    parts[0], parts[1], parts[2], parts[3] = part_a, part_r, part_u, part_c
    total = part_a * own_y + part_r * msg_r[:, :field]
    total = total + (part_u * msg_u[:, :field] + part_c * msg_c[:, :field])
    sums[0:1] = jnp.sum(total, axis=0, keepdims=True)
    sums[1:2] = jnp.sum(own_y * own_y, axis=0, keepdims=True)


def over_states(row, width):
    states = row.shape[1] // width
    total = row[:, :width]
    for a in range(1, states):
        total = total + row[:, a * width : (a + 1) * width]
    return jnp.concatenate([total] * states, axis=1)


def residual(sigma, y, e, theta, width):
    return (sigma - theta * y) / jnp.maximum(jnp.abs(spread(e, width) - theta), 1.0)


def theta_body(states, sums, sigma, y_a, e_a, theta, resid, squares):
    width = sigma.shape[1] // states
    rate = over_states(sums[0:1], width) / over_states(sums[1:2], width)
    theta[...] = rate
    value = residual(sigma[...], y_a[...].astype(F32), e_a[...], rate, width)
    resid[...] = value
    squares[...] = jnp.sum(value * value, axis=0, keepdims=True)


def second_body(
    states, theta, resid, sig_r, sig_u, sig_c, msg_r, msg_u, msg_c, c_aa, c_r, c_u, c_c, parts
):
    mols, field = resid.shape
    width = field // states

    def other(sigma, msg):
        e = msg[:, field + 2 * mols : field + 2 * mols + states]
        value = residual(sigma, msg[:, :field], e, theta[...], width)
        return stack(value, states).astype(BF)

    f_a = stack(resid[...], states).astype(BF)
    f_r = other(sig_r[...], msg_r)
    f_u = other(sig_u[...], msg_u)
    f_c = other(sig_c[...], msg_c)
    row_a = (dot(c_aa[...], f_a) + dot(c_r[0], f_r)) + (dot(c_u[0], f_u) + dot(c_c[0], f_c))
    parts[0] = unstack(row_a, states)
    parts[1] = unstack(dot(c_r[1], f_a) + dot(c_u[1], f_u), states)
    parts[2] = unstack(dot(c_u[2], f_a) + dot(c_u[3], f_r), states)
    parts[3] = unstack(dot(c_c[1], f_a), states)


def last_body(states, count, squares, resid, raw, e_a, corr, sigma):
    width = resid.shape[1] // states
    scale = jnp.sqrt(over_states(squares[...], width) / count + 1e-06)
    value = (resid[...] / scale).astype(BF)
    corr[...] = value
    sigma[...] = raw[...] / scale + spread(e_a[...], width) * value.astype(F32)


def shards(densities, trials, energies, metric, pair_local, pair_remote, pair_scale):
    mols = densities.shape[2]
    states = energies.shape[3]
    aux = metric.shape[0]
    field = trials.shape[3]
    pairs = pair_local.shape[2]
    width = mols * states
    nx, ny = lax.axis_size("gx"), lax.axis_size("gy")

    def spot(x, y):
        return (x % nx) * ny + y % ny

    def take(value, dx, dy, only=lambda x, y: True):
        table = [
            (spot(x + dx, y + dy), spot(x, y))
            for x in range(nx)
            for y in range(ny)
            if only(x, y)
        ]
        return lax.ppermute(value, AXES, table)

    def butterfly(value):
        step = 1
        while step < ny:
            value = value + lax.ppermute(
                value, AXES, [(spot(x, y ^ step), spot(x, y)) for x in range(nx) for y in range(ny)]
            )
            step *= 2
        step = 1
        while step < nx:
            value = value + lax.ppermute(
                value, AXES, [(spot(x ^ step, y), spot(x, y)) for x in range(nx) for y in range(ny)]
            )
            step *= 2
        return value

    rho_a, y_a, e_a = densities[0, 0], trials[0, 0], energies[0, 0]
    rho_r = take(rho_a, 1, 0)
    rho_u = take(rho_a, 0, 1)

    own, msg = call(
        functools.partial(weights_body, aux**-0.5),
        (shape(4, mols, 2 * mols), shape(3, mols, field + 4 * mols)),
        9 * 2 * 3 * mols * 2 * mols * (pairs // 9),
        12 * pairs,
    )(pair_local[0], pair_remote[0], pair_scale[0], y_a, e_a)
    msg_r = take(msg[0], 1, 0)
    msg_u = take(msg[1], 0, 1)
    msg_c = take(msg[2], 1, 1)

    near = take(rho_r, 0, 1, lambda x, y: y % 2 == 0)
    far = take(rho_u, 1, 0, lambda x, y: y % 2 == 1)
    rho_c = jnp.where(lax.axis_index("gy") % 2 == 0, near, far)

    block = 2 * width * width * aux
    proj = 2 * width * aux * aux
    size = width * aux * 2
    proj_a, c_aa = call(
        functools.partial(self_body, states),
        (shape(width, aux, dtype=BF), shape(width, width, dtype=BF)),
        proj + block,
        4 * size,
    )(rho_a, metric, own)
    proj_r, c_r = call(
        functools.partial(right_body, states),
        (shape(width, aux, dtype=BF), shape(2, width, width, dtype=BF)),
        proj + 2 * block,
        6 * size,
    )(rho_a, rho_r, metric, proj_a, own, msg_r)
    c_u, sig = call(
        functools.partial(up_body, states),
        (shape(4, width, width, dtype=BF), shape(3, width, field // states)),
        proj + 4 * block,
        9 * size,
    )(rho_a, rho_r, rho_u, metric, proj_a, proj_r, own, msg_r, msg_u, c_aa, c_r, y_a)
    c_c, parts, sums = call(
        functools.partial(corner_body, states),
        (shape(2, width, width, dtype=BF), shape(4, mols, field), shape(2, field)),
        proj + 2 * block,
        6 * size,
    )(rho_a, rho_c, metric, proj_a, own, msg_r, msg_u, msg_c, y_a, e_a, sig)

    def home(parts):
        below = take(parts[2:4], 0, -1)
        left = take(parts[1] + below[1], -1, 0)
        return (parts[0] + below[0]) + left

    sums = butterfly(sums)
    sigma = home(parts)
    sig_r = take(sigma, 1, 0)
    upper = take(jnp.stack([sigma, sig_r]), 0, 1)
    theta, resid, squares = call(
        functools.partial(theta_body, states),
        (shape(1, field), shape(mols, field), shape(1, field)),
        20 * mols * field,
        12 * mols * field,
    )(sums, sigma, y_a, e_a)
    parts2 = call(
        functools.partial(second_body, states),
        shape(4, mols, field),
        9 * 2 * width * field * mols,
        9 * width * width * 2,
    )(theta, resid, sig_r, upper[0], upper[1], msg_r, msg_u, msg_c, c_aa, c_r, c_u, c_c)
    squares = butterfly(squares)
    corr, sigma2 = call(
        functools.partial(last_body, states, float(width * nx * ny)),
        (shape(mols, field, dtype=BF), shape(mols, field)),
        20 * mols * field,
        16 * mols * field,
    )(squares, resid, home(parts2), e_a)
    out = (1, 1, mols, field)
    return (
        sigma.reshape(out),
        corr.reshape(out),
        sigma2.reshape(out),
        theta[0, : field // states],
    )


def solution(mesh):
    return jax.shard_map(
        shards,
        mesh=mesh,
        in_specs=(
            P("gx", "gy", None, None),
            P("gx", "gy", None, None),
            P("gx", "gy", None, None),
            P(),
            P("gx", "gy", None),
            P("gx", "gy", None),
            P("gx", "gy", None),
        ),
        out_specs=(
            P("gx", "gy", None, None),
            P("gx", "gy", None, None),
            P("gx", "gy", None, None),
            P(),
        ),
        check_vma=False,
    )
```

time: 654 us -> 224 us (0.34)
  local copies, waits for them, and re-layouts: 229 us -> 7.41 us
  blocking collectives: 150 us -> 0 us
  waiting for transfers between devices: 178 us -> 107 us
  matrix products: 38.4 us -> 0 us
  Pallas kernels: 0 us -> 37.3 us
  starting transfers between devices: 39.6 us -> 64.1 us
    mul x37 -> x0, local copies, waits for them, and re-layouts: 188 us -> none  [the longest x36 188 us: couple(): dense = dense.reshape(mols, states, mols, states) * weight[:, None, :, None]]
    psum x2 -> x0, blocking collectives: 150 us -> none  [the longest x1 75.8 us: shards(): lax.psum((jnp.sum(start_vecs * sigma_first, axis=(0, 1)), jnp.sum(start_v...]
    ppermute x12 -> x29, waiting for transfers between devices: 178 us -> 107 us  [the longest x13 54.5 us: take(): return lax.ppermute(value, AXES, table)]
    dot_general x13 -> x0, matrix products: 38.4 us -> none  [the longest x9 17.7 us: couple(): lax.dot_general(proj, far_block, (((1,), (1,)), ((), ())), preferred_elem...]
    pallas_call x0 -> x8, Pallas kernels: none -> 37.3 us  [call(): pl.pallas_call(body, out_shape=outs, in_specs=vmem(len(args)), out_specs=...]
    ppermute x12 -> x29, starting transfers between devices: 39.6 us -> 64.1 us  [the longest x13 44.1 us: take(): return lax.ppermute(value, AXES, table)]
    reshape x4 -> x0, local copies, waits for them, and re-layouts: 18.3 us -> none  [the longest x1 15 us: shards(): near_rho = halo_rho.reshape(9, width, aux)]
    dynamic_update_slice x18 -> x0, local copies, waits for them, and re-layouts: 12.7 us -> none  [shards(): coupled = lax.map(couple, (near_rho, weights))]
  transfers between devices with their start and end apart: 12 -> 29, of which waited for: 6 -> 22; matrix products, arithmetic and copies ran while one was open for 2% -> 2% of each run, Pallas kernels for 0% -> 11%
where the time goes in v1:
time: 224 us; the launch traced here: 223 us
  waiting for transfers between devices  107 us (48%)
  starting transfers between devices  64.1 us (29%)
  Pallas kernels  37.3 us (17%)
  local copies, waits for them, and re-layouts  7.41 us (3%)
  other arithmetic  7.02 us (3%)
    ppermute x13, waiting for transfers between devices, take(): return lax.ppermute(value, AXES, table)  54.5 us
    ppermute x13, starting transfers between devices, take(): return lax.ppermute(value, AXES, table)  44.1 us
    pallas_call x8, Pallas kernels, call(): pl.pallas_call(body, out_shape=outs, in_specs=vmem(len(args)), out_specs=...  37.3 us
    ppermute x8, waiting for transfers between devices, butterfly(): lax.ppermute(value, AXES, [(spot(x, y ^ step), spot(x, y)) for x in range...  28.8 us
    ppermute x8, waiting for transfers between devices, butterfly(): lax.ppermute(value, AXES, [(spot(x ^ step, y), spot(x, y)) for x in range...  23.6 us
    ppermute x8, starting transfers between devices, butterfly(): lax.ppermute(value, AXES, [(spot(x ^ step, y), spot(x, y)) for x in range...  13.6 us
    ppermute x8, starting transfers between devices, butterfly(): lax.ppermute(value, AXES, [(spot(x, y ^ step), spot(x, y)) for x in range...  6.35 us
  transfers between devices with their start and end apart: 29, of which 22 were waited for; matrix products, arithmetic and copies ran while one was open for 2% of the time, Pallas kernels for 11%

profile of v1, /device:TPU:24, one launch (start us, length us, event | category | flops | bytes accessed | tf_op | source)
XLA Modules:
  0.0 223.4 jit_solution(8729599391925399278)
XLA Ops:
  0.6 4.9 %collective-permute-start = (bf16[64,8192]{1,0:T(8,128)(2,1)}, bf16[64,8192]{1,0:T(8,128)(2,1)}, u32[]{:S(2)}, u32[]{:S(2)}) collective-permute-start(bf16[64,8192]{1,0:T(8,128)(2,1)} %bitcast.46), channel_id=1, source_target_pairs={{16,0},{17,1},{18,2},{19,3},{20,4},{21,5},{22,6},{23,7},{24,8},{25... | collective-permute-start | bytes 3145736 | tf_op jit(solution)/shard_map/ppermute | solution.py:240
  5.5 5.8 %collective-permute-start.2 = (bf16[64,8192]{1,0:T(8,128)(2,1)}, bf16[64,8192]{1,0:T(8,128)(2,1)}, u32[]{:S(2)}, u32[]{:S(2)}) collective-permute-start(bf16[64,8192]{1,0:T(8,128)(2,1)} %bitcast.47), channel_id=1, source_target_pairs={{1,0},{2,1},{3,2},{4,3},{5,4},{6,5},{7,6},{8,7},{9,8},{10,9},{11,1... | collective-permute-start | bytes 3145736 | tf_op jit(solution)/shard_map/ppermute | solution.py:240
  11.4 17.8 %collective-permute-done.rho_r = bf16[64,8192]{1,0:T(8,128)(2,1)} collective-permute-done((bf16[64,8192]{1,0:T(8,128)(2,1)}, bf16[64,8192]{1,0:T(8,128)(2,1)}, u32[]{:S(2)}, u32[]{:S(2)}) %collective-permute-start) | collective-permute-done | bytes 1048608 | tf_op jit(solution)/shard_map/ppermute | solution.py:240
  30.5 9.9 %collective-permute-done.2.rho_u = bf16[64,8192]{1,0:T(8,128)(2,1)} collective-permute-done((bf16[64,8192]{1,0:T(8,128)(2,1)}, bf16[64,8192]{1,0:T(8,128)(2,1)}, u32[]{:S(2)}, u32[]{:S(2)}) %collective-permute-start.2) | collective-permute-done | bytes 1048608 | tf_op jit(solution)/shard_map/ppermute | solution.py:240
  46.3 10.7 %collective-permute-start.4 = (f32[64,512]{1,0:T(8,128)S(1)}, f32[64,512]{1,0:T(8,128)S(1)}, u32[]{:S(2)}, u32[]{:S(2)}) collective-permute-start(f32[64,512]{1,0:T(8,128)S(1)} %get-tuple-element.38), channel_id=1, source_target_pairs={{16,0},{17,1},{18,2},{19,3},{20,4},{21,5},{22,6},{23,7},{24,8},{25... | collective-permute-start | bytes 393224 | tf_op jit(solution)/shard_map/ppermute | solution.py:240
  57.0 12.6 %collective-permute-start.5 = (f32[64,512]{1,0:T(8,128)S(1)}, f32[64,512]{1,0:T(8,128)S(1)}, u32[]{:S(2)}, u32[]{:S(2)}) collective-permute-start(f32[64,512]{1,0:T(8,128)S(1)} %get-tuple-element.37), channel_id=1, source_target_pairs={{1,0},{2,1},{3,2},{4,3},{5,4},{6,5},{7,6},{8,7},{9,8},{10,9},{11,1... | collective-permute-start | bytes 393224 | tf_op jit(solution)/shard_map/ppermute | solution.py:240
  69.5 4.5 %shard_map.103 = (bf16[512,1024]{1,0:T(8,128)(2,1)}, bf16[512,512]{1,0:T(8,128)(2,1)}) custom-call(bf16[64,8192]{1,0:T(8,128)(2,1)} %bitcast.48, bf16[1024,1024]{1,0:T(8,128)(2,1)} %metric.7, f32[4,64,128]{2,1,0:T(8,128)} %get-tuple-element.20.own), custom_call_target="tpu_custom_call" | custom-call | flops 1610612736 | bytes 4194304 | tf_op jit(solution)/shard_map/pallas_call | solution.py:22
  74.7 5.9 %shard_map.104 = (bf16[512,1024]{1,0:T(8,128)(2,1)}, bf16[2,512,512]{2,1,0:T(8,128)(2,1)}) custom-call(bf16[64,8192]{1,0:T(8,128)(2,1)} %bitcast.49, bf16[64,8192]{1,0:T(8,128)(2,1)} %collective-permute-done.rho_r, bf16[1024,1024]{1,0:T(8,128)(2,1)} %metric.7, bf16[512,1024]{1,0:T(8,128)(2,1)} %get-tuple-element.21.proj_a, ...), custom_call_target="tpu_custom_call" | custom-call | flops 2147483648 | bytes 6291456 | tf_op jit(solution)/shard_map/pallas_call | solution.py:22
  81.3 9.1 %shard_map.105 = (bf16[4,512,512]{2,1,0:T(8,128)(2,1)}, f32[3,512,32]{2,1,0:T(8,128)}) custom-call(bf16[64,8192]{1,0:T(8,128)(2,1)} %bitcast.50, bf16[64,8192]{1,0:T(8,128)(2,1)} %collective-permute-done.rho_r, bf16[64,8192]{1,0:T(8,128)(2,1)} %collective-permute-done.2.rho_u, bf16[1024,1024]{1,0:T(8,128)(2,1)} %metric.7, ...), custom_call_target="tpu_custom_call" | custom-call | flops 3221225472 | bytes 9437184 | tf_op jit(solution)/shard_map/pallas_call | solution.py:22
  92.1 6.6 %shard_map.106 = (bf16[2,512,512]{2,1,0:T(8,128)(2,1)}, f32[4,64,256]{2,1,0:T(8,128)}, f32[2,256]{1,0:T(2,128)}) custom-call(bf16[64,8192]{1,0:T(8,128)(2,1)} %bitcast.51, bf16[64,8192]{1,0:T(8,128)(2,1)} %broadcast_select_fusion.rho_c, bf16[1024,1024]{1,0:T(8,128)(2,1)} %metric.7, bf16[512,1024]{1,0:T(8,128)(2,1)} %get-tuple-element.21.proj_a, ...), custom_call_target="tpu_custom_call" | custom-call | flops 2147483648 | bytes 6291456 | tf_op jit(solution)/shard_map/pallas_call | solution.py:22
  99.6 3.9 %collective-permute-start.7 = (f32[2,64,256]{2,1,0:T(8,128)S(1)}, f32[2,64,256]{2,1,0:T(8,128)S(1)}, u32[]{:S(2)}, u32[]{:S(2)}) collective-permute-start(f32[2,64,256]{2,1,0:T(8,128)S(1)} %slice.52), channel_id=1, source_target_pairs={{15,0},{0,1},{1,2},{2,3},{3,4},{4,5},{5,6},{6,7},{7,8},{8,9},{9,10... | collective-permute-start | bytes 393224 | tf_op jit(solution)/shard_map/ppermute | solution.py:240
  103.6 6.6 %collective-permute-done.7 = f32[2,64,256]{2,1,0:T(8,128)S(1)} collective-permute-done((f32[2,64,256]{2,1,0:T(8,128)S(1)}, f32[2,64,256]{2,1,0:T(8,128)S(1)}, u32[]{:S(2)}, u32[]{:S(2)}) %collective-permute-start.7) | collective-permute-done | bytes 131104 | tf_op jit(solution)/shard_map/ppermute | solution.py:240
  111.6 6.6 %collective-permute-done.8 = f32[64,256]{1,0:T(8,128)S(1)} collective-permute-done((f32[64,256]{1,0:T(8,128)S(1)}, f32[64,256]{1,0:T(8,128)S(1)}, u32[]{:S(2)}, u32[]{:S(2)}) %collective-permute-start.8) | collective-permute-done | bytes 65568 | tf_op jit(solution)/shard_map/ppermute | solution.py:240
  127.7 5.7 %collective-permute-done.10 = f32[2,256]{1,0:T(2,128)S(1)} collective-permute-done((f32[2,256]{1,0:T(2,128)S(1)}, f32[2,256]{1,0:T(2,128)S(1)}, u32[]{:S(2)}, u32[]{:S(2)}) %collective-permute-start.10) | collective-permute-done | bytes 2080 | tf_op jit(solution)/shard_map/ppermute | solution.py:245
  133.4 3.6 %collective-permute-done.11 = f32[2,256]{1,0:T(2,128)S(1)} collective-permute-done((f32[2,256]{1,0:T(2,128)S(1)}, f32[2,256]{1,0:T(2,128)S(1)}, u32[]{:S(2)}, u32[]{:S(2)}) %collective-permute-start.11) | collective-permute-done | bytes 2080 | tf_op jit(solution)/shard_map/ppermute | solution.py:245
  142.1 3.6 %collective-permute-done.13 = f32[2,256]{1,0:T(2,128)S(1)} collective-permute-done((f32[2,256]{1,0:T(2,128)S(1)}, f32[2,256]{1,0:T(2,128)S(1)}, u32[]{:S(2)}, u32[]{:S(2)}) %collective-permute-start.13) | collective-permute-done | bytes 2080 | tf_op jit(solution)/shard_map/ppermute | solution.py:251
  145.7 5.4 %collective-permute-start.14 = (f32[2,256]{1,0:T(2,128)S(1)}, f32[2,256]{1,0:T(2,128)S(1)}, u32[]{:S(2)}, u32[]{:S(2)}) collective-permute-start(f32[2,256]{1,0:T(2,128)S(1)} %add.92), channel_id=1, source_target_pairs={{32,0},{33,1},{34,2},{35,3},{36,4},{37,5},{38,6},{39,7},{40,8},{41... | collective-permute-start | bytes 6152 | tf_op jit(solution)/shard_map/ppermute | solution.py:251
  152.7 3.6 %collective-permute-done.15 = f32[2,256]{1,0:T(2,128)S(1)} collective-permute-done((f32[2,256]{1,0:T(2,128)S(1)}, f32[2,256]{1,0:T(2,128)S(1)}, u32[]{:S(2)}, u32[]{:S(2)}) %collective-permute-start.15) | collective-permute-done | bytes 2080 | tf_op jit(solution)/shard_map/ppermute | solution.py:251
  164.3 5.1 %shard_map.108 = f32[4,64,256]{2,1,0:T(8,128)} custom-call(f32[1,256]{1,0:T(1,128)} %get-tuple-element.31.theta, f32[64,256]{1,0:T(8,128)} %get-tuple-element.30.resid, f32[64,256]{1,0:T(8,128)} %copy-done.1, f32[64,256]{1,0:T(8,128)} %get-tuple-element.40.sig_u, f32[64,256]{1,0:T(8,128)} %get-tuple-element.39.sig_c, f32[64,512]{1,0:T(8,128)} %copy-done.2, ...), custom_call_target="tpu_custom_call" | custom-call | flops 150994944 | bytes 4718592 | tf_op jit(solution)/shard_map/pallas_call | solution.py:22
  170.4 10.5 %collective-permute-done.27 = f32[2,64,256]{2,1,0:T(8,128)S(1)} collective-permute-done((f32[2,64,256]{2,1,0:T(8,128)S(1)}, f32[2,64,256]{2,1,0:T(8,128)S(1)}, u32[]{:S(2)}, u32[]{:S(2)}) %collective-permute-start.27) | collective-permute-done | bytes 131104 | tf_op jit(solution)/shard_map/ppermute | solution.py:240
  185.7 6.8 %collective-permute-done.18 = f32[1,256]{1,0:T(1,128)S(1)} collective-permute-done((f32[1,256]{1,0:T(1,128)S(1)}, f32[1,256]{1,0:T(1,128)S(1)}, u32[]{:S(2)}, u32[]{:S(2)}) %collective-permute-start.18) | collective-permute-done | bytes 1056 | tf_op jit(solution)/shard_map/ppermute | solution.py:245
  197.4 3.8 %collective-permute-done.20 = f32[1,256]{1,0:T(1,128)S(1)} collective-permute-done((f32[1,256]{1,0:T(1,128)S(1)}, f32[1,256]{1,0:T(1,128)S(1)}, u32[]{:S(2)}, u32[]{:S(2)}) %collective-permute-start.20) | collective-permute-done | bytes 1056 | tf_op jit(solution)/shard_map/ppermute | solution.py:245
  205.0 4.0 %collective-permute-start.22 = (f32[1,256]{1,0:T(1,128)S(1)}, f32[1,256]{1,0:T(1,128)S(1)}, u32[]{:S(2)}, u32[]{:S(2)}) collective-permute-start(f32[1,256]{1,0:T(1,128)S(1)} %add.100), channel_id=1, source_target_pairs={{32,0},{33,1},{34,2},{35,3},{36,4},{37,5},{38,6},{39,7},{40,8},{41... | collective-permute-start | bytes 3080 | tf_op jit(solution)/shard_map/ppermute | solution.py:251
  214.1 5.1 %collective-permute-done.24 = f32[1,256]{1,0:T(1,128)S(1)} collective-permute-done((f32[1,256]{1,0:T(1,128)S(1)}, f32[1,256]{1,0:T(1,128)S(1)}, u32[]{:S(2)}, u32[]{:S(2)}) %collective-permute-start.24) | collective-permute-done | bytes 1056 | tf_op jit(solution)/shard_map/ppermute | solution.py:251
  (84 shorter events, 60.5 us)
Async XLA Ops:
  0.6 28.6 %collective-permute-start = (bf16[64,8192]{1,0:T(8,128)(2,1)}, bf16[64,8192]{1,0:T(8,128)(2,1)}, u32[]{:S(2)}, u32[]{:S(2)}) collective-permute-start(bf16[64,8192]{1,0:T(8,128)(2,1)} %bitcast.46), channel_id=1, source_target_pairs={{16,0},{17,1},{18,2},{19,3},{20,4},{21,5},{22,6},{23,7},{24,8},{25... | collective-permute-start | bytes 3145736 | tf_op jit(solution)/shard_map/ppermute | solution.py:240
  5.5 34.9 %collective-permute-start.2 = (bf16[64,8192]{1,0:T(8,128)(2,1)}, bf16[64,8192]{1,0:T(8,128)(2,1)}, u32[]{:S(2)}, u32[]{:S(2)}) collective-permute-start(bf16[64,8192]{1,0:T(8,128)(2,1)} %bitcast.47), channel_id=1, source_target_pairs={{1,0},{2,1},{3,2},{4,3},{5,4},{6,5},{7,6},{8,7},{9,8},{10,9},{11,1... | collective-permute-start | bytes 3145736 | tf_op jit(solution)/shard_map/ppermute | solution.py:240
  29.2 61.2 %collective-permute-start.1 = (bf16[64,8192]{1,0:T(8,128)(2,1)}, bf16[64,8192]{1,0:T(8,128)(2,1)S(1)}, u32[]{:S(2)}, u32[]{:S(2)}) collective-permute-start(bf16[64,8192]{1,0:T(8,128)(2,1)} %collective-permute-done.rho_r), channel_id=1, source_target_pairs={{1,0},{3,2},{5,4},{7,6},{9,8},{11,10},{13,12},{15,14},{17,16},{19,... | collective-permute-start | bytes 3145736 | tf_op jit(solution)/shard_map/ppermute | solution.py:240
  40.4 49.9 %collective-permute-start.3 = (bf16[64,8192]{1,0:T(8,128)(2,1)}, bf16[64,8192]{1,0:T(8,128)(2,1)S(1)}, u32[]{:S(2)}, u32[]{:S(2)}) collective-permute-start(bf16[64,8192]{1,0:T(8,128)(2,1)} %collective-permute-done.2.rho_u), channel_id=1, source_target_pairs={{17,1},{19,3},{21,5},{23,7},{25,9},{27,11},{29,13},{31,15},{33,17}... | collective-permute-start | bytes 3145736 | tf_op jit(solution)/shard_map/ppermute | solution.py:240
  46.3 27.8 %collective-permute-start.4 = (f32[64,512]{1,0:T(8,128)S(1)}, f32[64,512]{1,0:T(8,128)S(1)}, u32[]{:S(2)}, u32[]{:S(2)}) collective-permute-start(f32[64,512]{1,0:T(8,128)S(1)} %get-tuple-element.38), channel_id=1, source_target_pairs={{16,0},{17,1},{18,2},{19,3},{20,4},{21,5},{22,6},{23,7},{24,8},{25... | collective-permute-start | bytes 393224 | tf_op jit(solution)/shard_map/ppermute | solution.py:240
  57.0 23.7 %collective-permute-start.5 = (f32[64,512]{1,0:T(8,128)S(1)}, f32[64,512]{1,0:T(8,128)S(1)}, u32[]{:S(2)}, u32[]{:S(2)}) collective-permute-start(f32[64,512]{1,0:T(8,128)S(1)} %get-tuple-element.37), channel_id=1, source_target_pairs={{1,0},{2,1},{3,2},{4,3},{5,4},{6,5},{7,6},{8,7},{9,8},{10,9},{11,1... | collective-permute-start | bytes 393224 | tf_op jit(solution)/shard_map/ppermute | solution.py:240
  69.5 22.0 %collective-permute-start.6 = (f32[64,512]{1,0:T(8,128)S(1)}, f32[64,512]{1,0:T(8,128)S(1)}, u32[]{:S(2)}, u32[]{:S(2)}) collective-permute-start(f32[64,512]{1,0:T(8,128)S(1)} %get-tuple-element.36), channel_id=1, source_target_pairs={{17,0},{18,1},{19,2},{20,3},{21,4},{22,5},{23,6},{24,7},{25,8},{26... | collective-permute-start | bytes 393224 | tf_op jit(solution)/shard_map/ppermute | solution.py:240
  99.6 10.6 %collective-permute-start.7 = (f32[2,64,256]{2,1,0:T(8,128)S(1)}, f32[2,64,256]{2,1,0:T(8,128)S(1)}, u32[]{:S(2)}, u32[]{:S(2)}) collective-permute-start(f32[2,64,256]{2,1,0:T(8,128)S(1)} %slice.52), channel_id=1, source_target_pairs={{15,0},{0,1},{1,2},{2,3},{3,4},{4,5},{5,6},{6,7},{7,8},{8,9},{9,10... | collective-permute-start | bytes 393224 | tf_op jit(solution)/shard_map/ppermute | solution.py:240
  111.1 7.1 %collective-permute-start.8 = (f32[64,256]{1,0:T(8,128)S(1)}, f32[64,256]{1,0:T(8,128)S(1)}, u32[]{:S(2)}, u32[]{:S(2)}) collective-permute-start(f32[64,256]{1,0:T(8,128)S(1)} %fusion.3), channel_id=1, source_target_pairs={{240,0},{241,1},{242,2},{243,3},{244,4},{245,5},{246,6},{247,7},{2... | collective-permute-start | bytes 196616 | tf_op jit(solution)/shard_map/ppermute | solution.py:240
  119.1 4.3 %collective-permute-start.25 = (f32[64,256]{1,0:T(8,128)S(1)}, f32[64,256]{1,0:T(8,128)S(1)}, u32[]{:S(2)}, u32[]{:S(2)}) collective-permute-start(f32[64,256]{1,0:T(8,128)S(1)} %fusion.5.sigma), channel_id=1, source_target_pairs={{16,0},{17,1},{18,2},{19,3},{20,4},{21,5},{22,6},{23,7},{24,8},{25... | collective-permute-start | bytes 196616 | tf_op jit(solution)/shard_map/ppermute | solution.py:240
  123.4 40.2 %collective-permute-start.26 = (f32[2,64,256]{2,1,0:T(8,128)S(1)}, f32[2,64,256]{2,1,0:T(8,128)S(1)}, u32[]{:S(2)}, u32[]{:S(2)}) collective-permute-start(f32[2,64,256]{2,1,0:T(8,128)S(1)} %pad_maximum_fusion), channel_id=1, source_target_pairs={{1,0},{2,1},{3,2},{4,3},{5,4},{6,5},{7,6},{8,7},{9,8},{10,9},{11,1... | collective-permute-start | bytes 393224 | tf_op jit(solution)/shard_map/ppermute | solution.py:240
  125.9 7.5 %collective-permute-start.10 = (f32[2,256]{1,0:T(2,128)S(1)}, f32[2,256]{1,0:T(2,128)S(1)}, u32[]{:S(2)}, u32[]{:S(2)}) collective-permute-start(f32[2,256]{1,0:T(2,128)S(1)} %add.88), channel_id=1, source_target_pairs={{2,0},{3,1},{0,2},{1,3},{6,4},{7,5},{4,6},{5,7},{10,8},{11,9},{8,1... | collective-permute-start | bytes 6152 | tf_op jit(solution)/shard_map/ppermute | solution.py:245
  133.4 3.6 %collective-permute-start.11 = (f32[2,256]{1,0:T(2,128)S(1)}, f32[2,256]{1,0:T(2,128)S(1)}, u32[]{:S(2)}, u32[]{:S(2)}) collective-permute-start(f32[2,256]{1,0:T(2,128)S(1)} %add.89), channel_id=1, source_target_pairs={{4,0},{5,1},{6,2},{7,3},{0,4},{1,5},{2,6},{3,7},{12,8},{13,9},{14,... | collective-permute-start | bytes 6152 | tf_op jit(solution)/shard_map/ppermute | solution.py:245
  137.0 5.1 %collective-permute-start.12 = (f32[2,256]{1,0:T(2,128)S(1)}, f32[2,256]{1,0:T(2,128)S(1)}, u32[]{:S(2)}, u32[]{:S(2)}) collective-permute-start(f32[2,256]{1,0:T(2,128)S(1)} %add.90), channel_id=1, source_target_pairs={{8,0},{9,1},{10,2},{11,3},{12,4},{13,5},{14,6},{15,7},{0,8},{1,9},... | collective-permute-start | bytes 6152 | tf_op jit(solution)/shard_map/ppermute | solution.py:245
  142.1 3.6 %collective-permute-start.13 = (f32[2,256]{1,0:T(2,128)S(1)}, f32[2,256]{1,0:T(2,128)S(1)}, u32[]{:S(2)}, u32[]{:S(2)}) collective-permute-start(f32[2,256]{1,0:T(2,128)S(1)} %add.91), channel_id=1, source_target_pairs={{16,0},{17,1},{18,2},{19,3},{20,4},{21,5},{22,6},{23,7},{24,8},{25... | collective-permute-start | bytes 6152 | tf_op jit(solution)/shard_map/ppermute | solution.py:251
  145.7 7.0 %collective-permute-start.14 = (f32[2,256]{1,0:T(2,128)S(1)}, f32[2,256]{1,0:T(2,128)S(1)}, u32[]{:S(2)}, u32[]{:S(2)}) collective-permute-start(f32[2,256]{1,0:T(2,128)S(1)} %add.92), channel_id=1, source_target_pairs={{32,0},{33,1},{34,2},{35,3},{36,4},{37,5},{38,6},{39,7},{40,8},{41... | collective-permute-start | bytes 6152 | tf_op jit(solution)/shard_map/ppermute | solution.py:251
  156.3 5.1 %collective-permute-start.16 = (f32[2,256]{1,0:T(2,128)S(1)}, f32[2,256]{1,0:T(2,128)S(1)}, u32[]{:S(2)}, u32[]{:S(2)}) collective-permute-start(f32[2,256]{1,0:T(2,128)S(1)} %add.94), channel_id=1, source_target_pairs={{128,0},{129,1},{130,2},{131,3},{132,4},{133,5},{134,6},{135,7},{1... | collective-permute-start | bytes 6152 | tf_op jit(solution)/shard_map/ppermute | solution.py:251
  170.3 10.6 %collective-permute-start.27 = (f32[2,64,256]{2,1,0:T(8,128)S(1)}, f32[2,64,256]{2,1,0:T(8,128)S(1)}, u32[]{:S(2)}, u32[]{:S(2)}) collective-permute-start(f32[2,64,256]{2,1,0:T(8,128)S(1)} %slice.69), channel_id=1, source_target_pairs={{15,0},{0,1},{1,2},{2,3},{3,4},{4,5},{5,6},{6,7},{7,8},{8,9},{9,10... | collective-permute-start | bytes 393224 | tf_op jit(solution)/shard_map/ppermute | solution.py:240
  181.7 38.0 %collective-permute-start.28 = (f32[64,256]{1,0:T(8,128)S(1)}, f32[64,256]{1,0:T(8,128)S(1)}, u32[]{:S(2)}, u32[]{:S(2)}) collective-permute-start(f32[64,256]{1,0:T(8,128)S(1)} %fusion), channel_id=1, source_target_pairs={{240,0},{241,1},{242,2},{243,3},{244,4},{245,5},{246,6},{247,7},{2... | collective-permute-start | bytes 196616 | tf_op jit(solution)/shard_map/ppermute | solution.py:240
  185.0 7.5 %collective-permute-start.18 = (f32[1,256]{1,0:T(1,128)S(1)}, f32[1,256]{1,0:T(1,128)S(1)}, u32[]{:S(2)}, u32[]{:S(2)}) collective-permute-start(f32[1,256]{1,0:T(1,128)S(1)} %add.96), channel_id=1, source_target_pairs={{2,0},{3,1},{0,2},{1,3},{6,4},{7,5},{4,6},{5,7},{10,8},{11,9},{8,1... | collective-permute-start | bytes 3080 | tf_op jit(solution)/shard_map/ppermute | solution.py:245
  196.1 5.1 %collective-permute-start.20 = (f32[1,256]{1,0:T(1,128)S(1)}, f32[1,256]{1,0:T(1,128)S(1)}, u32[]{:S(2)}, u32[]{:S(2)}) collective-permute-start(f32[1,256]{1,0:T(1,128)S(1)} %add.98), channel_id=1, source_target_pairs={{8,0},{9,1},{10,2},{11,3},{12,4},{13,5},{14,6},{15,7},{0,8},{1,9},... | collective-permute-start | bytes 3080 | tf_op jit(solution)/shard_map/ppermute | solution.py:245
  201.2 3.8 %collective-permute-start.21 = (f32[1,256]{1,0:T(1,128)S(1)}, f32[1,256]{1,0:T(1,128)S(1)}, u32[]{:S(2)}, u32[]{:S(2)}) collective-permute-start(f32[1,256]{1,0:T(1,128)S(1)} %add.99), channel_id=1, source_target_pairs={{16,0},{17,1},{18,2},{19,3},{20,4},{21,5},{22,6},{23,7},{24,8},{25... | collective-permute-start | bytes 3080 | tf_op jit(solution)/shard_map/ppermute | solution.py:251
  205.0 5.5 %collective-permute-start.22 = (f32[1,256]{1,0:T(1,128)S(1)}, f32[1,256]{1,0:T(1,128)S(1)}, u32[]{:S(2)}, u32[]{:S(2)}) collective-permute-start(f32[1,256]{1,0:T(1,128)S(1)} %add.100), channel_id=1, source_target_pairs={{32,0},{33,1},{34,2},{35,3},{36,4},{37,5},{38,6},{39,7},{40,8},{41... | collective-permute-start | bytes 3080 | tf_op jit(solution)/shard_map/ppermute | solution.py:251
  214.1 5.1 %collective-permute-start.24 = (f32[1,256]{1,0:T(1,128)S(1)}, f32[1,256]{1,0:T(1,128)S(1)}, u32[]{:S(2)}, u32[]{:S(2)}) collective-permute-start(f32[1,256]{1,0:T(1,128)S(1)} %add.102), channel_id=1, source_target_pairs={{128,0},{129,1},{130,2},{131,3},{132,4},{133,5},{134,6},{135,7},{1... | collective-permute-start | bytes 3080 | tf_op jit(solution)/shard_map/ppermute | solution.py:251
  (12 other events, 175.8 us)

commit v2 on v1

--- a/solution.py
+++ b/solution.py
@@ -7,6 +7,7 @@
 from jax.experimental.pallas import tpu as pltpu
 from jax.sharding import PartitionSpec as P
 
+
 BF = jnp.bfloat16
 F32 = jnp.float32
 AXES = ("gx", "gy")
@@ -18,11 +19,11 @@
     return [pl.BlockSpec(memory_space=pltpu.VMEM)] * count
 
 
-def call(body, outs, flops, moved):
+def call(body, outs, flops, moved, smem=0):
     return lambda *args: pl.pallas_call(
         body,
         out_shape=outs,
-        in_specs=vmem(len(args)),
+        in_specs=[pl.BlockSpec(memory_space=pltpu.SMEM)] * smem + vmem(len(args) - smem),
         out_specs=jax.tree.map(lambda _: pl.BlockSpec(memory_space=pltpu.VMEM), outs),
         compiler_params=pltpu.CompilerParams(vmem_limit_bytes=60 * 2**20),
         cost_estimate=pl.CostEstimate(flops=flops, bytes_accessed=moved, transcendentals=0),
@@ -70,7 +71,7 @@
     return out
 
 
-def weights_body(scale, loc, rem, sc, y, e, own, msg):
+def weights_body(scale, loc, rem, sc, y, e, own_a, own_r, own_u, own_c, msg_r, msg_u, msg_c):
     mols = y.shape[0]
     cap = loc.shape[1] // 9
     mol = lax.broadcasted_iota(jnp.int32, (mols, cap), 0)
@@ -92,17 +93,21 @@
         )
         return three[:mols] + (three[mols : 2 * mols] + three[2 * mols :])
 
-    for k, o in enumerate((SELF, TO_R, TO_U, TO_UR)):
-        own[k] = weight(o)
+    for own, o in ((own_a, SELF), (own_r, TO_R), (own_u, TO_U), (own_c, TO_UR)):
+        own[...] = weight(o)
     field = y.shape[1]
-    for k, (o, q) in enumerate(((R_TO_A, R_TO_U), (U_TO_A, U_TO_R), (UR_TO_A, None))):
+    for msg, o, q in (
+        (msg_r, R_TO_A, R_TO_U),
+        (msg_u, U_TO_A, U_TO_R),
+        (msg_c, UR_TO_A, None),
+    ):
         first = weight(o)
         if q is not None:
             lane = lax.broadcasted_iota(jnp.int32, first.shape, 1)
             first = jnp.where(lane < mols, first, weight(q))
-        msg[k, :, :field] = y[...].astype(F32)
-        msg[k, :, field : field + 2 * mols] = first
-        msg[k, :, field + 2 * mols :] = jnp.concatenate(
+        msg[:, :field] = y[...].astype(F32)
+        msg[:, field : field + 2 * mols] = first
+        msg[:, field + 2 * mols :] = jnp.concatenate(
             [e[...], jnp.zeros((mols, 2 * mols - e.shape[1]), F32)], axis=1
         )
 
@@ -110,14 +115,14 @@
 def self_body(states, rho, metric, own, proj, c_aa):
     rows = stack(rho, states)
     proj[...] = dot(rows, metric[...]).astype(BF)
-    c_aa[...] = couple(proj[...], rows, own[0])
+    c_aa[...] = couple(proj[...], rows, own[...])
 
 
 def right_body(states, rho_a, rho_r, metric, proj_a, own, msg_r, proj_r, c):
     mols = rho_a.shape[0]
     rows_a, rows_r = stack(rho_a, states), stack(rho_r, states)
     field = msg_r.shape[1] - 4 * mols
-    c[0] = couple(proj_a[...], rows_r, own[1])
+    c[0] = couple(proj_a[...], rows_r, own[...])
     proj_r[...] = dot(rows_r, metric[...]).astype(BF)
     c[1] = couple(proj_r[...], rows_a, twice(msg_r[:, field : field + mols]))
 
@@ -128,7 +133,7 @@
     mols = rho_a.shape[0]
     field = msg_r.shape[1] - 4 * mols
     rows_u = stack(rho_u, states)
-    c[0] = couple(proj_a[...], rows_u, own[2])
+    c[0] = couple(proj_a[...], rows_u, own[...])
     c[1] = couple(proj_r[...], rows_u, twice(msg_r[:, field + mols : field + 2 * mols]))
     proj_u = dot(rows_u, metric[...]).astype(BF)
     c[2] = couple(proj_u, stack(rho_a, states), twice(msg_u[:, field : field + mols]))
@@ -144,12 +149,38 @@
 
 
 def corner_body(
-    states, rho_a, rho_c, metric, proj_a, own, msg_r, msg_u, msg_c, y_a, e_a, sig, c, parts, sums
+    states,
+    second,
+    rho_a,
+    near,
+    far,
+    metric,
+    proj_a,
+    own,
+    msg_r,
+    msg_u,
+    msg_c,
+    y_a,
+    e_a,
+    sig,
+    c,
+    to_a,
+    to_r,
+    to_uc,
+    sums,
 ):
     mols = rho_a.shape[0]
     field = msg_r.shape[1] - 4 * mols
-    rows_c = stack(rho_c, states)
-    c[0] = couple(proj_a[...], rows_c, own[3])
+    width = near.shape[1] // states
+    pick = second[0, 0] == 1
+    rows_c = jnp.concatenate(
+        [
+            jnp.where(pick, far[:, a * width : (a + 1) * width], near[:, a * width : (a + 1) * width])
+            for a in range(states)
+        ],
+        axis=0,
+    )
+    c[0] = couple(proj_a[...], rows_c, own[...])
     proj_c = dot(rows_c, metric[...]).astype(BF)
     c[1] = couple(proj_c, stack(rho_a, states), twice(msg_c[:, field : field + mols]))
     f_a = stack(y_a, states)
@@ -160,7 +191,7 @@
     part_r = unstack(sig[1], states)
     part_u = unstack(sig[2], states)
     part_c = unstack(dot(c[1], f_a), states)
-    parts[0], parts[1], parts[2], parts[3] = part_a, part_r, part_u, part_c
+    to_a[...], to_r[...], to_uc[0], to_uc[1] = part_a, part_r, part_u, part_c
     total = part_a * own_y + part_r * msg_r[:, :field]
     total = total + (part_u * msg_u[:, :field] + part_c * msg_c[:, :field])
     sums[0:1] = jnp.sum(total, axis=0, keepdims=True)
@@ -189,7 +220,7 @@
 
 
 def second_body(
-    states, theta, resid, sig_r, sig_u, sig_c, msg_r, msg_u, msg_c, c_aa, c_r, c_u, c_c, parts
+    states, theta, resid, sig_r, sig_uc, msg_r, msg_u, msg_c, c_aa, c_r, c_u, c_c, to_a, to_r, to_uc
 ):
     mols, field = resid.shape
     width = field // states
@@ -201,13 +232,13 @@
 
     f_a = stack(resid[...], states).astype(BF)
     f_r = other(sig_r[...], msg_r)
-    f_u = other(sig_u[...], msg_u)
-    f_c = other(sig_c[...], msg_c)
+    f_u = other(sig_uc[0], msg_u)
+    f_c = other(sig_uc[1], msg_c)
     row_a = (dot(c_aa[...], f_a) + dot(c_r[0], f_r)) + (dot(c_u[0], f_u) + dot(c_c[0], f_c))
-    parts[0] = unstack(row_a, states)
-    parts[1] = unstack(dot(c_r[1], f_a) + dot(c_u[1], f_u), states)
-    parts[2] = unstack(dot(c_u[2], f_a) + dot(c_u[3], f_r), states)
-    parts[3] = unstack(dot(c_c[1], f_a), states)
+    to_a[...] = unstack(row_a, states)
+    to_r[...] = unstack(dot(c_r[1], f_a) + dot(c_u[1], f_u), states)
+    to_uc[0] = unstack(dot(c_u[2], f_a) + dot(c_u[3], f_r), states)
+    to_uc[1] = unstack(dot(c_c[1], f_a), states)
 
 
 def last_body(states, count, squares, resid, raw, e_a, corr, sigma):
@@ -239,38 +270,32 @@
         ]
         return lax.ppermute(value, AXES, table)
 
+    flips = [(0, 2), (1, 0), (2, 0), (0, 4), (0, 8), (4, 0), (8, 0), (0, 1)]
+
     def butterfly(value):
-        step = 1
-        while step < ny:
-            value = value + lax.ppermute(
-                value, AXES, [(spot(x, y ^ step), spot(x, y)) for x in range(nx) for y in range(ny)]
-            )
-            step *= 2
-        step = 1
-        while step < nx:
-            value = value + lax.ppermute(
-                value, AXES, [(spot(x ^ step, y), spot(x, y)) for x in range(nx) for y in range(ny)]
-            )
-            step *= 2
+        for fx, fy in flips:
+            table = [(spot(x ^ fx, y ^ fy), spot(x, y)) for x in range(nx) for y in range(ny)]
+            value = value + lax.ppermute(value, AXES, table)
         return value
 
     rho_a, y_a, e_a = densities[0, 0], trials[0, 0], energies[0, 0]
     rho_r = take(rho_a, 1, 0)
     rho_u = take(rho_a, 0, 1)
 
-    own, msg = call(
+    pair = shape(mols, 2 * mols)
+    note = shape(mols, field + 4 * mols)
+    own_a, own_r, own_u, own_c, msg_r, msg_u, msg_c = call(
         functools.partial(weights_body, aux**-0.5),
-        (shape(4, mols, 2 * mols), shape(3, mols, field + 4 * mols)),
+        (pair, pair, pair, pair, note, note, note),
         9 * 2 * 3 * mols * 2 * mols * (pairs // 9),
         12 * pairs,
     )(pair_local[0], pair_remote[0], pair_scale[0], y_a, e_a)
-    msg_r = take(msg[0], 1, 0)
-    msg_u = take(msg[1], 0, 1)
-    msg_c = take(msg[2], 1, 1)
+    msg_r = take(msg_r, 1, 0)
+    msg_u = take(msg_u, 0, 1)
+    msg_c = take(msg_c, 1, 1)
 
     near = take(rho_r, 0, 1, lambda x, y: y % 2 == 0)
     far = take(rho_u, 1, 0, lambda x, y: y % 2 == 1)
-    rho_c = jnp.where(lax.axis_index("gy") % 2 == 0, near, far)
 
     block = 2 * width * width * aux
     proj = 2 * width * aux * aux
@@ -280,54 +305,58 @@
         (shape(width, aux, dtype=BF), shape(width, width, dtype=BF)),
         proj + block,
         4 * size,
-    )(rho_a, metric, own)
+    )(rho_a, metric, own_a)
     proj_r, c_r = call(
         functools.partial(right_body, states),
         (shape(width, aux, dtype=BF), shape(2, width, width, dtype=BF)),
         proj + 2 * block,
         6 * size,
-    )(rho_a, rho_r, metric, proj_a, own, msg_r)
+    )(rho_a, rho_r, metric, proj_a, own_r, msg_r)
     c_u, sig = call(
         functools.partial(up_body, states),
         (shape(4, width, width, dtype=BF), shape(3, width, field // states)),
         proj + 4 * block,
         9 * size,
-    )(rho_a, rho_r, rho_u, metric, proj_a, proj_r, own, msg_r, msg_u, c_aa, c_r, y_a)
-    c_c, parts, sums = call(
+    )(rho_a, rho_r, rho_u, metric, proj_a, proj_r, own_u, msg_r, msg_u, c_aa, c_r, y_a)
+    one, two = shape(mols, field), shape(2, mols, field)
+    second = (lax.axis_index("gy") % 2).astype(jnp.int32).reshape(1, 1)
+    c_c, to_a, to_r, to_uc, sums = call(
         functools.partial(corner_body, states),
-        (shape(2, width, width, dtype=BF), shape(4, mols, field), shape(2, field)),
+        (shape(2, width, width, dtype=BF), one, one, two, shape(2, field)),
         proj + 2 * block,
         6 * size,
-    )(rho_a, rho_c, metric, proj_a, own, msg_r, msg_u, msg_c, y_a, e_a, sig)
-
-    def home(parts):
-        below = take(parts[2:4], 0, -1)
-        left = take(parts[1] + below[1], -1, 0)
-        return (parts[0] + below[0]) + left
+        smem=1,
+    )(second, rho_a, near, far, metric, proj_a, own_c, msg_r, msg_u, msg_c, y_a, e_a, sig)
+
+    def home(to_a, to_r, to_uc):
+        below = take(to_uc, 0, -1)
+        left = take(to_r + below[1], -1, 0)
+        return (to_a + below[0]) + left
 
     sums = butterfly(sums)
-    sigma = home(parts)
+    sigma = home(to_a, to_r, to_uc)
     sig_r = take(sigma, 1, 0)
-    upper = take(jnp.stack([sigma, sig_r]), 0, 1)
+    sig_uc = take(jnp.stack([sigma, sig_r]), 0, 1)
     theta, resid, squares = call(
         functools.partial(theta_body, states),
-        (shape(1, field), shape(mols, field), shape(1, field)),
+        (shape(1, field), one, shape(1, field)),
         20 * mols * field,
         12 * mols * field,
     )(sums, sigma, y_a, e_a)
-    parts2 = call(
+    to_a, to_r, to_uc = call(
         functools.partial(second_body, states),
-        shape(4, mols, field),
+        (one, one, two),
         9 * 2 * width * field * mols,
         9 * width * width * 2,
-    )(theta, resid, sig_r, upper[0], upper[1], msg_r, msg_u, msg_c, c_aa, c_r, c_u, c_c)
+    )(theta, resid, sig_r, sig_uc, msg_r, msg_u, msg_c, c_aa, c_r, c_u, c_c)
     squares = butterfly(squares)
+    raw = home(to_a, to_r, to_uc)
     corr, sigma2 = call(
         functools.partial(last_body, states, float(width * nx * ny)),
-        (shape(mols, field, dtype=BF), shape(mols, field)),
+        (shape(mols, field, dtype=BF), one),
         20 * mols * field,
         16 * mols * field,
-    )(squares, resid, home(parts2), e_a)
+    )(squares, resid, raw, e_a)
     out = (1, 1, mols, field)
     return (
         sigma.reshape(out),

time: 224 us -> 222 us (level)
  local copies, waits for them, and re-layouts: 7.41 us -> 4.81 us
  transfers between devices with their start and end apart: 29 -> 29, of which waited for: 22 -> 22; matrix products, arithmetic and copies ran while one was open for 2% -> 1% of each run, Pallas kernels for 11% -> 11%
where the time goes in v2:
time: 222 us; the launch traced here: 221 us
  waiting for transfers between devices  107 us (48%)
  starting transfers between devices  65.4 us (29%)
  Pallas kernels  37.2 us (17%)
  other arithmetic  5.92 us (3%)
  local copies, waits for them, and re-layouts  4.81 us (2%)
    ppermute x13, waiting for transfers between devices, take(): return lax.ppermute(value, AXES, table)  53.8 us
    ppermute x16, waiting for transfers between devices, butterfly(): value = value + lax.ppermute(value, AXES, table)  53.1 us
    ppermute x13, starting transfers between devices, take(): return lax.ppermute(value, AXES, table)  45.8 us
    pallas_call x8, Pallas kernels, call(): pl.pallas_call(body, out_shape=outs, in_specs=[pl.BlockSpec(memory_space=...  37.2 us
    ppermute x16, starting transfers between devices, butterfly(): value = value + lax.ppermute(value, AXES, table)  19.6 us
  transfers between devices with their start and end apart: 29, of which 22 were waited for; matrix products, arithmetic and copies ran while one was open for 1% of the time, Pallas kernels for 11%

profile of v2, /device:TPU:24, one launch (start us, length us, event | category | flops | bytes accessed | tf_op | source)
XLA Modules:
  0.0 221.0 jit_solution(937394906138604638)
XLA Ops:
  0.6 4.9 %collective-permute-start = (bf16[64,8192]{1,0:T(8,128)(2,1)}, bf16[64,8192]{1,0:T(8,128)(2,1)S(1)}, u32[]{:S(2)}, u32[]{:S(2)}) collective-permute-start(bf16[64,8192]{1,0:T(8,128)(2,1)} %bitcast.45), channel_id=1, source_target_pairs={{16,0},{17,1},{18,2},{19,3},{20,4},{21,5},{22,6},{23,7},{24,8},{25... | collective-permute-start | bytes 3145736 | tf_op jit(solution)/shard_map/ppermute | solution.py:271
  5.5 5.8 %collective-permute-start.2 = (bf16[64,8192]{1,0:T(8,128)(2,1)}, bf16[64,8192]{1,0:T(8,128)(2,1)S(1)}, u32[]{:S(2)}, u32[]{:S(2)}) collective-permute-start(bf16[64,8192]{1,0:T(8,128)(2,1)} %bitcast.46), channel_id=1, source_target_pairs={{1,0},{2,1},{3,2},{4,3},{5,4},{6,5},{7,6},{8,7},{9,8},{10,9},{11,1... | collective-permute-start | bytes 3145736 | tf_op jit(solution)/shard_map/ppermute | solution.py:271
  11.4 17.8 %collective-permute-done.rho_r = bf16[64,8192]{1,0:T(8,128)(2,1)S(1)} collective-permute-done((bf16[64,8192]{1,0:T(8,128)(2,1)}, bf16[64,8192]{1,0:T(8,128)(2,1)S(1)}, u32[]{:S(2)}, u32[]{:S(2)}) %collective-permute-start) | collective-permute-done | bytes 1048608 | tf_op jit(solution)/shard_map/ppermute | solution.py:271
  30.5 9.9 %collective-permute-done.2.rho_u = bf16[64,8192]{1,0:T(8,128)(2,1)S(1)} collective-permute-done((bf16[64,8192]{1,0:T(8,128)(2,1)}, bf16[64,8192]{1,0:T(8,128)(2,1)S(1)}, u32[]{:S(2)}, u32[]{:S(2)}) %collective-permute-start.2) | collective-permute-done | bytes 1048608 | tf_op jit(solution)/shard_map/ppermute | solution.py:271
  46.1 10.6 %collective-permute-start.4 = (f32[64,512]{1,0:T(8,128)}, f32[64,512]{1,0:T(8,128)S(1)}, u32[]{:S(2)}, u32[]{:S(2)}) collective-permute-start(f32[64,512]{1,0:T(8,128)} %get-tuple-element.33), channel_id=1, source_target_pairs={{16,0},{17,1},{18,2},{19,3},{20,4},{21,5},{22,6},{23,7},{24,8},{25... | collective-permute-start | bytes 393224 | tf_op jit(solution)/shard_map/ppermute | solution.py:271
  56.7 11.5 %collective-permute-start.5 = (f32[64,512]{1,0:T(8,128)}, f32[64,512]{1,0:T(8,128)S(1)}, u32[]{:S(2)}, u32[]{:S(2)}) collective-permute-start(f32[64,512]{1,0:T(8,128)} %get-tuple-element.34), channel_id=1, source_target_pairs={{1,0},{2,1},{3,2},{4,3},{5,4},{6,5},{7,6},{8,7},{9,8},{10,9},{11,1... | collective-permute-start | bytes 393224 | tf_op jit(solution)/shard_map/ppermute | solution.py:271
  68.2 4.4 %shard_map.103 = (bf16[512,1024]{1,0:T(8,128)(2,1)}, bf16[512,512]{1,0:T(8,128)(2,1)}) custom-call(bf16[64,8192]{1,0:T(8,128)(2,1)} %bitcast.47, bf16[1024,1024]{1,0:T(8,128)(2,1)} %metric.7, f32[64,128]{1,0:T(8,128)} %get-tuple-element.30.own), custom_call_target="tpu_custom_call" | custom-call | flops 1610612736 | bytes 4194304 | tf_op jit(solution)/shard_map/pallas_call | solution.py:23
  73.3 5.9 %shard_map.104 = (bf16[512,1024]{1,0:T(8,128)(2,1)}, bf16[2,512,512]{2,1,0:T(8,128)(2,1)}) custom-call(bf16[64,8192]{1,0:T(8,128)(2,1)} %bitcast.48, bf16[64,8192]{1,0:T(8,128)(2,1)} %copy-done.9, bf16[1024,1024]{1,0:T(8,128)(2,1)} %metric.7, bf16[512,1024]{1,0:T(8,128)(2,1)} %get-tuple-element.31.proj_a, f32[64,128]{1,0:T(8,128)} %get-tuple-element.36.own, ...), custom_call_target="tpu_custom_call" | custom-call | flops 2147483648 | bytes 6291456 | tf_op jit(solution)/shard_map/pallas_call | solution.py:23
  79.8 9.0 %shard_map.105 = (bf16[4,512,512]{2,1,0:T(8,128)(2,1)}, f32[3,512,32]{2,1,0:T(8,128)}) custom-call(bf16[64,8192]{1,0:T(8,128)(2,1)} %bitcast.49, bf16[64,8192]{1,0:T(8,128)(2,1)} %copy-done.9, bf16[64,8192]{1,0:T(8,128)(2,1)} %copy-done.10, bf16[1024,1024]{1,0:T(8,128)(2,1)} %metric.7, bf16[512,1024]{1,0:T(8,128)(2,1)} %get-tuple-element.31.proj_a, ...), custom_call_target="tpu_custom_call" | custom-call | flops 3221225472 | bytes 9437184 | tf_op jit(solution)/shard_map/pallas_call | solution.py:23
  89.8 6.9 %shard_map.106 = (bf16[2,512,512]{2,1,0:T(8,128)(2,1)}, f32[64,256]{1,0:T(8,128)}, f32[64,256]{1,0:T(8,128)}, f32[2,64,256]{2,1,0:T(8,128)}, f32[2,256]{1,0:T(2,128)}) custom-call(s32[1,1]{1,0:T(1,128)} %bitcast.second, bf16[64,8192]{1,0:T(8,128)(2,1)} %bitcast.50, bf16[64,8192]{1,0:T(8,128)(2,1)} %copy-done.8, bf16[64,8192]{1,0:T(8,128)(2,1)} %collective-permute-done.3.far, ...), custom_call_target="tpu_custom_call" | custom-call | flops 2147483648 | bytes 6291456 | tf_op jit(solution)/shard_map/pallas_call | solution.py:23
  96.7 5.3 %collective-permute-start.7 = (f32[2,64,256]{2,1,0:T(8,128)}, f32[2,64,256]{2,1,0:T(8,128)S(1)}, u32[]{:S(2)}, u32[]{:S(2)}) collective-permute-start(f32[2,64,256]{2,1,0:T(8,128)} %get-tuple-element.43), channel_id=1, source_target_pairs={{15,0},{0,1},{1,2},{2,3},{3,4},{4,5},{5,6},{6,7},{7,8},{8,9},{9,10... | collective-permute-start | bytes 393224 | tf_op jit(solution)/shard_map/ppermute | solution.py:271
  102.0 5.9 %collective-permute-done.7 = f32[2,64,256]{2,1,0:T(8,128)S(1)} collective-permute-done((f32[2,64,256]{2,1,0:T(8,128)}, f32[2,64,256]{2,1,0:T(8,128)S(1)}, u32[]{:S(2)}, u32[]{:S(2)}) %collective-permute-start.7) | collective-permute-done | bytes 131104 | tf_op jit(solution)/shard_map/ppermute | solution.py:271
  109.6 6.7 %collective-permute-done.8 = f32[64,256]{1,0:T(8,128)S(1)} collective-permute-done((f32[64,256]{1,0:T(8,128)S(1)}, f32[64,256]{1,0:T(8,128)S(1)}, u32[]{:S(2)}, u32[]{:S(2)}) %collective-permute-start.8) | collective-permute-done | bytes 65568 | tf_op jit(solution)/shard_map/ppermute | solution.py:271
  121.7 3.6 %collective-permute-start.9 = (f32[2,256]{1,0:T(2,128)}, f32[2,256]{1,0:T(2,128)S(1)}, u32[]{:S(2)}, u32[]{:S(2)}) collective-permute-start(f32[2,256]{1,0:T(2,128)} %get-tuple-element.45), channel_id=1, source_target_pairs={{2,0},{3,1},{0,2},{1,3},{6,4},{7,5},{4,6},{5,7},{10,8},{11,9},{8,1... | collective-permute-start | bytes 6152 | tf_op jit(solution)/shard_map/ppermute | solution.py:278
  125.3 4.4 %collective-permute-done.9 = f32[2,256]{1,0:T(2,128)S(1)} collective-permute-done((f32[2,256]{1,0:T(2,128)}, f32[2,256]{1,0:T(2,128)S(1)}, u32[]{:S(2)}, u32[]{:S(2)}) %collective-permute-start.9) | collective-permute-done | bytes 2080 | tf_op jit(solution)/shard_map/ppermute | solution.py:278
  130.4 3.6 %collective-permute-done.10 = f32[2,256]{1,0:T(2,128)S(1)} collective-permute-done((f32[2,256]{1,0:T(2,128)S(1)}, f32[2,256]{1,0:T(2,128)S(1)}, u32[]{:S(2)}, u32[]{:S(2)}) %collective-permute-start.10) | collective-permute-done | bytes 2080 | tf_op jit(solution)/shard_map/ppermute | solution.py:278
  134.0 5.8 %collective-permute-start.11 = (f32[2,256]{1,0:T(2,128)S(1)}, f32[2,256]{1,0:T(2,128)S(1)}, u32[]{:S(2)}, u32[]{:S(2)}) collective-permute-start(f32[2,256]{1,0:T(2,128)S(1)} %add.75), channel_id=1, source_target_pairs={{32,0},{33,1},{34,2},{35,3},{36,4},{37,5},{38,6},{39,7},{40,8},{41... | collective-permute-start | bytes 6152 | tf_op jit(solution)/shard_map/ppermute | solution.py:278
  154.7 4.0 %collective-permute-done.15 = f32[2,256]{1,0:T(2,128)S(1)} collective-permute-done((f32[2,256]{1,0:T(2,128)S(1)}, f32[2,256]{1,0:T(2,128)S(1)}, u32[]{:S(2)}, u32[]{:S(2)}) %collective-permute-start.15) | collective-permute-done | bytes 2080 | tf_op jit(solution)/shard_map/ppermute | solution.py:278
  162.7 5.0 %shard_map.108 = (f32[64,256]{1,0:T(8,128)}, f32[64,256]{1,0:T(8,128)}, f32[2,64,256]{2,1,0:T(8,128)}) custom-call(f32[1,256]{1,0:T(1,128)} %get-tuple-element.48.theta, f32[64,256]{1,0:T(8,128)} %get-tuple-element.47.resid, f32[64,256]{1,0:T(8,128)} %copy-done.1, f32[2,64,256]{2,1,0:T(8,128)} %copy-done.5, f32[64,512]{1,0:T(8,128)} %copy-done.2, ...), custom_call_target="tpu_custom_call" | custom-call | flops 150994944 | bytes 4718592 | tf_op jit(solution)/shard_map/pallas_call | solution.py:23
  167.9 10.5 %collective-permute-done.27 = f32[2,64,256]{2,1,0:T(8,128)S(1)} collective-permute-done((f32[2,64,256]{2,1,0:T(8,128)}, f32[2,64,256]{2,1,0:T(8,128)S(1)}, u32[]{:S(2)}, u32[]{:S(2)}) %collective-permute-start.27) | collective-permute-done | bytes 131104 | tf_op jit(solution)/shard_map/ppermute | solution.py:271
  181.7 7.2 %collective-permute-done.17 = f32[1,256]{1,0:T(1,128)S(1)} collective-permute-done((f32[1,256]{1,0:T(1,128)S(1)}, f32[1,256]{1,0:T(1,128)S(1)}, u32[]{:S(2)}, u32[]{:S(2)}) %collective-permute-start.17) | collective-permute-done | bytes 1056 | tf_op jit(solution)/shard_map/ppermute | solution.py:278
  192.7 4.0 %collective-permute-start.19 = (f32[1,256]{1,0:T(1,128)S(1)}, f32[1,256]{1,0:T(1,128)S(1)}, u32[]{:S(2)}, u32[]{:S(2)}) collective-permute-start(f32[1,256]{1,0:T(1,128)S(1)} %add.83), channel_id=1, source_target_pairs={{32,0},{33,1},{34,2},{35,3},{36,4},{37,5},{38,6},{39,7},{40,8},{41... | collective-permute-start | bytes 3080 | tf_op jit(solution)/shard_map/ppermute | solution.py:278
  202.1 4.8 %collective-permute-done.21 = f32[1,256]{1,0:T(1,128)S(1)} collective-permute-done((f32[1,256]{1,0:T(1,128)S(1)}, f32[1,256]{1,0:T(1,128)S(1)}, u32[]{:S(2)}, u32[]{:S(2)}) %collective-permute-start.21) | collective-permute-done | bytes 1056 | tf_op jit(solution)/shard_map/ppermute | solution.py:278
  210.5 5.1 %collective-permute-done.23 = f32[1,256]{1,0:T(1,128)S(1)} collective-permute-done((f32[1,256]{1,0:T(1,128)S(1)}, f32[1,256]{1,0:T(1,128)S(1)}, u32[]{:S(2)}, u32[]{:S(2)}) %collective-permute-start.23) | collective-permute-done | bytes 1056 | tf_op jit(solution)/shard_map/ppermute | solution.py:278
  (87 shorter events, 57.6 us)
Async XLA Ops:
  0.6 28.6 %collective-permute-start = (bf16[64,8192]{1,0:T(8,128)(2,1)}, bf16[64,8192]{1,0:T(8,128)(2,1)S(1)}, u32[]{:S(2)}, u32[]{:S(2)}) collective-permute-start(bf16[64,8192]{1,0:T(8,128)(2,1)} %bitcast.45), channel_id=1, source_target_pairs={{16,0},{17,1},{18,2},{19,3},{20,4},{21,5},{22,6},{23,7},{24,8},{25... | collective-permute-start | bytes 3145736 | tf_op jit(solution)/shard_map/ppermute | solution.py:271
  5.5 34.9 %collective-permute-start.2 = (bf16[64,8192]{1,0:T(8,128)(2,1)}, bf16[64,8192]{1,0:T(8,128)(2,1)S(1)}, u32[]{:S(2)}, u32[]{:S(2)}) collective-permute-start(bf16[64,8192]{1,0:T(8,128)(2,1)} %bitcast.46), channel_id=1, source_target_pairs={{1,0},{2,1},{3,2},{4,3},{5,4},{6,5},{7,6},{8,7},{9,8},{10,9},{11,1... | collective-permute-start | bytes 3145736 | tf_op jit(solution)/shard_map/ppermute | solution.py:271
  29.2 59.6 %collective-permute-start.1 = (bf16[64,8192]{1,0:T(8,128)(2,1)S(1)}, bf16[64,8192]{1,0:T(8,128)(2,1)S(1)}, u32[]{:S(2)}, u32[]{:S(2)}) collective-permute-start(bf16[64,8192]{1,0:T(8,128)(2,1)S(1)} %collective-permute-done.rho_r), channel_id=1, source_target_pairs={{1,0},{3,2},{5,4},{7,6},{9,8},{11,10},{13,12},{15,14},{17,16},{19,... | collective-permute-start | bytes 3145736 | tf_op jit(solution)/shard_map/ppermute | solution.py:271
  40.4 48.4 %collective-permute-start.3 = (bf16[64,8192]{1,0:T(8,128)(2,1)S(1)}, bf16[64,8192]{1,0:T(8,128)(2,1)}, u32[]{:S(2)}, u32[]{:S(2)}) collective-permute-start(bf16[64,8192]{1,0:T(8,128)(2,1)S(1)} %collective-permute-done.2.rho_u), channel_id=1, source_target_pairs={{17,1},{19,3},{21,5},{23,7},{25,9},{27,11},{29,13},{31,15},{33,17}... | collective-permute-start | bytes 3145736 | tf_op jit(solution)/shard_map/ppermute | solution.py:271
  46.1 26.6 %collective-permute-start.4 = (f32[64,512]{1,0:T(8,128)}, f32[64,512]{1,0:T(8,128)S(1)}, u32[]{:S(2)}, u32[]{:S(2)}) collective-permute-start(f32[64,512]{1,0:T(8,128)} %get-tuple-element.33), channel_id=1, source_target_pairs={{16,0},{17,1},{18,2},{19,3},{20,4},{21,5},{22,6},{23,7},{24,8},{25... | collective-permute-start | bytes 393224 | tf_op jit(solution)/shard_map/ppermute | solution.py:271
  56.7 22.5 %collective-permute-start.5 = (f32[64,512]{1,0:T(8,128)}, f32[64,512]{1,0:T(8,128)S(1)}, u32[]{:S(2)}, u32[]{:S(2)}) collective-permute-start(f32[64,512]{1,0:T(8,128)} %get-tuple-element.34), channel_id=1, source_target_pairs={{1,0},{2,1},{3,2},{4,3},{5,4},{6,5},{7,6},{8,7},{9,8},{10,9},{11,1... | collective-permute-start | bytes 393224 | tf_op jit(solution)/shard_map/ppermute | solution.py:271
  68.2 20.6 %collective-permute-start.6 = (f32[64,512]{1,0:T(8,128)}, f32[64,512]{1,0:T(8,128)S(1)}, u32[]{:S(2)}, u32[]{:S(2)}) collective-permute-start(f32[64,512]{1,0:T(8,128)} %get-tuple-element.35), channel_id=1, source_target_pairs={{17,0},{18,1},{19,2},{20,3},{21,4},{22,5},{23,6},{24,7},{25,8},{26... | collective-permute-start | bytes 393224 | tf_op jit(solution)/shard_map/ppermute | solution.py:271
  96.7 11.2 %collective-permute-start.7 = (f32[2,64,256]{2,1,0:T(8,128)}, f32[2,64,256]{2,1,0:T(8,128)S(1)}, u32[]{:S(2)}, u32[]{:S(2)}) collective-permute-start(f32[2,64,256]{2,1,0:T(8,128)} %get-tuple-element.43), channel_id=1, source_target_pairs={{15,0},{0,1},{1,2},{2,3},{3,4},{4,5},{5,6},{6,7},{7,8},{8,9},{9,10... | collective-permute-start | bytes 393224 | tf_op jit(solution)/shard_map/ppermute | solution.py:271
  108.7 7.6 %collective-permute-start.8 = (f32[64,256]{1,0:T(8,128)S(1)}, f32[64,256]{1,0:T(8,128)S(1)}, u32[]{:S(2)}, u32[]{:S(2)}) collective-permute-start(f32[64,256]{1,0:T(8,128)S(1)} %fusion.3), channel_id=1, source_target_pairs={{240,0},{241,1},{242,2},{243,3},{244,4},{245,5},{246,6},{247,7},{2... | collective-permute-start | bytes 196616 | tf_op jit(solution)/shard_map/ppermute | solution.py:271
  117.2 4.3 %collective-permute-start.25 = (f32[64,256]{1,0:T(8,128)S(1)}, f32[64,256]{1,0:T(8,128)S(1)}, u32[]{:S(2)}, u32[]{:S(2)}) collective-permute-start(f32[64,256]{1,0:T(8,128)S(1)} %fusion.5.sigma), channel_id=1, source_target_pairs={{16,0},{17,1},{18,2},{19,3},{20,4},{21,5},{22,6},{23,7},{24,8},{25... | collective-permute-start | bytes 196616 | tf_op jit(solution)/shard_map/ppermute | solution.py:271
  121.6 40.5 %collective-permute-start.26 = (f32[2,64,256]{2,1,0:T(8,128)S(1)}, f32[2,64,256]{2,1,0:T(8,128)S(1)}, u32[]{:S(2)}, u32[]{:S(2)}) collective-permute-start(f32[2,64,256]{2,1,0:T(8,128)S(1)} %pad_maximum_fusion), channel_id=1, source_target_pairs={{1,0},{2,1},{3,2},{4,3},{5,4},{6,5},{7,6},{8,7},{9,8},{10,9},{11,1... | collective-permute-start | bytes 393224 | tf_op jit(solution)/shard_map/ppermute | solution.py:271
  121.7 8.0 %collective-permute-start.9 = (f32[2,256]{1,0:T(2,128)}, f32[2,256]{1,0:T(2,128)S(1)}, u32[]{:S(2)}, u32[]{:S(2)}) collective-permute-start(f32[2,256]{1,0:T(2,128)} %get-tuple-element.45), channel_id=1, source_target_pairs={{2,0},{3,1},{0,2},{1,3},{6,4},{7,5},{4,6},{5,7},{10,8},{11,9},{8,1... | collective-permute-start | bytes 6152 | tf_op jit(solution)/shard_map/ppermute | solution.py:278
  130.4 3.6 %collective-permute-start.10 = (f32[2,256]{1,0:T(2,128)S(1)}, f32[2,256]{1,0:T(2,128)S(1)}, u32[]{:S(2)}, u32[]{:S(2)}) collective-permute-start(f32[2,256]{1,0:T(2,128)S(1)} %add.74), channel_id=1, source_target_pairs={{16,0},{17,1},{18,2},{19,3},{20,4},{21,5},{22,6},{23,7},{24,8},{25... | collective-permute-start | bytes 6152 | tf_op jit(solution)/shard_map/ppermute | solution.py:278
  134.0 7.3 %collective-permute-start.11 = (f32[2,256]{1,0:T(2,128)S(1)}, f32[2,256]{1,0:T(2,128)S(1)}, u32[]{:S(2)}, u32[]{:S(2)}) collective-permute-start(f32[2,256]{1,0:T(2,128)S(1)} %add.75), channel_id=1, source_target_pairs={{32,0},{33,1},{34,2},{35,3},{36,4},{37,5},{38,6},{39,7},{40,8},{41... | collective-permute-start | bytes 6152 | tf_op jit(solution)/shard_map/ppermute | solution.py:278
  141.3 3.6 %collective-permute-start.12 = (f32[2,256]{1,0:T(2,128)S(1)}, f32[2,256]{1,0:T(2,128)S(1)}, u32[]{:S(2)}, u32[]{:S(2)}) collective-permute-start(f32[2,256]{1,0:T(2,128)S(1)} %add.76), channel_id=1, source_target_pairs={{4,0},{5,1},{6,2},{7,3},{0,4},{1,5},{2,6},{3,7},{12,8},{13,9},{14,... | collective-permute-start | bytes 6152 | tf_op jit(solution)/shard_map/ppermute | solution.py:278
  144.9 5.1 %collective-permute-start.13 = (f32[2,256]{1,0:T(2,128)S(1)}, f32[2,256]{1,0:T(2,128)S(1)}, u32[]{:S(2)}, u32[]{:S(2)}) collective-permute-start(f32[2,256]{1,0:T(2,128)S(1)} %add.77), channel_id=1, source_target_pairs={{8,0},{9,1},{10,2},{11,3},{12,4},{13,5},{14,6},{15,7},{0,8},{1,9},... | collective-permute-start | bytes 6152 | tf_op jit(solution)/shard_map/ppermute | solution.py:278
  153.6 5.1 %collective-permute-start.15 = (f32[2,256]{1,0:T(2,128)S(1)}, f32[2,256]{1,0:T(2,128)S(1)}, u32[]{:S(2)}, u32[]{:S(2)}) collective-permute-start(f32[2,256]{1,0:T(2,128)S(1)} %add.79), channel_id=1, source_target_pairs={{128,0},{129,1},{130,2},{131,3},{132,4},{133,5},{134,6},{135,7},{1... | collective-permute-start | bytes 6152 | tf_op jit(solution)/shard_map/ppermute | solution.py:278
  167.7 10.7 %collective-permute-start.27 = (f32[2,64,256]{2,1,0:T(8,128)}, f32[2,64,256]{2,1,0:T(8,128)S(1)}, u32[]{:S(2)}, u32[]{:S(2)}) collective-permute-start(f32[2,64,256]{2,1,0:T(8,128)} %get-tuple-element.52), channel_id=1, source_target_pairs={{15,0},{0,1},{1,2},{2,3},{3,4},{4,5},{5,6},{6,7},{7,8},{8,9},{9,10... | collective-permute-start | bytes 393224 | tf_op jit(solution)/shard_map/ppermute | solution.py:271
  179.3 38.0 %collective-permute-start.28 = (f32[64,256]{1,0:T(8,128)S(1)}, f32[64,256]{1,0:T(8,128)S(1)}, u32[]{:S(2)}, u32[]{:S(2)}) collective-permute-start(f32[64,256]{1,0:T(8,128)S(1)} %fusion), channel_id=1, source_target_pairs={{240,0},{241,1},{242,2},{243,3},{244,4},{245,5},{246,6},{247,7},{2... | collective-permute-start | bytes 196616 | tf_op jit(solution)/shard_map/ppermute | solution.py:271
  181.4 7.5 %collective-permute-start.17 = (f32[1,256]{1,0:T(1,128)S(1)}, f32[1,256]{1,0:T(1,128)S(1)}, u32[]{:S(2)}, u32[]{:S(2)}) collective-permute-start(f32[1,256]{1,0:T(1,128)S(1)} %copy-done.7), channel_id=1, source_target_pairs={{2,0},{3,1},{0,2},{1,3},{6,4},{7,5},{4,6},{5,7},{10,8},{11,9},{8,1... | collective-permute-start | bytes 3080 | tf_op jit(solution)/shard_map/ppermute | solution.py:278
  188.9 3.8 %collective-permute-start.18 = (f32[1,256]{1,0:T(1,128)S(1)}, f32[1,256]{1,0:T(1,128)S(1)}, u32[]{:S(2)}, u32[]{:S(2)}) collective-permute-start(f32[1,256]{1,0:T(1,128)S(1)} %add.82), channel_id=1, source_target_pairs={{16,0},{17,1},{18,2},{19,3},{20,4},{21,5},{22,6},{23,7},{24,8},{25... | collective-permute-start | bytes 3080 | tf_op jit(solution)/shard_map/ppermute | solution.py:278
  192.7 5.5 %collective-permute-start.19 = (f32[1,256]{1,0:T(1,128)S(1)}, f32[1,256]{1,0:T(1,128)S(1)}, u32[]{:S(2)}, u32[]{:S(2)}) collective-permute-start(f32[1,256]{1,0:T(1,128)S(1)} %add.83), channel_id=1, source_target_pairs={{32,0},{33,1},{34,2},{35,3},{36,4},{37,5},{38,6},{39,7},{40,8},{41... | collective-permute-start | bytes 3080 | tf_op jit(solution)/shard_map/ppermute | solution.py:278
  201.8 5.1 %collective-permute-start.21 = (f32[1,256]{1,0:T(1,128)S(1)}, f32[1,256]{1,0:T(1,128)S(1)}, u32[]{:S(2)}, u32[]{:S(2)}) collective-permute-start(f32[1,256]{1,0:T(1,128)S(1)} %add.85), channel_id=1, source_target_pairs={{8,0},{9,1},{10,2},{11,3},{12,4},{13,5},{14,6},{15,7},{0,8},{1,9},... | collective-permute-start | bytes 3080 | tf_op jit(solution)/shard_map/ppermute | solution.py:278
  210.5 5.1 %collective-permute-start.23 = (f32[1,256]{1,0:T(1,128)S(1)}, f32[1,256]{1,0:T(1,128)S(1)}, u32[]{:S(2)}, u32[]{:S(2)}) collective-permute-start(f32[1,256]{1,0:T(1,128)S(1)} %add.87), channel_id=1, source_target_pairs={{128,0},{129,1},{130,2},{131,3},{132,4},{133,5},{134,6},{135,7},{1... | collective-permute-start | bytes 3080 | tf_op jit(solution)/shard_map/ppermute | solution.py:278
  (16 other events, 250.8 us)

commit v3 on v2

--- a/solution.py
+++ b/solution.py
@@ -19,13 +19,13 @@
     return [pl.BlockSpec(memory_space=pltpu.VMEM)] * count
 
 
-def call(body, outs, flops, moved, smem=0):
+def call(body, outs, flops, moved, smem=0, limit=24):
     return lambda *args: pl.pallas_call(
         body,
         out_shape=outs,
         in_specs=[pl.BlockSpec(memory_space=pltpu.SMEM)] * smem + vmem(len(args) - smem),
         out_specs=jax.tree.map(lambda _: pl.BlockSpec(memory_space=pltpu.VMEM), outs),
-        compiler_params=pltpu.CompilerParams(vmem_limit_bytes=60 * 2**20),
+        compiler_params=pltpu.CompilerParams(vmem_limit_bytes=limit * 2**20),
         cost_estimate=pl.CostEstimate(flops=flops, bytes_accessed=moved, transcendentals=0),
     )(*args)
 
@@ -118,34 +118,34 @@
     c_aa[...] = couple(proj[...], rows, own[...])
 
 
-def right_body(states, rho_a, rho_r, metric, proj_a, own, msg_r, proj_r, c):
+def first_body(states, rho_a, rho_u, metric, proj_a, own, msg_u, proj_u, c):
     mols = rho_a.shape[0]
-    rows_a, rows_r = stack(rho_a, states), stack(rho_r, states)
-    field = msg_r.shape[1] - 4 * mols
-    c[0] = couple(proj_a[...], rows_r, own[...])
-    proj_r[...] = dot(rows_r, metric[...]).astype(BF)
-    c[1] = couple(proj_r[...], rows_a, twice(msg_r[:, field : field + mols]))
-
-
-def up_body(
-    states, rho_a, rho_r, rho_u, metric, proj_a, proj_r, own, msg_r, msg_u, c_aa, c_r, y_a, c, sig
+    field = msg_u.shape[1] - 4 * mols
+    rows_a, rows_u = stack(rho_a, states), stack(rho_u, states)
+    c[0] = couple(proj_a[...], rows_u, own[...])
+    proj_u[...] = dot(rows_u, metric[...]).astype(BF)
+    c[1] = couple(proj_u[...], rows_a, twice(msg_u[:, field : field + mols]))
+
+
+def next_body(
+    states, rho_a, rho_u, rho_r, metric, proj_a, proj_u, own, msg_u, msg_r, c_aa, c_u, y_a, c, sig
 ):
     mols = rho_a.shape[0]
     field = msg_r.shape[1] - 4 * mols
-    rows_u = stack(rho_u, states)
-    c[0] = couple(proj_a[...], rows_u, own[...])
-    c[1] = couple(proj_r[...], rows_u, twice(msg_r[:, field + mols : field + 2 * mols]))
-    proj_u = dot(rows_u, metric[...]).astype(BF)
-    c[2] = couple(proj_u, stack(rho_a, states), twice(msg_u[:, field : field + mols]))
+    rows_r = stack(rho_r, states)
+    c[0] = couple(proj_a[...], rows_r, own[...])
+    c[1] = couple(proj_u[...], rows_r, twice(msg_u[:, field + mols : field + 2 * mols]))
+    proj_r = dot(rows_r, metric[...]).astype(BF)
+    c[2] = couple(proj_r, stack(rho_a, states), twice(msg_r[:, field : field + mols]))
     c[3] = couple(
-        proj_u, stack(rho_r, states), twice(msg_u[:, field + mols : field + 2 * mols])
+        proj_r, stack(rho_u, states), twice(msg_r[:, field + mols : field + 2 * mols])
     )
     f_a = stack(y_a, states)
     f_r = stack(msg_r[:, :field], states).astype(BF)
     f_u = stack(msg_u[:, :field], states).astype(BF)
-    sig[0] = dot(c_aa[...], f_a) + (dot(c_r[0], f_r) + dot(c[0], f_u))
-    sig[1] = dot(c_r[1], f_a) + dot(c[1], f_u)
-    sig[2] = dot(c[2], f_a) + dot(c[3], f_r)
+    sig[0] = dot(c_aa[...], f_a) + (dot(c_u[0], f_u) + dot(c[0], f_r))
+    sig[1] = dot(c[2], f_a) + dot(c[3], f_u)
+    sig[2] = dot(c_u[1], f_a) + dot(c[1], f_r)
 
 
 def corner_body(
@@ -210,10 +210,12 @@
     return (sigma - theta * y) / jnp.maximum(jnp.abs(spread(e, width) - theta), 1.0)
 
 
-def theta_body(states, sums, sigma, y_a, e_a, theta, resid, squares):
+def theta_body(states, part, rest, sigma, y_a, e_a, theta, short, resid, squares):
     width = sigma.shape[1] // states
+    sums = part[...] + rest[...]
     rate = over_states(sums[0:1], width) / over_states(sums[1:2], width)
     theta[...] = rate
+    short[...] = rate[:, :width]
     value = residual(sigma[...], y_a[...].astype(F32), e_a[...], rate, width)
     resid[...] = value
     squares[...] = jnp.sum(value * value, axis=0, keepdims=True)
@@ -234,19 +236,20 @@
     f_r = other(sig_r[...], msg_r)
     f_u = other(sig_uc[0], msg_u)
     f_c = other(sig_uc[1], msg_c)
-    row_a = (dot(c_aa[...], f_a) + dot(c_r[0], f_r)) + (dot(c_u[0], f_u) + dot(c_c[0], f_c))
+    row_a = (dot(c_aa[...], f_a) + dot(c_u[0], f_u)) + (dot(c_r[0], f_r) + dot(c_c[0], f_c))
     to_a[...] = unstack(row_a, states)
-    to_r[...] = unstack(dot(c_r[1], f_a) + dot(c_u[1], f_u), states)
-    to_uc[0] = unstack(dot(c_u[2], f_a) + dot(c_u[3], f_r), states)
+    to_r[...] = unstack(dot(c_r[2], f_a) + dot(c_r[3], f_u), states)
+    to_uc[0] = unstack(dot(c_u[1], f_a) + dot(c_r[1], f_r), states)
     to_uc[1] = unstack(dot(c_c[1], f_a), states)
 
 
-def last_body(states, count, squares, resid, raw, e_a, corr, sigma):
+def last_body(states, count, part, rest, resid, to_a, below, left, e_a, corr, sigma):
     width = resid.shape[1] // states
-    scale = jnp.sqrt(over_states(squares[...], width) / count + 1e-06)
+    scale = jnp.sqrt(over_states(part[...] + rest[...], width) / count + 1e-06)
     value = (resid[...] / scale).astype(BF)
     corr[...] = value
-    sigma[...] = raw[...] / scale + spread(e_a[...], width) * value.astype(F32)
+    raw = (to_a[...] + below[0]) + left[...]
+    sigma[...] = raw / scale + spread(e_a[...], width) * value.astype(F32)
 
 
 def shards(densities, trials, energies, metric, pair_local, pair_remote, pair_scale):
@@ -270,16 +273,36 @@
         ]
         return lax.ppermute(value, AXES, table)
 
-    flips = [(0, 2), (1, 0), (2, 0), (0, 4), (0, 8), (4, 0), (8, 0), (0, 1)]
+    def along_z(table):
+        def partner(x, y):
+            z = table[(y // 2 % 2) * 4 + x % 4]
+            return x // 4 * 4 + z % 4, y // 4 * 4 + z // 4 * 2 + y % 2
+
+        return partner
+
+    def flip(fx, fy):
+        return lambda x, y: (x ^ fx, y ^ fy)
+
+    steps = [
+        along_z((3, 6, 5, 0, 7, 2, 1, 4)),
+        along_z((7, 2, 1, 4, 3, 6, 5, 0)),
+        along_z((1, 0, 3, 2, 5, 4, 7, 6)),
+        flip(0, 4),
+        flip(0, 12),
+        flip(4, 0),
+        flip(12, 0),
+        flip(0, 1),
+    ]
 
     def butterfly(value):
-        for fx, fy in flips:
-            table = [(spot(x ^ fx, y ^ fy), spot(x, y)) for x in range(nx) for y in range(ny)]
-            value = value + lax.ppermute(value, AXES, table)
-        return value
+        for k, partner in enumerate(steps):
+            table = [(spot(*partner(x, y)), spot(x, y)) for x in range(nx) for y in range(ny)]
+            other = lax.ppermute(value, AXES, table)
+            if k == len(steps) - 1:
+                return value, other
+            value = value + other
 
     rho_a, y_a, e_a = densities[0, 0], trials[0, 0], energies[0, 0]
-    rho_r = take(rho_a, 1, 0)
     rho_u = take(rho_a, 0, 1)
 
     pair = shape(mols, 2 * mols)
@@ -294,6 +317,7 @@
     msg_u = take(msg_u, 0, 1)
     msg_c = take(msg_c, 1, 1)
 
+    rho_r = take(rho_a, 1, 0)
     near = take(rho_r, 0, 1, lambda x, y: y % 2 == 0)
     far = take(rho_u, 1, 0, lambda x, y: y % 2 == 1)
 
@@ -306,18 +330,18 @@
         proj + block,
         4 * size,
     )(rho_a, metric, own_a)
-    proj_r, c_r = call(
-        functools.partial(right_body, states),
+    proj_u, c_u = call(
+        functools.partial(first_body, states),
         (shape(width, aux, dtype=BF), shape(2, width, width, dtype=BF)),
         proj + 2 * block,
         6 * size,
-    )(rho_a, rho_r, metric, proj_a, own_r, msg_r)
-    c_u, sig = call(
-        functools.partial(up_body, states),
+    )(rho_a, rho_u, metric, proj_a, own_u, msg_u)
+    c_r, sig = call(
+        functools.partial(next_body, states),
         (shape(4, width, width, dtype=BF), shape(3, width, field // states)),
         proj + 4 * block,
         9 * size,
-    )(rho_a, rho_r, rho_u, metric, proj_a, proj_r, own_u, msg_r, msg_u, c_aa, c_r, y_a)
+    )(rho_a, rho_u, rho_r, metric, proj_a, proj_u, own_r, msg_u, msg_r, c_aa, c_u, y_a)
     one, two = shape(mols, field), shape(2, mols, field)
     second = (lax.axis_index("gy") % 2).astype(jnp.int32).reshape(1, 1)
     c_c, to_a, to_r, to_uc, sums = call(
@@ -328,21 +352,22 @@
         smem=1,
     )(second, rho_a, near, far, metric, proj_a, own_c, msg_r, msg_u, msg_c, y_a, e_a, sig)
 
-    def home(to_a, to_r, to_uc):
+    def home(to_r, to_uc):
         below = take(to_uc, 0, -1)
         left = take(to_r + below[1], -1, 0)
-        return (to_a + below[0]) + left
+        return below, left
 
     sums = butterfly(sums)
-    sigma = home(to_a, to_r, to_uc)
+    below, left = home(to_r, to_uc)
+    sigma = (to_a + below[0]) + left
     sig_r = take(sigma, 1, 0)
     sig_uc = take(jnp.stack([sigma, sig_r]), 0, 1)
-    theta, resid, squares = call(
+    theta, short, resid, squares = call(
         functools.partial(theta_body, states),
-        (shape(1, field), one, shape(1, field)),
+        (shape(1, field), shape(1, field // states), one, shape(1, field)),
         20 * mols * field,
         12 * mols * field,
-    )(sums, sigma, y_a, e_a)
+    )(*sums, sigma, y_a, e_a)
     to_a, to_r, to_uc = call(
         functools.partial(second_body, states),
         (one, one, two),
@@ -350,19 +375,19 @@
         9 * width * width * 2,
     )(theta, resid, sig_r, sig_uc, msg_r, msg_u, msg_c, c_aa, c_r, c_u, c_c)
     squares = butterfly(squares)
-    raw = home(to_a, to_r, to_uc)
+    below, left = home(to_r, to_uc)
     corr, sigma2 = call(
         functools.partial(last_body, states, float(width * nx * ny)),
         (shape(mols, field, dtype=BF), one),
         20 * mols * field,
         16 * mols * field,
-    )(squares, resid, raw, e_a)
+    )(*squares, resid, to_a, below, left, e_a)
     out = (1, 1, mols, field)
     return (
         sigma.reshape(out),
         corr.reshape(out),
         sigma2.reshape(out),
-        theta[0, : field // states],
+        short.reshape(field // states),
     )
 
 

time: 222 us -> 206 us (0.928)
  Pallas kernels: 37.2 us -> 18.4 us
  waiting for transfers between devices: 107 us -> 122 us
  starting transfers between devices: 65.4 us -> 55.6 us
  other arithmetic: 5.92 us -> 0.09 us
    pallas_call x8, Pallas kernels: 37.2 us -> 18.4 us  [call(): pl.pallas_call(body, out_shape=outs, in_specs=[pl.BlockSpec(memory_space=...]
    ppermute x13, waiting for transfers between devices: 53.8 us -> 70.4 us  [take(): return lax.ppermute(value, AXES, table)]
    ppermute x13, starting transfers between devices: 45.8 us -> 33.4 us  [take(): return lax.ppermute(value, AXES, table)]
    add x18 -> x15, other arithmetic: 4.21 us -> 0.06 us  [the longest x14 0.04 us: butterfly(): value = value + other]
    ppermute x16, starting transfers between devices: 19.6 us -> 22.2 us  [butterfly(): other = lax.ppermute(value, AXES, table)]
    unnamed x23 -> x21, local copies, waits for them, and re-layouts: 4.3 us -> 6.6 us
  transfers between devices with their start and end apart: 29 -> 29, of which waited for: 22 -> 22; matrix products, arithmetic and copies ran while one was open for 1% -> 0% of each run, Pallas kernels for 11% -> 6%
where the time goes in v3:
time: 206 us; the launch traced here: 203 us
  waiting for transfers between devices  122 us (59%)
  starting transfers between devices  55.6 us (27%)
  Pallas kernels  18.4 us (9%)
  local copies, waits for them, and re-layouts  6.6 us (3%)
    ppermute x13, waiting for transfers between devices, take(): return lax.ppermute(value, AXES, table)  70.4 us
    ppermute x16, waiting for transfers between devices, butterfly(): other = lax.ppermute(value, AXES, table)  51.6 us
    ppermute x13, starting transfers between devices, take(): return lax.ppermute(value, AXES, table)  33.4 us
    ppermute x16, starting transfers between devices, butterfly(): other = lax.ppermute(value, AXES, table)  22.2 us
    pallas_call x8, Pallas kernels, call(): pl.pallas_call(body, out_shape=outs, in_specs=[pl.BlockSpec(memory_space=...  18.4 us
    unnamed x21, local copies, waits for them, and re-layouts  6.6 us
  transfers between devices with their start and end apart: 29, of which 22 were waited for; matrix products, arithmetic and copies ran while one was open for 0% of the time, Pallas kernels for 6%

profile of v3, /device:TPU:24, one launch (start us, length us, event | category | flops | bytes accessed | tf_op | source)
XLA Modules:
  0.0 203.4 jit_solution(6954046238395167189)
XLA Ops:
  0.6 8.9 %collective-permute-start.2 = (bf16[64,8192]{1,0:T(8,128)(2,1)}, bf16[64,8192]{1,0:T(8,128)(2,1)S(1)}, u32[]{:S(2)}, u32[]{:S(2)}) collective-permute-start(bf16[64,8192]{1,0:T(8,128)(2,1)} %bitcast.38), channel_id=1, source_target_pairs={{1,0},{2,1},{3,2},{4,3},{5,4},{6,5},{7,6},{8,7},{9,8},{10,9},{11,1... | collective-permute-start | bytes 3145736 | tf_op jit(solution)/shard_map/ppermute | solution.py:274
  11.6 18.3 %collective-permute-done.2.rho_u = bf16[64,8192]{1,0:T(8,128)(2,1)S(1)} collective-permute-done((bf16[64,8192]{1,0:T(8,128)(2,1)}, bf16[64,8192]{1,0:T(8,128)(2,1)S(1)}, u32[]{:S(2)}, u32[]{:S(2)}) %collective-permute-start.2) | collective-permute-done | bytes 1048608 | tf_op jit(solution)/shard_map/ppermute | solution.py:274
  30.7 23.6 %collective-permute-done.rho_r = bf16[64,8192]{1,0:T(8,128)(2,1)} collective-permute-done((bf16[64,8192]{1,0:T(8,128)(2,1)}, bf16[64,8192]{1,0:T(8,128)(2,1)}, u32[]{:S(2)}, u32[]{:S(2)}) %collective-permute-start) | collective-permute-done | bytes 1048608 | tf_op jit(solution)/shard_map/ppermute | solution.py:274
  60.5 16.1 %collective-permute-start.5 = (f32[64,512]{1,0:T(8,128)S(1)}, f32[64,512]{1,0:T(8,128)S(1)}, u32[]{:S(2)}, u32[]{:S(2)}) collective-permute-start(f32[64,512]{1,0:T(8,128)S(1)} %get-tuple-element.35), channel_id=1, source_target_pairs={{1,0},{2,1},{3,2},{4,3},{5,4},{6,5},{7,6},{8,7},{9,8},{10,9},{11,1... | collective-permute-start | bytes 393224 | tf_op jit(solution)/shard_map/ppermute | solution.py:274
  83.6 5.9 %shard_map.105 = (bf16[4,512,512]{2,1,0:T(8,128)(2,1)S(1)}, f32[3,512,32]{2,1,0:T(8,128)S(1)}) custom-call(bf16[64,8192]{1,0:T(8,128)(2,1)S(1)} %bitcast.42, bf16[64,8192]{1,0:T(8,128)(2,1)S(1)} %collective-permute-done.2.rho_u, bf16[64,8192]{1,0:T(8,128)(2,1)} %collective-permute-done.rho_r, bf16[1024,1024]{1,0:T(8,128)(2,1)S(1)} %copy-done.4, ...), custom_call_target="tpu_custom_call" | custom-call | flops 3221225472 | bytes 9437184 | tf_op jit(solution)/shard_map/pallas_call | solution.py:23
  89.6 4.0 %shard_map.106 = (bf16[2,512,512]{2,1,0:T(8,128)(2,1)S(1)}, f32[64,256]{1,0:T(8,128)S(1)}, f32[64,256]{1,0:T(8,128)S(1)}, f32[2,64,256]{2,1,0:T(8,128)S(1)}, f32[2,256]{1,0:T(2,128)S(1)}) custom-call(s32[1,1]{1,0:T(1,128)} %bitcast.second, bf16[64,8192]{1,0:T(8,128)(2,1)S(1)} %bitcast.43, bf16[64,8192]{1,0:T(8,128)(2,1)} %collective-permute-done.1.near, ...), custom_call_target="tpu_custom_call" | custom-call | flops 2147483648 | bytes 6291456 | tf_op jit(solution)/shard_map/pallas_call | solution.py:23
  93.7 10.5 %collective-permute-done.7 = f32[2,64,256]{2,1,0:T(8,128)S(1)} collective-permute-done((f32[2,64,256]{2,1,0:T(8,128)S(1)}, f32[2,64,256]{2,1,0:T(8,128)S(1)}, u32[]{:S(2)}, u32[]{:S(2)}) %collective-permute-start.7) | collective-permute-done | bytes 131104 | tf_op jit(solution)/shard_map/ppermute | solution.py:274
  104.2 3.7 %collective-permute-start.8 = (f32[64,256]{1,0:T(8,128)S(1)}, f32[64,256]{1,0:T(8,128)S(1)}, u32[]{:S(2)}, u32[]{:S(2)}) collective-permute-start(f32[64,256]{1,0:T(8,128)S(1)} %fusion.1), channel_id=1, source_target_pairs={{240,0},{241,1},{242,2},{243,3},{244,4},{245,5},{246,6},{247,7},{2... | collective-permute-start | bytes 196616 | tf_op jit(solution)/shard_map/ppermute | solution.py:274
  107.9 3.3 %collective-permute-done.8 = f32[64,256]{1,0:T(8,128)S(1)} collective-permute-done((f32[64,256]{1,0:T(8,128)S(1)}, f32[64,256]{1,0:T(8,128)S(1)}, u32[]{:S(2)}, u32[]{:S(2)}) %collective-permute-start.8) | collective-permute-done | bytes 65568 | tf_op jit(solution)/shard_map/ppermute | solution.py:274
  111.4 4.2 %collective-permute-done.25.sig_r = f32[64,256]{1,0:T(8,128)S(1)} collective-permute-done((f32[64,256]{1,0:T(8,128)S(1)}, f32[64,256]{1,0:T(8,128)S(1)}, u32[]{:S(2)}, u32[]{:S(2)}) %collective-permute-start.25) | collective-permute-done | bytes 65568 | tf_op jit(solution)/shard_map/ppermute | solution.py:274
  115.7 5.0 %collective-permute-start.9 = (f32[2,256]{1,0:T(2,128)S(1)}, f32[2,256]{1,0:T(2,128)S(1)}, u32[]{:S(2)}, u32[]{:S(2)}) collective-permute-start(f32[2,256]{1,0:T(2,128)S(1)} %get-tuple-element.46), channel_id=1, source_target_pairs={{48,0},{49,1},{50,2},{51,3},{52,4},{53,5},{54,6},{55,7},{56,8},{57... | collective-permute-start | bytes 6152 | tf_op jit(solution)/shard_map/ppermute | solution.py:300
  123.4 4.8 %collective-permute-done.10 = f32[2,256]{1,0:T(2,128)S(1)} collective-permute-done((f32[2,256]{1,0:T(2,128)S(1)}, f32[2,256]{1,0:T(2,128)S(1)}, u32[]{:S(2)}, u32[]{:S(2)}) %collective-permute-start.10) | collective-permute-done | bytes 2080 | tf_op jit(solution)/shard_map/ppermute | solution.py:300
  131.7 3.6 %collective-permute-done.12 = f32[2,256]{1,0:T(2,128)S(1)} collective-permute-done((f32[2,256]{1,0:T(2,128)S(1)}, f32[2,256]{1,0:T(2,128)S(1)}, u32[]{:S(2)}, u32[]{:S(2)}) %collective-permute-start.12) | collective-permute-done | bytes 2080 | tf_op jit(solution)/shard_map/ppermute | solution.py:300
  135.3 4.8 %collective-permute-done.13 = f32[2,256]{1,0:T(2,128)S(1)} collective-permute-done((f32[2,256]{1,0:T(2,128)S(1)}, f32[2,256]{1,0:T(2,128)S(1)}, u32[]{:S(2)}, u32[]{:S(2)}) %collective-permute-start.13) | collective-permute-done | bytes 2080 | tf_op jit(solution)/shard_map/ppermute | solution.py:300
  140.2 3.6 %collective-permute-done.14 = f32[2,256]{1,0:T(2,128)S(1)} collective-permute-done((f32[2,256]{1,0:T(2,128)S(1)}, f32[2,256]{1,0:T(2,128)S(1)}, u32[]{:S(2)}, u32[]{:S(2)}) %collective-permute-start.14) | collective-permute-done | bytes 2080 | tf_op jit(solution)/shard_map/ppermute | solution.py:300
  143.7 8.1 %collective-permute-start.15 = (f32[2,256]{1,0:T(2,128)S(1)}, f32[2,256]{1,0:T(2,128)S(1)}, u32[]{:S(2)}, u32[]{:S(2)}) collective-permute-start(f32[2,256]{1,0:T(2,128)S(1)} %add.67), channel_id=1, source_target_pairs={{192,0},{193,1},{194,2},{195,3},{196,4},{197,5},{198,6},{199,7},{2... | collective-permute-start | bytes 6152 | tf_op jit(solution)/shard_map/ppermute | solution.py:300
  157.2 10.3 %collective-permute-done.27.below = f32[2,64,256]{2,1,0:T(8,128)S(1)} collective-permute-done((f32[2,64,256]{2,1,0:T(8,128)S(1)}, f32[2,64,256]{2,1,0:T(8,128)S(1)}, u32[]{:S(2)}, u32[]{:S(2)}) %collective-permute-start.27) | collective-permute-done | bytes 131104 | tf_op jit(solution)/shard_map/ppermute | solution.py:274
  167.6 6.5 %collective-permute-start.17 = (f32[1,256]{1,0:T(1,128)S(1)}, f32[1,256]{1,0:T(1,128)S(1)}, u32[]{:S(2)}, u32[]{:S(2)}) collective-permute-start(f32[1,256]{1,0:T(1,128)S(1)} %get-tuple-element.47), channel_id=1, source_target_pairs={{48,0},{49,1},{50,2},{51,3},{52,4},{53,5},{54,6},{55,7},{56,8},{57... | collective-permute-start | bytes 3080 | tf_op jit(solution)/shard_map/ppermute | solution.py:300
  177.6 3.5 %collective-permute-done.18 = f32[1,256]{1,0:T(1,128)S(1)} collective-permute-done((f32[1,256]{1,0:T(1,128)S(1)}, f32[1,256]{1,0:T(1,128)S(1)}, u32[]{:S(2)}, u32[]{:S(2)}) %collective-permute-start.18) | collective-permute-done | bytes 1056 | tf_op jit(solution)/shard_map/ppermute | solution.py:300
  181.1 3.6 %collective-permute-done.19 = f32[1,256]{1,0:T(1,128)S(1)} collective-permute-done((f32[1,256]{1,0:T(1,128)S(1)}, f32[1,256]{1,0:T(1,128)S(1)}, u32[]{:S(2)}, u32[]{:S(2)}) %collective-permute-start.19) | collective-permute-done | bytes 1056 | tf_op jit(solution)/shard_map/ppermute | solution.py:300
  184.7 3.6 %collective-permute-done.20 = f32[1,256]{1,0:T(1,128)S(1)} collective-permute-done((f32[1,256]{1,0:T(1,128)S(1)}, f32[1,256]{1,0:T(1,128)S(1)}, u32[]{:S(2)}, u32[]{:S(2)}) %collective-permute-start.20) | collective-permute-done | bytes 1056 | tf_op jit(solution)/shard_map/ppermute | solution.py:300
  188.3 4.8 %collective-permute-done.21 = f32[1,256]{1,0:T(1,128)S(1)} collective-permute-done((f32[1,256]{1,0:T(1,128)S(1)}, f32[1,256]{1,0:T(1,128)S(1)}, u32[]{:S(2)}, u32[]{:S(2)}) %collective-permute-start.21) | collective-permute-done | bytes 1056 | tf_op jit(solution)/shard_map/ppermute | solution.py:300
  193.1 3.6 %collective-permute-done.22 = f32[1,256]{1,0:T(1,128)S(1)} collective-permute-done((f32[1,256]{1,0:T(1,128)S(1)}, f32[1,256]{1,0:T(1,128)S(1)}, u32[]{:S(2)}, u32[]{:S(2)}) %collective-permute-start.22) | collective-permute-done | bytes 1056 | tf_op jit(solution)/shard_map/ppermute | solution.py:300
  197.6 3.8 %collective-permute-done.23 = f32[1,256]{1,0:T(1,128)S(1)} collective-permute-done((f32[1,256]{1,0:T(1,128)S(1)}, f32[1,256]{1,0:T(1,128)S(1)}, u32[]{:S(2)}, u32[]{:S(2)}) %collective-permute-start.23) | collective-permute-done | bytes 1056 | tf_op jit(solution)/shard_map/ppermute | solution.py:300
  (81 shorter events, 34.6 us)
Async XLA Ops:
  0.6 29.3 %collective-permute-start.2 = (bf16[64,8192]{1,0:T(8,128)(2,1)}, bf16[64,8192]{1,0:T(8,128)(2,1)S(1)}, u32[]{:S(2)}, u32[]{:S(2)}) collective-permute-start(bf16[64,8192]{1,0:T(8,128)(2,1)} %bitcast.38), channel_id=1, source_target_pairs={{1,0},{2,1},{3,2},{4,3},{5,4},{6,5},{7,6},{8,7},{9,8},{10,9},{11,1... | collective-permute-start | bytes 3145736 | tf_op jit(solution)/shard_map/ppermute | solution.py:274
  9.5 44.8 %collective-permute-start = (bf16[64,8192]{1,0:T(8,128)(2,1)}, bf16[64,8192]{1,0:T(8,128)(2,1)}, u32[]{:S(2)}, u32[]{:S(2)}) collective-permute-start(bf16[64,8192]{1,0:T(8,128)(2,1)} %bitcast.39), channel_id=1, source_target_pairs={{16,0},{17,1},{18,2},{19,3},{20,4},{21,5},{22,6},{23,7},{24,8},{25... | collective-permute-start | bytes 3145736 | tf_op jit(solution)/shard_map/ppermute | solution.py:274
  30.0 59.6 %collective-permute-start.3 = (bf16[64,8192]{1,0:T(8,128)(2,1)S(1)}, bf16[64,8192]{1,0:T(8,128)(2,1)S(1)}, u32[]{:S(2)}, u32[]{:S(2)}) collective-permute-start(bf16[64,8192]{1,0:T(8,128)(2,1)S(1)} %collective-permute-done.2.rho_u), channel_id=1, source_target_pairs={{17,1},{19,3},{21,5},{23,7},{25,9},{27,11},{29,13},{31,15},{33,17}... | collective-permute-start | bytes 3145736 | tf_op jit(solution)/shard_map/ppermute | solution.py:274
  54.3 35.3 %collective-permute-start.1 = (bf16[64,8192]{1,0:T(8,128)(2,1)}, bf16[64,8192]{1,0:T(8,128)(2,1)}, u32[]{:S(2)}, u32[]{:S(2)}) collective-permute-start(bf16[64,8192]{1,0:T(8,128)(2,1)} %collective-permute-done.rho_r), channel_id=1, source_target_pairs={{1,0},{3,2},{5,4},{7,6},{9,8},{11,10},{13,12},{15,14},{17,16},{19,... | collective-permute-start | bytes 3145736 | tf_op jit(solution)/shard_map/ppermute | solution.py:274
  60.5 20.7 %collective-permute-start.5 = (f32[64,512]{1,0:T(8,128)S(1)}, f32[64,512]{1,0:T(8,128)S(1)}, u32[]{:S(2)}, u32[]{:S(2)}) collective-permute-start(f32[64,512]{1,0:T(8,128)S(1)} %get-tuple-element.35), channel_id=1, source_target_pairs={{1,0},{2,1},{3,2},{4,3},{5,4},{6,5},{7,6},{8,7},{9,8},{10,9},{11,1... | collective-permute-start | bytes 393224 | tf_op jit(solution)/shard_map/ppermute | solution.py:274
  76.5 7.1 %collective-permute-start.4 = (f32[64,512]{1,0:T(8,128)S(1)}, f32[64,512]{1,0:T(8,128)S(1)}, u32[]{:S(2)}, u32[]{:S(2)}) collective-permute-start(f32[64,512]{1,0:T(8,128)S(1)} %get-tuple-element.34), channel_id=1, source_target_pairs={{16,0},{17,1},{18,2},{19,3},{20,4},{21,5},{22,6},{23,7},{24,8},{25... | collective-permute-start | bytes 393224 | tf_op jit(solution)/shard_map/ppermute | solution.py:274
  76.5 13.0 %collective-permute-start.6 = (f32[64,512]{1,0:T(8,128)S(1)}, f32[64,512]{1,0:T(8,128)S(1)}, u32[]{:S(2)}, u32[]{:S(2)}) collective-permute-start(f32[64,512]{1,0:T(8,128)S(1)} %get-tuple-element.36), channel_id=1, source_target_pairs={{17,0},{18,1},{19,2},{20,3},{21,4},{22,5},{23,6},{24,7},{25,8},{26... | collective-permute-start | bytes 393224 | tf_op jit(solution)/shard_map/ppermute | solution.py:274
  93.6 10.6 %collective-permute-start.7 = (f32[2,64,256]{2,1,0:T(8,128)S(1)}, f32[2,64,256]{2,1,0:T(8,128)S(1)}, u32[]{:S(2)}, u32[]{:S(2)}) collective-permute-start(f32[2,64,256]{2,1,0:T(8,128)S(1)} %get-tuple-element.44), channel_id=1, source_target_pairs={{15,0},{0,1},{1,2},{2,3},{3,4},{4,5},{5,6},{6,7},{7,8},{8,9},{9,10... | collective-permute-start | bytes 393224 | tf_op jit(solution)/shard_map/ppermute | solution.py:274
  104.2 7.0 %collective-permute-start.8 = (f32[64,256]{1,0:T(8,128)S(1)}, f32[64,256]{1,0:T(8,128)S(1)}, u32[]{:S(2)}, u32[]{:S(2)}) collective-permute-start(f32[64,256]{1,0:T(8,128)S(1)} %fusion.1), channel_id=1, source_target_pairs={{240,0},{241,1},{242,2},{243,3},{244,4},{245,5},{246,6},{247,7},{2... | collective-permute-start | bytes 196616 | tf_op jit(solution)/shard_map/ppermute | solution.py:274
  111.3 4.3 %collective-permute-start.25 = (f32[64,256]{1,0:T(8,128)S(1)}, f32[64,256]{1,0:T(8,128)S(1)}, u32[]{:S(2)}, u32[]{:S(2)}) collective-permute-start(f32[64,256]{1,0:T(8,128)S(1)} %fusion.3.sigma), channel_id=1, source_target_pairs={{16,0},{17,1},{18,2},{19,3},{20,4},{21,5},{22,6},{23,7},{24,8},{25... | collective-permute-start | bytes 196616 | tf_op jit(solution)/shard_map/ppermute | solution.py:274
  115.6 39.6 %collective-permute-start.26 = (f32[2,64,256]{2,1,0:T(8,128)S(1)}, f32[2,64,256]{2,1,0:T(8,128)S(1)}, u32[]{:S(2)}, u32[]{:S(2)}) collective-permute-start(f32[2,64,256]{2,1,0:T(8,128)S(1)} %pad_maximum_fusion), channel_id=1, source_target_pairs={{1,0},{2,1},{3,2},{4,3},{5,4},{6,5},{7,6},{8,7},{9,8},{10,9},{11,1... | collective-permute-start | bytes 393224 | tf_op jit(solution)/shard_map/ppermute | solution.py:274
  115.7 7.6 %collective-permute-start.9 = (f32[2,256]{1,0:T(2,128)S(1)}, f32[2,256]{1,0:T(2,128)S(1)}, u32[]{:S(2)}, u32[]{:S(2)}) collective-permute-start(f32[2,256]{1,0:T(2,128)S(1)} %get-tuple-element.46), channel_id=1, source_target_pairs={{48,0},{49,1},{50,2},{51,3},{52,4},{53,5},{54,6},{55,7},{56,8},{57... | collective-permute-start | bytes 6152 | tf_op jit(solution)/shard_map/ppermute | solution.py:300
  123.3 4.8 %collective-permute-start.10 = (f32[2,256]{1,0:T(2,128)S(1)}, f32[2,256]{1,0:T(2,128)S(1)}, u32[]{:S(2)}, u32[]{:S(2)}) collective-permute-start(f32[2,256]{1,0:T(2,128)S(1)} %add.62), channel_id=1, source_target_pairs={{50,0},{51,1},{48,2},{49,3},{54,4},{55,5},{52,6},{53,7},{58,8},{59... | collective-permute-start | bytes 6152 | tf_op jit(solution)/shard_map/ppermute | solution.py:300
  128.2 3.6 %collective-permute-start.11 = (f32[2,256]{1,0:T(2,128)S(1)}, f32[2,256]{1,0:T(2,128)S(1)}, u32[]{:S(2)}, u32[]{:S(2)}) collective-permute-start(f32[2,256]{1,0:T(2,128)S(1)} %add.63), channel_id=1, source_target_pairs={{16,0},{17,1},{18,2},{19,3},{20,4},{21,5},{22,6},{23,7},{24,8},{25... | collective-permute-start | bytes 6152 | tf_op jit(solution)/shard_map/ppermute | solution.py:300
  131.7 3.6 %collective-permute-start.12 = (f32[2,256]{1,0:T(2,128)S(1)}, f32[2,256]{1,0:T(2,128)S(1)}, u32[]{:S(2)}, u32[]{:S(2)}) collective-permute-start(f32[2,256]{1,0:T(2,128)S(1)} %add.64), channel_id=1, source_target_pairs={{4,0},{5,1},{6,2},{7,3},{0,4},{1,5},{2,6},{3,7},{12,8},{13,9},{14,... | collective-permute-start | bytes 6152 | tf_op jit(solution)/shard_map/ppermute | solution.py:300
  135.3 4.8 %collective-permute-start.13 = (f32[2,256]{1,0:T(2,128)S(1)}, f32[2,256]{1,0:T(2,128)S(1)}, u32[]{:S(2)}, u32[]{:S(2)}) collective-permute-start(f32[2,256]{1,0:T(2,128)S(1)} %add.65), channel_id=1, source_target_pairs={{12,0},{13,1},{14,2},{15,3},{8,4},{9,5},{10,6},{11,7},{4,8},{5,9},... | collective-permute-start | bytes 6152 | tf_op jit(solution)/shard_map/ppermute | solution.py:300
  140.1 3.6 %collective-permute-start.14 = (f32[2,256]{1,0:T(2,128)S(1)}, f32[2,256]{1,0:T(2,128)S(1)}, u32[]{:S(2)}, u32[]{:S(2)}) collective-permute-start(f32[2,256]{1,0:T(2,128)S(1)} %add.66), channel_id=1, source_target_pairs={{64,0},{65,1},{66,2},{67,3},{68,4},{69,5},{70,6},{71,7},{72,8},{73... | collective-permute-start | bytes 6152 | tf_op jit(solution)/shard_map/ppermute | solution.py:300
  143.7 9.6 %collective-permute-start.15 = (f32[2,256]{1,0:T(2,128)S(1)}, f32[2,256]{1,0:T(2,128)S(1)}, u32[]{:S(2)}, u32[]{:S(2)}) collective-permute-start(f32[2,256]{1,0:T(2,128)S(1)} %add.67), channel_id=1, source_target_pairs={{192,0},{193,1},{194,2},{195,3},{196,4},{197,5},{198,6},{199,7},{2... | collective-permute-start | bytes 6152 | tf_op jit(solution)/shard_map/ppermute | solution.py:300
  156.9 10.6 %collective-permute-start.27 = (f32[2,64,256]{2,1,0:T(8,128)S(1)}, f32[2,64,256]{2,1,0:T(8,128)S(1)}, u32[]{:S(2)}, u32[]{:S(2)}) collective-permute-start(f32[2,64,256]{2,1,0:T(8,128)S(1)} %get-tuple-element.53), channel_id=1, source_target_pairs={{15,0},{0,1},{1,2},{2,3},{3,4},{4,5},{5,6},{6,7},{7,8},{8,9},{9,10... | collective-permute-start | bytes 393224 | tf_op jit(solution)/shard_map/ppermute | solution.py:274
  167.5 35.1 %collective-permute-start.28 = (f32[64,256]{1,0:T(8,128)S(1)}, f32[64,256]{1,0:T(8,128)S(1)}, u32[]{:S(2)}, u32[]{:S(2)}) collective-permute-start(f32[64,256]{1,0:T(8,128)S(1)} %fusion), channel_id=1, source_target_pairs={{240,0},{241,1},{242,2},{243,3},{244,4},{245,5},{246,6},{247,7},{2... | collective-permute-start | bytes 196616 | tf_op jit(solution)/shard_map/ppermute | solution.py:274
  167.6 8.7 %collective-permute-start.17 = (f32[1,256]{1,0:T(1,128)S(1)}, f32[1,256]{1,0:T(1,128)S(1)}, u32[]{:S(2)}, u32[]{:S(2)}) collective-permute-start(f32[1,256]{1,0:T(1,128)S(1)} %get-tuple-element.47), channel_id=1, source_target_pairs={{48,0},{49,1},{50,2},{51,3},{52,4},{53,5},{54,6},{55,7},{56,8},{57... | collective-permute-start | bytes 3080 | tf_op jit(solution)/shard_map/ppermute | solution.py:300
  176.3 4.8 %collective-permute-start.18 = (f32[1,256]{1,0:T(1,128)S(1)}, f32[1,256]{1,0:T(1,128)S(1)}, u32[]{:S(2)}, u32[]{:S(2)}) collective-permute-start(f32[1,256]{1,0:T(1,128)S(1)} %add.69), channel_id=1, source_target_pairs={{50,0},{51,1},{48,2},{49,3},{54,4},{55,5},{52,6},{53,7},{58,8},{59... | collective-permute-start | bytes 3080 | tf_op jit(solution)/shard_map/ppermute | solution.py:300
  188.3 4.8 %collective-permute-start.21 = (f32[1,256]{1,0:T(1,128)S(1)}, f32[1,256]{1,0:T(1,128)S(1)}, u32[]{:S(2)}, u32[]{:S(2)}) collective-permute-start(f32[1,256]{1,0:T(1,128)S(1)} %add.72), channel_id=1, source_target_pairs={{12,0},{13,1},{14,2},{15,3},{8,4},{9,5},{10,6},{11,7},{4,8},{5,9},... | collective-permute-start | bytes 3080 | tf_op jit(solution)/shard_map/ppermute | solution.py:300
  196.7 4.8 %collective-permute-start.23 = (f32[1,256]{1,0:T(1,128)S(1)}, f32[1,256]{1,0:T(1,128)S(1)}, u32[]{:S(2)}, u32[]{:S(2)}) collective-permute-start(f32[1,256]{1,0:T(1,128)S(1)} %add.74), channel_id=1, source_target_pairs={{192,0},{193,1},{194,2},{195,3},{196,4},{197,5},{198,6},{199,7},{2... | collective-permute-start | bytes 3080 | tf_op jit(solution)/shard_map/ppermute | solution.py:300
  (15 other events, 71.8 us)

commit v4 on v3

--- a/solution.py
+++ b/solution.py
@@ -19,13 +19,14 @@
     return [pl.BlockSpec(memory_space=pltpu.VMEM)] * count
 
 
-def call(body, outs, flops, moved, smem=0, limit=24):
+def call(body, outs, flops, moved, smem=0, scratch=()):
     return lambda *args: pl.pallas_call(
         body,
         out_shape=outs,
         in_specs=[pl.BlockSpec(memory_space=pltpu.SMEM)] * smem + vmem(len(args) - smem),
         out_specs=jax.tree.map(lambda _: pl.BlockSpec(memory_space=pltpu.VMEM), outs),
-        compiler_params=pltpu.CompilerParams(vmem_limit_bytes=limit * 2**20),
+        scratch_shapes=scratch,
+        compiler_params=pltpu.CompilerParams(vmem_limit_bytes=24 * 2**20),
         cost_estimate=pl.CostEstimate(flops=flops, bytes_accessed=moved, transcendentals=0),
     )(*args)
 
@@ -112,85 +113,98 @@
         )
 
 
-def self_body(states, rho, metric, own, proj, c_aa):
+def choose(core, low, high):
+    return jnp.where(core[0, 0] == 1, high, low)
+
+
+def self_body(states, rho, metric, own, proj, back, c_aa):
     rows = stack(rho, states)
     proj[...] = dot(rows, metric[...]).astype(BF)
+    back[...] = dot_nt(rows, metric[...]).astype(BF)
     c_aa[...] = couple(proj[...], rows, own[...])
 
 
-def first_body(states, rho_a, rho_u, metric, proj_a, own, msg_u, proj_u, c):
-    mols = rho_a.shape[0]
+def first_body(states, core, rho, proj, back, own_u, own_c, msg_u, msg_c, c):
+    mols = rho.shape[0]
     field = msg_u.shape[1] - 4 * mols
-    rows_a, rows_u = stack(rho_a, states), stack(rho_u, states)
-    c[0] = couple(proj_a[...], rows_u, own[...])
-    proj_u[...] = dot(rows_u, metric[...]).astype(BF)
-    c[1] = couple(proj_u[...], rows_a, twice(msg_u[:, field : field + mols]))
-
-
-def next_body(
-    states, rho_a, rho_u, rho_r, metric, proj_a, proj_u, own, msg_u, msg_r, c_aa, c_u, y_a, c, sig
-):
+    part = slice(field, field + mols)
+    rows = stack(rho, states)
+    c[0] = couple(proj[...], rows, choose(core, own_u[...], own_c[...]))
+    c[1] = couple(rows, back[...], twice(choose(core, msg_u[:, part], msg_c[:, part])))
+
+
+def right_body(states, rho_a, rho_r, metric, proj_a, own, msg_r, proj_r, back_r, c):
     mols = rho_a.shape[0]
     field = msg_r.shape[1] - 4 * mols
-    rows_r = stack(rho_r, states)
-    c[0] = couple(proj_a[...], rows_r, own[...])
-    c[1] = couple(proj_u[...], rows_r, twice(msg_u[:, field + mols : field + 2 * mols]))
-    proj_r = dot(rows_r, metric[...]).astype(BF)
-    c[2] = couple(proj_r, stack(rho_a, states), twice(msg_r[:, field : field + mols]))
-    c[3] = couple(
-        proj_r, stack(rho_u, states), twice(msg_r[:, field + mols : field + 2 * mols])
-    )
+    rows = stack(rho_r, states)
+    proj_r[...] = dot(rows, metric[...]).astype(BF)
+    back_r[...] = dot_nt(rows, metric[...]).astype(BF)
+    c[0] = couple(proj_a[...], rows, own[...])
+    c[1] = couple(proj_r[...], stack(rho_a, states), twice(msg_r[:, field : field + mols]))
+
+
+def fields(states, core, y_a, msg_r, msg_u, msg_c):
+    field = y_a.shape[1]
     f_a = stack(y_a, states)
-    f_r = stack(msg_r[:, :field], states).astype(BF)
-    f_u = stack(msg_u[:, :field], states).astype(BF)
-    sig[0] = dot(c_aa[...], f_a) + (dot(c_u[0], f_u) + dot(c[0], f_r))
-    sig[1] = dot(c[2], f_a) + dot(c[3], f_u)
-    sig[2] = dot(c_u[1], f_a) + dot(c[1], f_r)
+    f_r, f_u, f_c = [stack(m[:, :field], states).astype(BF) for m in (msg_r, msg_u, msg_c)]
+    return f_a, f_r, f_u, choose(core, f_u, f_c), choose(core, f_c, f_u)
+
+
+def sums_of(core, c_aa, c_f, c_r, c_s, f_a, f_r, f_u, f_first, f_last):
+    row_a = (dot(c_aa[...], f_a) + dot(c_f[0], f_first)) + (dot(c_r[0], f_r) + dot(c_s[0], f_last))
+    row_r = dot(c_r[1], f_a) + dot(c_s[2], f_u)
+    first, last = dot(c_f[1], f_a), dot(c_s[1], f_a)
+    row_u = choose(core, first, last) + dot(c_s[3], f_r)
+    return row_a, row_r, row_u, choose(core, last, first)
 
 
 def corner_body(
     states,
-    second,
-    rho_a,
+    core,
+    rho_f,
     near,
-    far,
-    metric,
+    shifted,
     proj_a,
-    own,
+    back_a,
+    proj_r,
+    back_r,
+    own_u,
+    own_c,
     msg_r,
     msg_u,
     msg_c,
     y_a,
     e_a,
-    sig,
+    c_aa,
+    c_f,
+    c_r,
     c,
     to_a,
     to_r,
     to_uc,
     sums,
+    rows,
 ):
-    mols = rho_a.shape[0]
-    field = msg_r.shape[1] - 4 * mols
-    width = near.shape[1] // states
-    pick = second[0, 0] == 1
-    rows_c = jnp.concatenate(
-        [
-            jnp.where(pick, far[:, a * width : (a + 1) * width], near[:, a * width : (a + 1) * width])
-            for a in range(states)
-        ],
-        axis=0,
-    )
-    c[0] = couple(proj_a[...], rows_c, own[...])
-    proj_c = dot(rows_c, metric[...]).astype(BF)
-    c[1] = couple(proj_c, stack(rho_a, states), twice(msg_c[:, field : field + mols]))
-    f_a = stack(y_a, states)
-    f_c = stack(msg_c[:, :field], states).astype(BF)
+    mols, field = y_a.shape
+    width = rho_f.shape[1] // states
+    part = slice(field, field + mols)
+    half = slice(field + mols, field + 2 * mols)
+    for a in range(states):
+        lanes = slice(a * width, (a + 1) * width)
+        place = slice(a * mols, (a + 1) * mols)
+        rows[0, place] = rho_f[:, lanes]
+        rows[1, place] = choose(core, near[:, lanes], shifted[:, lanes])
+    upper = rows.at[core[0, 0]]
+    last = rows[1]
+    c[0] = couple(proj_a[...], last, choose(core, own_c[...], own_u[...]))
+    c[1] = couple(last, back_a[...], twice(choose(core, msg_c[:, part], msg_u[:, part])))
+    c[2] = couple(proj_r[...], upper[...], twice(msg_r[:, half]))
+    c[3] = couple(upper[...], back_r[...], twice(msg_u[:, half]))
+    f = fields(states, core, y_a, msg_r, msg_u, msg_c)
+    row_a, row_r, row_u, row_c = sums_of(core, c_aa, c_f, c_r, c, *f)
     own_y = y_a[...].astype(F32)
-    part_a = unstack(sig[0] + dot(c[0], f_c), states)
-    part_a = part_a + spread(e_a[...], field // states) * own_y
-    part_r = unstack(sig[1], states)
-    part_u = unstack(sig[2], states)
-    part_c = unstack(dot(c[1], f_a), states)
+    part_a = unstack(row_a, states) + spread(e_a[...], field // states) * own_y
+    part_r, part_u, part_c = [unstack(row, states) for row in (row_r, row_u, row_c)]
     to_a[...], to_r[...], to_uc[0], to_uc[1] = part_a, part_r, part_u, part_c
     total = part_a * own_y + part_r * msg_r[:, :field]
     total = total + (part_u * msg_u[:, :field] + part_c * msg_c[:, :field])
@@ -222,7 +236,22 @@
 
 
 def second_body(
-    states, theta, resid, sig_r, sig_uc, msg_r, msg_u, msg_c, c_aa, c_r, c_u, c_c, to_a, to_r, to_uc
+    states,
+    core,
+    theta,
+    resid,
+    sig_r,
+    sig_uc,
+    msg_r,
+    msg_u,
+    msg_c,
+    c_aa,
+    c_f,
+    c_r,
+    c_s,
+    to_a,
+    to_r,
+    to_uc,
 ):
     mols, field = resid.shape
     width = field // states
@@ -236,11 +265,10 @@
     f_r = other(sig_r[...], msg_r)
     f_u = other(sig_uc[0], msg_u)
     f_c = other(sig_uc[1], msg_c)
-    row_a = (dot(c_aa[...], f_a) + dot(c_u[0], f_u)) + (dot(c_r[0], f_r) + dot(c_c[0], f_c))
-    to_a[...] = unstack(row_a, states)
-    to_r[...] = unstack(dot(c_r[2], f_a) + dot(c_r[3], f_u), states)
-    to_uc[0] = unstack(dot(c_u[1], f_a) + dot(c_r[1], f_r), states)
-    to_uc[1] = unstack(dot(c_c[1], f_a), states)
+    rows = sums_of(
+        core, c_aa, c_f, c_r, c_s, f_a, f_r, f_u, choose(core, f_u, f_c), choose(core, f_c, f_u)
+    )
+    to_a[...], to_r[...], to_uc[0], to_uc[1] = [unstack(row, states) for row in rows]
 
 
 def last_body(states, count, part, rest, resid, to_a, below, left, e_a, corr, sigma):
@@ -303,7 +331,9 @@
             value = value + other
 
     rho_a, y_a, e_a = densities[0, 0], trials[0, 0], energies[0, 0]
-    rho_u = take(rho_a, 0, 1)
+    core = (lax.axis_index("gy") % 2).astype(jnp.int32).reshape(1, 1)
+    table = [(spot(x + y % 2, y + 1), spot(x, y)) for x in range(nx) for y in range(ny)]
+    rho_f = lax.ppermute(rho_a, AXES, table)
 
     pair = shape(mols, 2 * mols)
     note = shape(mols, field + 4 * mols)
@@ -319,38 +349,53 @@
 
     rho_r = take(rho_a, 1, 0)
     near = take(rho_r, 0, 1, lambda x, y: y % 2 == 0)
-    far = take(rho_u, 1, 0, lambda x, y: y % 2 == 1)
+    shifted = take(rho_f, -1, 0, lambda x, y: y % 2 == 1)
 
     block = 2 * width * width * aux
     proj = 2 * width * aux * aux
     size = width * aux * 2
-    proj_a, c_aa = call(
-        functools.partial(self_body, states),
-        (shape(width, aux, dtype=BF), shape(width, width, dtype=BF)),
-        proj + block,
-        4 * size,
+    wide, square = shape(width, aux, dtype=BF), shape(width, width, dtype=BF)
+    squares_of = lambda count: shape(count, width, width, dtype=BF)
+    proj_a, back_a, c_aa = call(
+        functools.partial(self_body, states), (wide, wide, square), 2 * proj + block, 5 * size
     )(rho_a, metric, own_a)
-    proj_u, c_u = call(
-        functools.partial(first_body, states),
-        (shape(width, aux, dtype=BF), shape(2, width, width, dtype=BF)),
-        proj + 2 * block,
-        6 * size,
-    )(rho_a, rho_u, metric, proj_a, own_u, msg_u)
-    c_r, sig = call(
-        functools.partial(next_body, states),
-        (shape(4, width, width, dtype=BF), shape(3, width, field // states)),
-        proj + 4 * block,
+    c_f = call(functools.partial(first_body, states), squares_of(2), 2 * block, 4 * size, 1)(
+        core, rho_f, proj_a, back_a, own_u, own_c, msg_u, msg_c
+    )
+    proj_r, back_r, c_r = call(
+        functools.partial(right_body, states),
+        (wide, wide, squares_of(2)),
+        2 * proj + 2 * block,
+        8 * size,
+    )(rho_a, rho_r, metric, proj_a, own_r, msg_r)
+    one, two = shape(mols, field), shape(2, mols, field)
+    c_s, to_a, to_r, to_uc, sums = call(
+        functools.partial(corner_body, states),
+        (squares_of(4), one, one, two, shape(2, field)),
+        4 * block,
         9 * size,
-    )(rho_a, rho_u, rho_r, metric, proj_a, proj_u, own_r, msg_u, msg_r, c_aa, c_u, y_a)
-    one, two = shape(mols, field), shape(2, mols, field)
-    second = (lax.axis_index("gy") % 2).astype(jnp.int32).reshape(1, 1)
-    c_c, to_a, to_r, to_uc, sums = call(
-        functools.partial(corner_body, states),
-        (shape(2, width, width, dtype=BF), one, one, two, shape(2, field)),
-        proj + 2 * block,
-        6 * size,
-        smem=1,
-    )(second, rho_a, near, far, metric, proj_a, own_c, msg_r, msg_u, msg_c, y_a, e_a, sig)
+        1,
+        [pltpu.VMEM((2, width, aux), BF)],
+    )(
+        core,
+        rho_f,
+        near,
+        shifted,
+        proj_a,
+        back_a,
+        proj_r,
+        back_r,
+        own_u,
+        own_c,
+        msg_r,
+        msg_u,
+        msg_c,
+        y_a,
+        e_a,
+        c_aa,
+        c_f,
+        c_r,
+    )
 
     def home(to_r, to_uc):
         below = take(to_uc, 0, -1)
@@ -373,7 +418,8 @@
         (one, one, two),
         9 * 2 * width * field * mols,
         9 * width * width * 2,
-    )(theta, resid, sig_r, sig_uc, msg_r, msg_u, msg_c, c_aa, c_r, c_u, c_c)
+        1,
+    )(core, theta, resid, sig_r, sig_uc, msg_r, msg_u, msg_c, c_aa, c_f, c_r, c_s)
     squares = butterfly(squares)
     below, left = home(to_r, to_uc)
     corr, sigma2 = call(

time: 206 us -> 210 us (1.019)
  local copies, waits for them, and re-layouts: 6.6 us -> 11.3 us
  starting transfers between devices: 55.6 us -> 52.3 us
  waiting for transfers between devices: 122 us -> 125 us
    unnamed x21 -> x45, local copies, waits for them, and re-layouts: 6.6 us -> 11.3 us
    ppermute x13 -> x12, starting transfers between devices: 33.4 us -> 29.7 us  [take(): return lax.ppermute(value, AXES, table)]
    ppermute x0 -> x1, starting transfers between devices: none -> 3.59 us  [shards(): rho_f = lax.ppermute(rho_a, AXES, table)]
    ppermute x16, starting transfers between devices: 22.2 us -> 19 us  [butterfly(): other = lax.ppermute(value, AXES, table)]
    ppermute x16, waiting for transfers between devices: 51.6 us -> 54.1 us  [butterfly(): other = lax.ppermute(value, AXES, table)]
    ppermute x13 -> x12, waiting for transfers between devices: 70.4 us -> 70.5 us  [take(): return lax.ppermute(value, AXES, table)]
  transfers between devices with their start and end apart: 29 -> 29, of which waited for: 22 -> 22; matrix products, arithmetic and copies ran while one was open for 0% -> 0% of each run, Pallas kernels for 6% -> 5%
where the time goes in v4:
time: 210 us; the launch traced here: 208 us
  waiting for transfers between devices  125 us (60%)
  starting transfers between devices  52.3 us (25%)
  Pallas kernels  19.3 us (9%)
  local copies, waits for them, and re-layouts  11.3 us (5%)
    ppermute x12, waiting for transfers between devices, take(): return lax.ppermute(value, AXES, table)  70.5 us
    ppermute x16, waiting for transfers between devices, butterfly(): other = lax.ppermute(value, AXES, table)  54.1 us
    ppermute x12, starting transfers between devices, take(): return lax.ppermute(value, AXES, table)  29.7 us
    pallas_call x8, Pallas kernels, call(): pl.pallas_call(body, out_shape=outs, in_specs=[pl.BlockSpec(memory_space=...  19.3 us
    ppermute x16, starting transfers between devices, butterfly(): other = lax.ppermute(value, AXES, table)  19 us
    unnamed x45, local copies, waits for them, and re-layouts  11.3 us
  transfers between devices with their start and end apart: 29, of which 22 were waited for; matrix products, arithmetic and copies ran while one was open for 0% of the time, Pallas kernels for 5%

profile of v4, /device:TPU:24, one launch (start us, length us, event | category | flops | bytes accessed | tf_op | source)
XLA Modules:
  0.0 208.4 jit_solution(16475699521071284207)
XLA Ops:
  0.6 4.9 %collective-permute-start.1 = (bf16[64,8192]{1,0:T(8,128)(2,1)}, bf16[64,8192]{1,0:T(8,128)(2,1)}, u32[]{:S(2)}, u32[]{:S(2)}) collective-permute-start(bf16[64,8192]{1,0:T(8,128)(2,1)} %bitcast.37), channel_id=1, source_target_pairs={{16,0},{17,1},{18,2},{19,3},{20,4},{21,5},{22,6},{23,7},{24,8},{25... | collective-permute-start | bytes 3145736 | tf_op jit(solution)/shard_map/ppermute | solution.py:302
  5.5 3.6 %collective-permute-start = (bf16[64,8192]{1,0:T(8,128)(2,1)}, bf16[64,8192]{1,0:T(8,128)(2,1)S(1)}, u32[]{:S(2)}, u32[]{:S(2)}) collective-permute-start(bf16[64,8192]{1,0:T(8,128)(2,1)} %bitcast.38), channel_id=1, source_target_pairs={{1,0},{18,1},{3,2},{20,3},{5,4},{22,5},{7,6},{24,7},{9,8},{26,9},{... | collective-permute-start | bytes 3145736 | tf_op jit(solution)/shard_map/ppermute | solution.py:336
  9.1 41.6 %collective-permute-done.1.rho_r = bf16[64,8192]{1,0:T(8,128)(2,1)} collective-permute-done((bf16[64,8192]{1,0:T(8,128)(2,1)}, bf16[64,8192]{1,0:T(8,128)(2,1)}, u32[]{:S(2)}, u32[]{:S(2)}) %collective-permute-start.1) | collective-permute-done | bytes 1048608 | tf_op jit(solution)/shard_map/ppermute | solution.py:302
  61.1 5.2 %collective-permute-start.4 = (f32[64,512]{1,0:T(8,128)}, f32[64,512]{1,0:T(8,128)S(1)}, u32[]{:S(2)}, u32[]{:S(2)}) collective-permute-start(f32[64,512]{1,0:T(8,128)} %get-tuple-element.35), channel_id=1, source_target_pairs={{16,0},{17,1},{18,2},{19,3},{20,4},{21,5},{22,6},{23,7},{24,8},{25... | collective-permute-start | bytes 393224 | tf_op jit(solution)/shard_map/ppermute | solution.py:302
  66.2 8.5 %collective-permute-start.5 = (f32[64,512]{1,0:T(8,128)}, f32[64,512]{1,0:T(8,128)S(1)}, u32[]{:S(2)}, u32[]{:S(2)}) collective-permute-start(f32[64,512]{1,0:T(8,128)} %get-tuple-element.40), channel_id=1, source_target_pairs={{1,0},{2,1},{3,2},{4,3},{5,4},{6,5},{7,6},{8,7},{9,8},{10,9},{11,1... | collective-permute-start | bytes 393224 | tf_op jit(solution)/shard_map/ppermute | solution.py:302
  84.7 4.7 %shard_map.104 = (bf16[512,1024]{1,0:T(8,128)(2,1)S(1)}, bf16[512,1024]{1,0:T(8,128)(2,1)S(1)}, bf16[2,512,512]{2,1,0:T(8,128)(2,1)S(1)}) custom-call(bf16[64,8192]{1,0:T(8,128)(2,1)S(1)} %bitcast.40, bf16[64,8192]{1,0:T(8,128)(2,1)} %collective-permute-done.1.rho_r, bf16[1024,1024]{1,0:T(8,128)(2,1)S(1)} %copy-done.14, ...), custom_call_target="tpu_custom_call" | custom-call | flops 3221225472 | bytes 8388608 | tf_op jit(solution)/shard_map/pallas_call | solution.py:23
  89.5 5.3 %shard_map.106 = (bf16[4,512,512]{2,1,0:T(8,128)(2,1)S(1)}, f32[64,256]{1,0:T(8,128)S(1)}, f32[64,256]{1,0:T(8,128)S(1)}, f32[2,64,256]{2,1,0:T(8,128)S(1)}, f32[2,256]{1,0:T(2,128)S(1)}) custom-call(s32[1,1]{1,0:T(1,128)} %bitcast.core, bf16[64,8192]{1,0:T(8,128)(2,1)S(1)} %collective-permute-done.rho.rho_f, bf16[64,8192]{1,0:T(8,128)(2,1)} %collective-permute-done.2.near, ...), custom_call_target="tpu_custom_call" | custom-call | flops 2147483648 | bytes 9437184 | tf_op jit(solution)/shard_map/pallas_call | solution.py:23
  94.9 4.8 %collective-permute-start.7 = (f32[2,64,256]{2,1,0:T(8,128)S(1)}, f32[2,64,256]{2,1,0:T(8,128)S(1)}, u32[]{:S(2)}, u32[]{:S(2)}) collective-permute-start(f32[2,64,256]{2,1,0:T(8,128)S(1)} %get-tuple-element.45), channel_id=1, source_target_pairs={{15,0},{0,1},{1,2},{2,3},{3,4},{4,5},{5,6},{6,7},{7,8},{8,9},{9,10... | collective-permute-start | bytes 393224 | tf_op jit(solution)/shard_map/ppermute | solution.py:302
  99.6 8.1 %collective-permute-done.7 = f32[2,64,256]{2,1,0:T(8,128)S(1)} collective-permute-done((f32[2,64,256]{2,1,0:T(8,128)S(1)}, f32[2,64,256]{2,1,0:T(8,128)S(1)}, u32[]{:S(2)}, u32[]{:S(2)}) %collective-permute-start.7) | collective-permute-done | bytes 131104 | tf_op jit(solution)/shard_map/ppermute | solution.py:302
  109.2 6.5 %collective-permute-done.8 = f32[64,256]{1,0:T(8,128)S(1)} collective-permute-done((f32[64,256]{1,0:T(8,128)S(1)}, f32[64,256]{1,0:T(8,128)S(1)}, u32[]{:S(2)}, u32[]{:S(2)}) %collective-permute-start.8) | collective-permute-done | bytes 65568 | tf_op jit(solution)/shard_map/ppermute | solution.py:302
  120.1 12.2 %collective-permute-start.9 = (f32[2,256]{1,0:T(2,128)S(1)}, f32[2,256]{1,0:T(2,128)S(1)}, u32[]{:S(2)}, u32[]{:S(2)}) collective-permute-start(f32[2,256]{1,0:T(2,128)S(1)} %get-tuple-element.47), channel_id=1, source_target_pairs={{48,0},{49,1},{50,2},{51,3},{52,4},{53,5},{54,6},{55,7},{56,8},{57... | collective-permute-start | bytes 6152 | tf_op jit(solution)/shard_map/ppermute | solution.py:328
  135.2 4.8 %collective-permute-done.10 = f32[2,256]{1,0:T(2,128)S(1)} collective-permute-done((f32[2,256]{1,0:T(2,128)S(1)}, f32[2,256]{1,0:T(2,128)S(1)}, u32[]{:S(2)}, u32[]{:S(2)}) %collective-permute-start.10) | collective-permute-done | bytes 2080 | tf_op jit(solution)/shard_map/ppermute | solution.py:328
  140.0 3.6 %collective-permute-done.11 = f32[2,256]{1,0:T(2,128)S(1)} collective-permute-done((f32[2,256]{1,0:T(2,128)S(1)}, f32[2,256]{1,0:T(2,128)S(1)}, u32[]{:S(2)}, u32[]{:S(2)}) %collective-permute-start.11) | collective-permute-done | bytes 2080 | tf_op jit(solution)/shard_map/ppermute | solution.py:328
  143.6 3.6 %collective-permute-done.12 = f32[2,256]{1,0:T(2,128)S(1)} collective-permute-done((f32[2,256]{1,0:T(2,128)S(1)}, f32[2,256]{1,0:T(2,128)S(1)}, u32[]{:S(2)}, u32[]{:S(2)}) %collective-permute-start.12) | collective-permute-done | bytes 2080 | tf_op jit(solution)/shard_map/ppermute | solution.py:328
  147.5 4.5 %collective-permute-done.13 = f32[2,256]{1,0:T(2,128)S(1)} collective-permute-done((f32[2,256]{1,0:T(2,128)S(1)}, f32[2,256]{1,0:T(2,128)S(1)}, u32[]{:S(2)}, u32[]{:S(2)}) %collective-permute-start.13) | collective-permute-done | bytes 2080 | tf_op jit(solution)/shard_map/ppermute | solution.py:328
  152.0 3.6 %collective-permute-done.14 = f32[2,256]{1,0:T(2,128)S(1)} collective-permute-done((f32[2,256]{1,0:T(2,128)S(1)}, f32[2,256]{1,0:T(2,128)S(1)}, u32[]{:S(2)}, u32[]{:S(2)}) %collective-permute-start.14) | collective-permute-done | bytes 2080 | tf_op jit(solution)/shard_map/ppermute | solution.py:328
  156.5 3.9 %collective-permute-done.15 = f32[2,256]{1,0:T(2,128)S(1)} collective-permute-done((f32[2,256]{1,0:T(2,128)S(1)}, f32[2,256]{1,0:T(2,128)S(1)}, u32[]{:S(2)}, u32[]{:S(2)}) %collective-permute-start.15) | collective-permute-done | bytes 2080 | tf_op jit(solution)/shard_map/ppermute | solution.py:328
  164.3 11.4 %collective-permute-done.27.below = f32[2,64,256]{2,1,0:T(8,128)S(1)} collective-permute-done((f32[2,64,256]{2,1,0:T(8,128)S(1)}, f32[2,64,256]{2,1,0:T(8,128)S(1)}, u32[]{:S(2)}, u32[]{:S(2)}) %collective-permute-start.27) | collective-permute-done | bytes 131104 | tf_op jit(solution)/shard_map/ppermute | solution.py:302
  175.8 3.3 %collective-permute-start.17 = (f32[1,256]{1,0:T(1,128)S(1)}, f32[1,256]{1,0:T(1,128)S(1)}, u32[]{:S(2)}, u32[]{:S(2)}) collective-permute-start(f32[1,256]{1,0:T(1,128)S(1)} %get-tuple-element.48), channel_id=1, source_target_pairs={{48,0},{49,1},{50,2},{51,3},{52,4},{53,5},{54,6},{55,7},{56,8},{57... | collective-permute-start | bytes 3080 | tf_op jit(solution)/shard_map/ppermute | solution.py:328
  181.3 4.8 %collective-permute-done.18 = f32[1,256]{1,0:T(1,128)S(1)} collective-permute-done((f32[1,256]{1,0:T(1,128)S(1)}, f32[1,256]{1,0:T(1,128)S(1)}, u32[]{:S(2)}, u32[]{:S(2)}) %collective-permute-start.18) | collective-permute-done | bytes 1056 | tf_op jit(solution)/shard_map/ppermute | solution.py:328
  186.5 3.3 %collective-permute-done.19 = f32[1,256]{1,0:T(1,128)S(1)} collective-permute-done((f32[1,256]{1,0:T(1,128)S(1)}, f32[1,256]{1,0:T(1,128)S(1)}, u32[]{:S(2)}, u32[]{:S(2)}) %collective-permute-start.19) | collective-permute-done | bytes 1056 | tf_op jit(solution)/shard_map/ppermute | solution.py:328
  189.7 3.6 %collective-permute-done.20 = f32[1,256]{1,0:T(1,128)S(1)} collective-permute-done((f32[1,256]{1,0:T(1,128)S(1)}, f32[1,256]{1,0:T(1,128)S(1)}, u32[]{:S(2)}, u32[]{:S(2)}) %collective-permute-start.20) | collective-permute-done | bytes 1056 | tf_op jit(solution)/shard_map/ppermute | solution.py:328
  193.3 4.8 %collective-permute-done.21 = f32[1,256]{1,0:T(1,128)S(1)} collective-permute-done((f32[1,256]{1,0:T(1,128)S(1)}, f32[1,256]{1,0:T(1,128)S(1)}, u32[]{:S(2)}, u32[]{:S(2)}) %collective-permute-start.21) | collective-permute-done | bytes 1056 | tf_op jit(solution)/shard_map/ppermute | solution.py:328
  201.7 4.8 %collective-permute-done.23 = f32[1,256]{1,0:T(1,128)S(1)} collective-permute-done((f32[1,256]{1,0:T(1,128)S(1)}, f32[1,256]{1,0:T(1,128)S(1)}, u32[]{:S(2)}, u32[]{:S(2)}) %collective-permute-start.23) | collective-permute-done | bytes 1056 | tf_op jit(solution)/shard_map/ppermute | solution.py:328
  (105 shorter events, 42.5 us)
Async XLA Ops:
  0.6 50.1 %collective-permute-start.1 = (bf16[64,8192]{1,0:T(8,128)(2,1)}, bf16[64,8192]{1,0:T(8,128)(2,1)}, u32[]{:S(2)}, u32[]{:S(2)}) collective-permute-start(bf16[64,8192]{1,0:T(8,128)(2,1)} %bitcast.37), channel_id=1, source_target_pairs={{16,0},{17,1},{18,2},{19,3},{20,4},{21,5},{22,6},{23,7},{24,8},{25... | collective-permute-start | bytes 3145736 | tf_op jit(solution)/shard_map/ppermute | solution.py:302
  5.5 46.5 %collective-permute-start = (bf16[64,8192]{1,0:T(8,128)(2,1)}, bf16[64,8192]{1,0:T(8,128)(2,1)S(1)}, u32[]{:S(2)}, u32[]{:S(2)}) collective-permute-start(bf16[64,8192]{1,0:T(8,128)(2,1)} %bitcast.38), channel_id=1, source_target_pairs={{1,0},{18,1},{3,2},{20,3},{5,4},{22,5},{7,6},{24,7},{9,8},{26,9},{... | collective-permute-start | bytes 3145736 | tf_op jit(solution)/shard_map/ppermute | solution.py:336
  50.7 38.7 %collective-permute-start.2 = (bf16[64,8192]{1,0:T(8,128)(2,1)}, bf16[64,8192]{1,0:T(8,128)(2,1)}, u32[]{:S(2)}, u32[]{:S(2)}) collective-permute-start(bf16[64,8192]{1,0:T(8,128)(2,1)} %collective-permute-done.1.rho_r), channel_id=1, source_target_pairs={{1,0},{3,2},{5,4},{7,6},{9,8},{11,10},{13,12},{15,14},{17,16},{19,... | collective-permute-start | bytes 3145736 | tf_op jit(solution)/shard_map/ppermute | solution.py:302
  52.0 37.4 %collective-permute-start.3 = (bf16[64,8192]{1,0:T(8,128)(2,1)S(1)}, bf16[64,8192]{1,0:T(8,128)(2,1)}, u32[]{:S(2)}, u32[]{:S(2)}) collective-permute-start(bf16[64,8192]{1,0:T(8,128)(2,1)S(1)} %collective-permute-done.rho.rho_f), channel_id=1, source_target_pairs={{241,1},{243,3},{245,5},{247,7},{249,9},{251,11},{253,13},{255,15}... | collective-permute-start | bytes 3145736 | tf_op jit(solution)/shard_map/ppermute | solution.py:302
  61.1 23.1 %collective-permute-start.4 = (f32[64,512]{1,0:T(8,128)}, f32[64,512]{1,0:T(8,128)S(1)}, u32[]{:S(2)}, u32[]{:S(2)}) collective-permute-start(f32[64,512]{1,0:T(8,128)} %get-tuple-element.35), channel_id=1, source_target_pairs={{16,0},{17,1},{18,2},{19,3},{20,4},{21,5},{22,6},{23,7},{24,8},{25... | collective-permute-start | bytes 393224 | tf_op jit(solution)/shard_map/ppermute | solution.py:302
  66.2 15.0 %collective-permute-start.5 = (f32[64,512]{1,0:T(8,128)}, f32[64,512]{1,0:T(8,128)S(1)}, u32[]{:S(2)}, u32[]{:S(2)}) collective-permute-start(f32[64,512]{1,0:T(8,128)} %get-tuple-element.40), channel_id=1, source_target_pairs={{1,0},{2,1},{3,2},{4,3},{5,4},{6,5},{7,6},{8,7},{9,8},{10,9},{11,1... | collective-permute-start | bytes 393224 | tf_op jit(solution)/shard_map/ppermute | solution.py:302
  74.7 6.6 %collective-permute-start.6 = (f32[64,512]{1,0:T(8,128)}, f32[64,512]{1,0:T(8,128)S(1)}, u32[]{:S(2)}, u32[]{:S(2)}) collective-permute-start(f32[64,512]{1,0:T(8,128)} %get-tuple-element.41), channel_id=1, source_target_pairs={{17,0},{18,1},{19,2},{20,3},{21,4},{22,5},{23,6},{24,7},{25,8},{26... | collective-permute-start | bytes 393224 | tf_op jit(solution)/shard_map/ppermute | solution.py:302
  94.9 12.9 %collective-permute-start.7 = (f32[2,64,256]{2,1,0:T(8,128)S(1)}, f32[2,64,256]{2,1,0:T(8,128)S(1)}, u32[]{:S(2)}, u32[]{:S(2)}) collective-permute-start(f32[2,64,256]{2,1,0:T(8,128)S(1)} %get-tuple-element.45), channel_id=1, source_target_pairs={{15,0},{0,1},{1,2},{2,3},{3,4},{4,5},{5,6},{6,7},{7,8},{8,9},{9,10... | collective-permute-start | bytes 393224 | tf_op jit(solution)/shard_map/ppermute | solution.py:302
  107.8 7.9 %collective-permute-start.8 = (f32[64,256]{1,0:T(8,128)S(1)}, f32[64,256]{1,0:T(8,128)S(1)}, u32[]{:S(2)}, u32[]{:S(2)}) collective-permute-start(f32[64,256]{1,0:T(8,128)S(1)} %fusion.1), channel_id=1, source_target_pairs={{240,0},{241,1},{242,2},{243,3},{244,4},{245,5},{246,6},{247,7},{2... | collective-permute-start | bytes 196616 | tf_op jit(solution)/shard_map/ppermute | solution.py:302
  115.7 4.3 %collective-permute-start.25 = (f32[64,256]{1,0:T(8,128)S(1)}, f32[64,256]{1,0:T(8,128)S(1)}, u32[]{:S(2)}, u32[]{:S(2)}) collective-permute-start(f32[64,256]{1,0:T(8,128)S(1)} %fusion.3.sigma), channel_id=1, source_target_pairs={{16,0},{17,1},{18,2},{19,3},{20,4},{21,5},{22,6},{23,7},{24,8},{25... | collective-permute-start | bytes 196616 | tf_op jit(solution)/shard_map/ppermute | solution.py:302
  120.0 42.2 %collective-permute-start.26 = (f32[2,64,256]{2,1,0:T(8,128)S(1)}, f32[2,64,256]{2,1,0:T(8,128)S(1)}, u32[]{:S(2)}, u32[]{:S(2)}) collective-permute-start(f32[2,64,256]{2,1,0:T(8,128)S(1)} %pad_maximum_fusion), channel_id=1, source_target_pairs={{1,0},{2,1},{3,2},{4,3},{5,4},{6,5},{7,6},{8,7},{9,8},{10,9},{11,1... | collective-permute-start | bytes 393224 | tf_op jit(solution)/shard_map/ppermute | solution.py:302
  120.1 15.1 %collective-permute-start.9 = (f32[2,256]{1,0:T(2,128)S(1)}, f32[2,256]{1,0:T(2,128)S(1)}, u32[]{:S(2)}, u32[]{:S(2)}) collective-permute-start(f32[2,256]{1,0:T(2,128)S(1)} %get-tuple-element.47), channel_id=1, source_target_pairs={{48,0},{49,1},{50,2},{51,3},{52,4},{53,5},{54,6},{55,7},{56,8},{57... | collective-permute-start | bytes 6152 | tf_op jit(solution)/shard_map/ppermute | solution.py:328
  135.2 4.8 %collective-permute-start.10 = (f32[2,256]{1,0:T(2,128)S(1)}, f32[2,256]{1,0:T(2,128)S(1)}, u32[]{:S(2)}, u32[]{:S(2)}) collective-permute-start(f32[2,256]{1,0:T(2,128)S(1)} %add.62), channel_id=1, source_target_pairs={{50,0},{51,1},{48,2},{49,3},{54,4},{55,5},{52,6},{53,7},{58,8},{59... | collective-permute-start | bytes 6152 | tf_op jit(solution)/shard_map/ppermute | solution.py:328
  140.0 3.6 %collective-permute-start.11 = (f32[2,256]{1,0:T(2,128)S(1)}, f32[2,256]{1,0:T(2,128)S(1)}, u32[]{:S(2)}, u32[]{:S(2)}) collective-permute-start(f32[2,256]{1,0:T(2,128)S(1)} %add.63), channel_id=1, source_target_pairs={{16,0},{17,1},{18,2},{19,3},{20,4},{21,5},{22,6},{23,7},{24,8},{25... | collective-permute-start | bytes 6152 | tf_op jit(solution)/shard_map/ppermute | solution.py:328
  143.6 3.6 %collective-permute-start.12 = (f32[2,256]{1,0:T(2,128)S(1)}, f32[2,256]{1,0:T(2,128)S(1)}, u32[]{:S(2)}, u32[]{:S(2)}) collective-permute-start(f32[2,256]{1,0:T(2,128)S(1)} %add.64), channel_id=1, source_target_pairs={{4,0},{5,1},{6,2},{7,3},{0,4},{1,5},{2,6},{3,7},{12,8},{13,9},{14,... | collective-permute-start | bytes 6152 | tf_op jit(solution)/shard_map/ppermute | solution.py:328
  147.2 4.8 %collective-permute-start.13 = (f32[2,256]{1,0:T(2,128)S(1)}, f32[2,256]{1,0:T(2,128)S(1)}, u32[]{:S(2)}, u32[]{:S(2)}) collective-permute-start(f32[2,256]{1,0:T(2,128)S(1)} %add.65), channel_id=1, source_target_pairs={{12,0},{13,1},{14,2},{15,3},{8,4},{9,5},{10,6},{11,7},{4,8},{5,9},... | collective-permute-start | bytes 6152 | tf_op jit(solution)/shard_map/ppermute | solution.py:328
  152.0 3.6 %collective-permute-start.14 = (f32[2,256]{1,0:T(2,128)S(1)}, f32[2,256]{1,0:T(2,128)S(1)}, u32[]{:S(2)}, u32[]{:S(2)}) collective-permute-start(f32[2,256]{1,0:T(2,128)S(1)} %add.66), channel_id=1, source_target_pairs={{64,0},{65,1},{66,2},{67,3},{68,4},{69,5},{70,6},{71,7},{72,8},{73... | collective-permute-start | bytes 6152 | tf_op jit(solution)/shard_map/ppermute | solution.py:328
  155.6 4.8 %collective-permute-start.15 = (f32[2,256]{1,0:T(2,128)S(1)}, f32[2,256]{1,0:T(2,128)S(1)}, u32[]{:S(2)}, u32[]{:S(2)}) collective-permute-start(f32[2,256]{1,0:T(2,128)S(1)} %add.67), channel_id=1, source_target_pairs={{192,0},{193,1},{194,2},{195,3},{196,4},{197,5},{198,6},{199,7},{2... | collective-permute-start | bytes 6152 | tf_op jit(solution)/shard_map/ppermute | solution.py:328
  164.0 11.7 %collective-permute-start.27 = (f32[2,64,256]{2,1,0:T(8,128)S(1)}, f32[2,64,256]{2,1,0:T(8,128)S(1)}, u32[]{:S(2)}, u32[]{:S(2)}) collective-permute-start(f32[2,64,256]{2,1,0:T(8,128)S(1)} %get-tuple-element.53), channel_id=1, source_target_pairs={{15,0},{0,1},{1,2},{2,3},{3,4},{4,5},{5,6},{6,7},{7,8},{8,9},{9,10... | collective-permute-start | bytes 393224 | tf_op jit(solution)/shard_map/ppermute | solution.py:302
  175.7 31.9 %collective-permute-start.28 = (f32[64,256]{1,0:T(8,128)S(1)}, f32[64,256]{1,0:T(8,128)S(1)}, u32[]{:S(2)}, u32[]{:S(2)}) collective-permute-start(f32[64,256]{1,0:T(8,128)S(1)} %fusion), channel_id=1, source_target_pairs={{240,0},{241,1},{242,2},{243,3},{244,4},{245,5},{246,6},{247,7},{2... | collective-permute-start | bytes 196616 | tf_op jit(solution)/shard_map/ppermute | solution.py:302
  175.8 5.5 %collective-permute-start.17 = (f32[1,256]{1,0:T(1,128)S(1)}, f32[1,256]{1,0:T(1,128)S(1)}, u32[]{:S(2)}, u32[]{:S(2)}) collective-permute-start(f32[1,256]{1,0:T(1,128)S(1)} %get-tuple-element.48), channel_id=1, source_target_pairs={{48,0},{49,1},{50,2},{51,3},{52,4},{53,5},{54,6},{55,7},{56,8},{57... | collective-permute-start | bytes 3080 | tf_op jit(solution)/shard_map/ppermute | solution.py:328
  181.3 4.8 %collective-permute-start.18 = (f32[1,256]{1,0:T(1,128)S(1)}, f32[1,256]{1,0:T(1,128)S(1)}, u32[]{:S(2)}, u32[]{:S(2)}) collective-permute-start(f32[1,256]{1,0:T(1,128)S(1)} %add.69), channel_id=1, source_target_pairs={{50,0},{51,1},{48,2},{49,3},{54,4},{55,5},{52,6},{53,7},{58,8},{59... | collective-permute-start | bytes 3080 | tf_op jit(solution)/shard_map/ppermute | solution.py:328
  193.3 4.8 %collective-permute-start.21 = (f32[1,256]{1,0:T(1,128)S(1)}, f32[1,256]{1,0:T(1,128)S(1)}, u32[]{:S(2)}, u32[]{:S(2)}) collective-permute-start(f32[1,256]{1,0:T(1,128)S(1)} %add.72), channel_id=1, source_target_pairs={{12,0},{13,1},{14,2},{15,3},{8,4},{9,5},{10,6},{11,7},{4,8},{5,9},... | collective-permute-start | bytes 3080 | tf_op jit(solution)/shard_map/ppermute | solution.py:328
  201.7 4.8 %collective-permute-start.23 = (f32[1,256]{1,0:T(1,128)S(1)}, f32[1,256]{1,0:T(1,128)S(1)}, u32[]{:S(2)}, u32[]{:S(2)}) collective-permute-start(f32[1,256]{1,0:T(1,128)S(1)} %add.74), channel_id=1, source_target_pairs={{192,0},{193,1},{194,2},{195,3},{196,4},{197,5},{198,6},{199,7},{2... | collective-permute-start | bytes 3080 | tf_op jit(solution)/shard_map/ppermute | solution.py:328
  (27 other events, 120.9 us)

commit v5 on v4

--- a/solution.py
+++ b/solution.py
@@ -124,19 +124,23 @@
     c_aa[...] = couple(proj[...], rows, own[...])
 
 
-def first_body(states, core, rho, proj, back, own_u, own_c, msg_u, msg_c, c):
-    mols = rho.shape[0]
+def stack_two(low, high, states):
+    return jnp.concatenate([stack(low, states // 2), stack(high, states // 2)], axis=0)
+
+
+def first_body(states, core, low, high, proj, back, own_u, own_c, msg_u, msg_c, c):
+    mols = low.shape[0]
     field = msg_u.shape[1] - 4 * mols
     part = slice(field, field + mols)
-    rows = stack(rho, states)
+    rows = stack_two(low, high, states)
     c[0] = couple(proj[...], rows, choose(core, own_u[...], own_c[...]))
     c[1] = couple(rows, back[...], twice(choose(core, msg_u[:, part], msg_c[:, part])))
 
 
-def right_body(states, rho_a, rho_r, metric, proj_a, own, msg_r, proj_r, back_r, c):
+def right_body(states, rho_a, low, high, metric, proj_a, own, msg_r, proj_r, back_r, c):
     mols = rho_a.shape[0]
     field = msg_r.shape[1] - 4 * mols
-    rows = stack(rho_r, states)
+    rows = stack_two(low, high, states)
     proj_r[...] = dot(rows, metric[...]).astype(BF)
     back_r[...] = dot_nt(rows, metric[...]).astype(BF)
     c[0] = couple(proj_a[...], rows, own[...])
@@ -161,9 +165,12 @@
 def corner_body(
     states,
     core,
-    rho_f,
-    near,
-    shifted,
+    first_low,
+    first_high,
+    near_low,
+    near_high,
+    shift_low,
+    shift_high,
     proj_a,
     back_a,
     proj_r,
@@ -186,13 +193,16 @@
     rows,
 ):
     mols, field = y_a.shape
-    width = rho_f.shape[1] // states
+    width = first_low.shape[1] * 2 // states
     part = slice(field, field + mols)
     half = slice(field + mols, field + 2 * mols)
+    halves = ((first_low, near_low, shift_low), (first_high, near_high, shift_high))
     for a in range(states):
-        lanes = slice(a * width, (a + 1) * width)
+        first, near, shifted = halves[a * 2 // states]
+        b = a % (states // 2)
+        lanes = slice(b * width, (b + 1) * width)
         place = slice(a * mols, (a + 1) * mols)
-        rows[0, place] = rho_f[:, lanes]
+        rows[0, place] = first[:, lanes]
         rows[1, place] = choose(core, near[:, lanes], shifted[:, lanes])
     upper = rows.at[core[0, 0]]
     last = rows[1]
@@ -322,7 +332,7 @@
         flip(0, 1),
     ]
 
-    def butterfly(value):
+    def butterfly(value, steps):
         for k, partner in enumerate(steps):
             table = [(spot(*partner(x, y)), spot(x, y)) for x in range(nx) for y in range(ny)]
             other = lax.ppermute(value, AXES, table)
@@ -333,7 +343,11 @@
     rho_a, y_a, e_a = densities[0, 0], trials[0, 0], energies[0, 0]
     core = (lax.axis_index("gy") % 2).astype(jnp.int32).reshape(1, 1)
     table = [(spot(x + y % 2, y + 1), spot(x, y)) for x in range(nx) for y in range(ny)]
-    rho_f = lax.ppermute(rho_a, AXES, table)
+    half = rho_a.shape[1] // 2
+    first_low = lax.ppermute(rho_a[:, :half], AXES, table)
+    first_high = lax.ppermute(rho_a[:, half:], AXES, table)
+    right_low = take(rho_a[:, :half], 1, 0)
+    right_high = take(rho_a[:, half:], 1, 0)
 
     pair = shape(mols, 2 * mols)
     note = shape(mols, field + 4 * mols)
@@ -347,9 +361,11 @@
     msg_u = take(msg_u, 0, 1)
     msg_c = take(msg_c, 1, 1)
 
-    rho_r = take(rho_a, 1, 0)
-    near = take(rho_r, 0, 1, lambda x, y: y % 2 == 0)
-    shifted = take(rho_f, -1, 0, lambda x, y: y % 2 == 1)
+    even, odd = (lambda x, y: y % 2 == 0), (lambda x, y: y % 2 == 1)
+    shift_low = take(first_low, -1, 0, odd)
+    shift_high = take(first_high, -1, 0, odd)
+    near_low = take(right_low, 0, 1, even)
+    near_high = take(right_high, 0, 1, even)
 
     block = 2 * width * width * aux
     proj = 2 * width * aux * aux
@@ -360,14 +376,14 @@
         functools.partial(self_body, states), (wide, wide, square), 2 * proj + block, 5 * size
     )(rho_a, metric, own_a)
     c_f = call(functools.partial(first_body, states), squares_of(2), 2 * block, 4 * size, 1)(
-        core, rho_f, proj_a, back_a, own_u, own_c, msg_u, msg_c
+        core, first_low, first_high, proj_a, back_a, own_u, own_c, msg_u, msg_c
     )
     proj_r, back_r, c_r = call(
         functools.partial(right_body, states),
         (wide, wide, squares_of(2)),
         2 * proj + 2 * block,
         8 * size,
-    )(rho_a, rho_r, metric, proj_a, own_r, msg_r)
+    )(rho_a, right_low, right_high, metric, proj_a, own_r, msg_r)
     one, two = shape(mols, field), shape(2, mols, field)
     c_s, to_a, to_r, to_uc, sums = call(
         functools.partial(corner_body, states),
@@ -378,9 +394,12 @@
         [pltpu.VMEM((2, width, aux), BF)],
     )(
         core,
-        rho_f,
-        near,
-        shifted,
+        first_low,
+        first_high,
+        near_low,
+        near_high,
+        shift_low,
+        shift_high,
         proj_a,
         back_a,
         proj_r,
@@ -402,7 +421,7 @@
         left = take(to_r + below[1], -1, 0)
         return below, left
 
-    sums = butterfly(sums)
+    sums = butterfly(sums, steps)
     below, left = home(to_r, to_uc)
     sigma = (to_a + below[0]) + left
     sig_r = take(sigma, 1, 0)
@@ -420,7 +439,7 @@
         9 * width * width * 2,
         1,
     )(core, theta, resid, sig_r, sig_uc, msg_r, msg_u, msg_c, c_aa, c_f, c_r, c_s)
-    squares = butterfly(squares)
+    squares = butterfly(squares, [steps[3], *steps[:3], *steps[4:]])
     below, left = home(to_r, to_uc)
     corr, sigma2 = call(
         functools.partial(last_body, states, float(width * nx * ny)),

time: 210 us -> 204 us (0.971)
  waiting for transfers between devices: 125 us -> 120 us
  local copies, waits for them, and re-layouts: 11.3 us -> 7.63 us
    unnamed x45 -> x43, local copies, waits for them, and re-layouts: 11.3 us -> 6.32 us
    ppermute x16, waiting for transfers between devices: 54.1 us -> 49.3 us  [butterfly(): other = lax.ppermute(value, AXES, table)]
    ppermute x12 -> x15, waiting for transfers between devices: 70.5 us -> 71 us  [take(): return lax.ppermute(value, AXES, table)]
    ppermute x12 -> x15, starting transfers between devices: 29.7 us -> 29.2 us  [take(): return lax.ppermute(value, AXES, table)]
  transfers between devices with their start and end apart: 29 -> 33, of which waited for: 22 -> 22; matrix products, arithmetic and copies ran while one was open for 0% -> 0% of each run, Pallas kernels for 5% -> 6%
where the time goes in v5:
time: 204 us; the launch traced here: 202 us
  waiting for transfers between devices  120 us (59%)
  starting transfers between devices  52.6 us (26%)
  Pallas kernels  20.4 us (10%)
  local copies, waits for them, and re-layouts  7.63 us (4%)
    ppermute x15, waiting for transfers between devices, take(): return lax.ppermute(value, AXES, table)  71 us
    ppermute x16, waiting for transfers between devices, butterfly(): other = lax.ppermute(value, AXES, table)  49.3 us
    ppermute x15, starting transfers between devices, take(): return lax.ppermute(value, AXES, table)  29.2 us
    pallas_call x8, Pallas kernels, call(): pl.pallas_call(body, out_shape=outs, in_specs=[pl.BlockSpec(memory_space=...  20.4 us
    ppermute x16, starting transfers between devices, butterfly(): other = lax.ppermute(value, AXES, table)  19.7 us
    unnamed x43, local copies, waits for them, and re-layouts  6.32 us
  transfers between devices with their start and end apart: 33, of which 22 were waited for; matrix products, arithmetic and copies ran while one was open for 0% of the time, Pallas kernels for 6%

profile of v5, /device:TPU:24, one launch (start us, length us, event | category | flops | bytes accessed | tf_op | source)
XLA Modules:
  0.0 202.0 jit_solution(9452175118687410427)
XLA Ops:
  2.0 4.9 %collective-permute-start.4 = (bf16[64,4096]{1,0:T(8,128)(2,1)S(1)}, bf16[64,4096]{1,0:T(8,128)(2,1)}, u32[]{:S(2)}, u32[]{:S(2)}) collective-permute-start(bf16[64,4096]{1,0:T(8,128)(2,1)S(1)} %get-tuple-element.58), channel_id=1, source_target_pairs={{16,0},{17,1},{18,2},{19,3},{20,4},{21,5},{22,6},{23,7},{24,8},{25... | collective-permute-start | bytes 1572872 | tf_op jit(solution)/shard_map/ppermute | solution.py:312
  6.9 3.6 %collective-permute-start.1 = (bf16[64,4096]{1,0:T(8,128)(2,1)S(1)}, bf16[64,4096]{1,0:T(8,128)(2,1)S(1)}, u32[]{:S(2)}, u32[]{:S(2)}) collective-permute-start(bf16[64,4096]{1,0:T(8,128)(2,1)S(1)} %get-tuple-element.58), channel_id=1, source_target_pairs={{1,0},{18,1},{3,2},{20,3},{5,4},{22,5},{7,6},{24,7},{9,8},{26,9},{... | collective-permute-start | bytes 1572872 | tf_op jit(solution)/shard_map/ppermute | solution.py:348
  18.3 39.1 %collective-permute-done.9.msg_u = f32[64,512]{1,0:T(8,128)S(1)} collective-permute-done((f32[64,512]{1,0:T(8,128)S(1)}, f32[64,512]{1,0:T(8,128)S(1)}, u32[]{:S(2)}, u32[]{:S(2)}) %collective-permute-start.9) | collective-permute-done | bytes 131104 | tf_op jit(solution)/shard_map/ppermute | solution.py:312
  57.4 4.4 %collective-permute-done.10.msg_c = f32[64,512]{1,0:T(8,128)S(1)} collective-permute-done((f32[64,512]{1,0:T(8,128)S(1)}, f32[64,512]{1,0:T(8,128)S(1)}, u32[]{:S(2)}, u32[]{:S(2)}) %collective-permute-start.10) | collective-permute-done | bytes 131104 | tf_op jit(solution)/shard_map/ppermute | solution.py:312
  61.8 4.9 %collective-permute-start.8 = (f32[64,512]{1,0:T(8,128)}, f32[64,512]{1,0:T(8,128)S(1)}, u32[]{:S(2)}, u32[]{:S(2)}) collective-permute-start(f32[64,512]{1,0:T(8,128)} %get-tuple-element.35), channel_id=1, source_target_pairs={{16,0},{17,1},{18,2},{19,3},{20,4},{21,5},{22,6},{23,7},{24,8},{25... | collective-permute-start | bytes 393224 | tf_op jit(solution)/shard_map/ppermute | solution.py:312
  82.1 4.6 %shard_map.104 = (bf16[512,1024]{1,0:T(8,128)(2,1)S(1)}, bf16[512,1024]{1,0:T(8,128)(2,1)S(1)}, bf16[2,512,512]{2,1,0:T(8,128)(2,1)S(1)}) custom-call(bf16[64,8192]{1,0:T(8,128)(2,1)S(1)} %bitcast.29, bf16[64,4096]{1,0:T(8,128)(2,1)} %collective-permute-done.2.low, bf16[64,4096]{1,0:T(8,128)(2,1)} %collective-permute-done.4.high, ...), custom_call_target="tpu_custom_call" | custom-call | flops 3221225472 | bytes 8388608 | tf_op jit(solution)/shard_map/pallas_call | solution.py:23
  86.8 5.5 %shard_map.106 = (bf16[4,512,512]{2,1,0:T(8,128)(2,1)S(1)}, f32[64,256]{1,0:T(8,128)S(1)}, f32[64,256]{1,0:T(8,128)S(1)}, f32[2,64,256]{2,1,0:T(8,128)S(1)}, f32[2,256]{1,0:T(2,128)S(1)}) custom-call(s32[1,1]{1,0:T(1,128)} %bitcast.core, bf16[64,4096]{1,0:T(8,128)(2,1)} %collective-permute-done.low.first_low, ...), custom_call_target="tpu_custom_call" | custom-call | flops 2147483648 | bytes 9437184 | tf_op jit(solution)/shard_map/pallas_call | solution.py:23
  92.3 7.1 %collective-permute-start.11 = (f32[2,64,256]{2,1,0:T(8,128)S(1)}, f32[2,64,256]{2,1,0:T(8,128)S(1)}, u32[]{:S(2)}, u32[]{:S(2)}) collective-permute-start(f32[2,64,256]{2,1,0:T(8,128)S(1)} %get-tuple-element.45), channel_id=1, source_target_pairs={{15,0},{0,1},{1,2},{2,3},{3,4},{4,5},{5,6},{6,7},{7,8},{8,9},{9,10... | collective-permute-start | bytes 393224 | tf_op jit(solution)/shard_map/ppermute | solution.py:312
  99.4 8.0 %collective-permute-done.11 = f32[2,64,256]{2,1,0:T(8,128)S(1)} collective-permute-done((f32[2,64,256]{2,1,0:T(8,128)S(1)}, f32[2,64,256]{2,1,0:T(8,128)S(1)}, u32[]{:S(2)}, u32[]{:S(2)}) %collective-permute-start.11) | collective-permute-done | bytes 131104 | tf_op jit(solution)/shard_map/ppermute | solution.py:312
  107.7 6.7 %collective-permute-done.12 = f32[64,256]{1,0:T(8,128)S(1)} collective-permute-done((f32[64,256]{1,0:T(8,128)S(1)}, f32[64,256]{1,0:T(8,128)S(1)}, u32[]{:S(2)}, u32[]{:S(2)}) %collective-permute-start.12) | collective-permute-done | bytes 65568 | tf_op jit(solution)/shard_map/ppermute | solution.py:312
  118.9 8.1 %collective-permute-start.13 = (f32[2,256]{1,0:T(2,128)S(1)}, f32[2,256]{1,0:T(2,128)S(1)}, u32[]{:S(2)}, u32[]{:S(2)}) collective-permute-start(f32[2,256]{1,0:T(2,128)S(1)} %get-tuple-element.47), channel_id=1, source_target_pairs={{48,0},{49,1},{50,2},{51,3},{52,4},{53,5},{54,6},{55,7},{56,8},{57... | collective-permute-start | bytes 6152 | tf_op jit(solution)/shard_map/ppermute | solution.py:338
  127.0 2.9 %collective-permute-done.13 = f32[2,256]{1,0:T(2,128)S(1)} collective-permute-done((f32[2,256]{1,0:T(2,128)S(1)}, f32[2,256]{1,0:T(2,128)S(1)}, u32[]{:S(2)}, u32[]{:S(2)}) %collective-permute-start.13) | collective-permute-done | bytes 2080 | tf_op jit(solution)/shard_map/ppermute | solution.py:338
  129.9 4.8 %collective-permute-done.14 = f32[2,256]{1,0:T(2,128)S(1)} collective-permute-done((f32[2,256]{1,0:T(2,128)S(1)}, f32[2,256]{1,0:T(2,128)S(1)}, u32[]{:S(2)}, u32[]{:S(2)}) %collective-permute-start.14) | collective-permute-done | bytes 2080 | tf_op jit(solution)/shard_map/ppermute | solution.py:338
  134.7 3.6 %collective-permute-done.15 = f32[2,256]{1,0:T(2,128)S(1)} collective-permute-done((f32[2,256]{1,0:T(2,128)S(1)}, f32[2,256]{1,0:T(2,128)S(1)}, u32[]{:S(2)}, u32[]{:S(2)}) %collective-permute-start.15) | collective-permute-done | bytes 2080 | tf_op jit(solution)/shard_map/ppermute | solution.py:338
  138.3 3.6 %collective-permute-done.16 = f32[2,256]{1,0:T(2,128)S(1)} collective-permute-done((f32[2,256]{1,0:T(2,128)S(1)}, f32[2,256]{1,0:T(2,128)S(1)}, u32[]{:S(2)}, u32[]{:S(2)}) %collective-permute-start.16) | collective-permute-done | bytes 2080 | tf_op jit(solution)/shard_map/ppermute | solution.py:338
  143.5 3.2 %collective-permute-done.17 = f32[2,256]{1,0:T(2,128)S(1)} collective-permute-done((f32[2,256]{1,0:T(2,128)S(1)}, f32[2,256]{1,0:T(2,128)S(1)}, u32[]{:S(2)}, u32[]{:S(2)}) %collective-permute-start.17) | collective-permute-done | bytes 2080 | tf_op jit(solution)/shard_map/ppermute | solution.py:338
  146.7 3.6 %collective-permute-done.18 = f32[2,256]{1,0:T(2,128)S(1)} collective-permute-done((f32[2,256]{1,0:T(2,128)S(1)}, f32[2,256]{1,0:T(2,128)S(1)}, u32[]{:S(2)}, u32[]{:S(2)}) %collective-permute-start.18) | collective-permute-done | bytes 2080 | tf_op jit(solution)/shard_map/ppermute | solution.py:338
  151.0 4.1 %collective-permute-done.19 = f32[2,256]{1,0:T(2,128)S(1)} collective-permute-done((f32[2,256]{1,0:T(2,128)S(1)}, f32[2,256]{1,0:T(2,128)S(1)}, u32[]{:S(2)}, u32[]{:S(2)}) %collective-permute-start.19) | collective-permute-done | bytes 2080 | tf_op jit(solution)/shard_map/ppermute | solution.py:338
  159.0 10.3 %collective-permute-done.31.below = f32[2,64,256]{2,1,0:T(8,128)S(1)} collective-permute-done((f32[2,64,256]{2,1,0:T(8,128)S(1)}, f32[2,64,256]{2,1,0:T(8,128)S(1)}, u32[]{:S(2)}, u32[]{:S(2)}) %collective-permute-start.31) | collective-permute-done | bytes 131104 | tf_op jit(solution)/shard_map/ppermute | solution.py:312
  169.5 3.6 %collective-permute-done.21 = f32[1,256]{1,0:T(1,128)S(1)} collective-permute-done((f32[1,256]{1,0:T(1,128)S(1)}, f32[1,256]{1,0:T(1,128)S(1)}, u32[]{:S(2)}, u32[]{:S(2)}) %collective-permute-start.21) | collective-permute-done | bytes 1056 | tf_op jit(solution)/shard_map/ppermute | solution.py:338
  173.1 3.8 %collective-permute-start.22 = (f32[1,256]{1,0:T(1,128)S(1)}, f32[1,256]{1,0:T(1,128)S(1)}, u32[]{:S(2)}, u32[]{:S(2)}) collective-permute-start(f32[1,256]{1,0:T(1,128)S(1)} %add.69), channel_id=1, source_target_pairs={{48,0},{49,1},{50,2},{51,3},{52,4},{53,5},{54,6},{55,7},{56,8},{57... | collective-permute-start | bytes 3080 | tf_op jit(solution)/shard_map/ppermute | solution.py:338
  179.9 3.3 %collective-permute-done.23 = f32[1,256]{1,0:T(1,128)S(1)} collective-permute-done((f32[1,256]{1,0:T(1,128)S(1)}, f32[1,256]{1,0:T(1,128)S(1)}, u32[]{:S(2)}, u32[]{:S(2)}) %collective-permute-start.23) | collective-permute-done | bytes 1056 | tf_op jit(solution)/shard_map/ppermute | solution.py:338
  187.2 4.4 %collective-permute-done.25 = f32[1,256]{1,0:T(1,128)S(1)} collective-permute-done((f32[1,256]{1,0:T(1,128)S(1)}, f32[1,256]{1,0:T(1,128)S(1)}, u32[]{:S(2)}, u32[]{:S(2)}) %collective-permute-start.25) | collective-permute-done | bytes 1056 | tf_op jit(solution)/shard_map/ppermute | solution.py:338
  195.9 4.1 %collective-permute-done.27 = f32[1,256]{1,0:T(1,128)S(1)} collective-permute-done((f32[1,256]{1,0:T(1,128)S(1)}, f32[1,256]{1,0:T(1,128)S(1)}, u32[]{:S(2)}, u32[]{:S(2)}) %collective-permute-start.27) | collective-permute-done | bytes 1056 | tf_op jit(solution)/shard_map/ppermute | solution.py:338
  (112 shorter events, 48.9 us)
Async XLA Ops:
  2.0 64.7 %collective-permute-start.4 = (bf16[64,4096]{1,0:T(8,128)(2,1)S(1)}, bf16[64,4096]{1,0:T(8,128)(2,1)}, u32[]{:S(2)}, u32[]{:S(2)}) collective-permute-start(bf16[64,4096]{1,0:T(8,128)(2,1)S(1)} %get-tuple-element.58), channel_id=1, source_target_pairs={{16,0},{17,1},{18,2},{19,3},{20,4},{21,5},{22,6},{23,7},{24,8},{25... | collective-permute-start | bytes 1572872 | tf_op jit(solution)/shard_map/ppermute | solution.py:312
  6.9 61.1 %collective-permute-start.1 = (bf16[64,4096]{1,0:T(8,128)(2,1)S(1)}, bf16[64,4096]{1,0:T(8,128)(2,1)S(1)}, u32[]{:S(2)}, u32[]{:S(2)}) collective-permute-start(bf16[64,4096]{1,0:T(8,128)(2,1)S(1)} %get-tuple-element.58), channel_id=1, source_target_pairs={{1,0},{18,1},{3,2},{20,3},{5,4},{22,5},{7,6},{24,7},{9,8},{26,9},{... | collective-permute-start | bytes 1572872 | tf_op jit(solution)/shard_map/ppermute | solution.py:348
  10.5 59.0 %collective-permute-start.2 = (bf16[64,4096]{1,0:T(8,128)(2,1)S(1)}, bf16[64,4096]{1,0:T(8,128)(2,1)}, u32[]{:S(2)}, u32[]{:S(2)}) collective-permute-start(bf16[64,4096]{1,0:T(8,128)(2,1)S(1)} %get-tuple-element.59), channel_id=1, source_target_pairs={{16,0},{17,1},{18,2},{19,3},{20,4},{21,5},{22,6},{23,7},{24,8},{25... | collective-permute-start | bytes 1572872 | tf_op jit(solution)/shard_map/ppermute | solution.py:312
  13.3 57.5 %collective-permute-start = (bf16[64,4096]{1,0:T(8,128)(2,1)S(1)}, bf16[64,4096]{1,0:T(8,128)(2,1)}, u32[]{:S(2)}, u32[]{:S(2)}) collective-permute-start(bf16[64,4096]{1,0:T(8,128)(2,1)S(1)} %get-tuple-element.59), channel_id=1, source_target_pairs={{1,0},{18,1},{3,2},{20,3},{5,4},{22,5},{7,6},{24,7},{9,8},{26,9},{... | collective-permute-start | bytes 1572872 | tf_op jit(solution)/shard_map/ppermute | solution.py:347
  16.9 40.5 %collective-permute-start.9 = (f32[64,512]{1,0:T(8,128)S(1)}, f32[64,512]{1,0:T(8,128)S(1)}, u32[]{:S(2)}, u32[]{:S(2)}) collective-permute-start(f32[64,512]{1,0:T(8,128)S(1)} %get-tuple-element.40), channel_id=1, source_target_pairs={{1,0},{2,1},{3,2},{4,3},{5,4},{6,5},{7,6},{8,7},{9,8},{10,9},{11,1... | collective-permute-start | bytes 393224 | tf_op jit(solution)/shard_map/ppermute | solution.py:312
  57.4 4.4 %collective-permute-start.10 = (f32[64,512]{1,0:T(8,128)S(1)}, f32[64,512]{1,0:T(8,128)S(1)}, u32[]{:S(2)}, u32[]{:S(2)}) collective-permute-start(f32[64,512]{1,0:T(8,128)S(1)} %get-tuple-element.41), channel_id=1, source_target_pairs={{17,0},{18,1},{19,2},{20,3},{21,4},{22,5},{23,6},{24,7},{25,8},{26... | collective-permute-start | bytes 393224 | tf_op jit(solution)/shard_map/ppermute | solution.py:312
  61.8 20.2 %collective-permute-start.8 = (f32[64,512]{1,0:T(8,128)}, f32[64,512]{1,0:T(8,128)S(1)}, u32[]{:S(2)}, u32[]{:S(2)}) collective-permute-start(f32[64,512]{1,0:T(8,128)} %get-tuple-element.35), channel_id=1, source_target_pairs={{16,0},{17,1},{18,2},{19,3},{20,4},{21,5},{22,6},{23,7},{24,8},{25... | collective-permute-start | bytes 393224 | tf_op jit(solution)/shard_map/ppermute | solution.py:312
  66.7 20.0 %collective-permute-start.5 = (bf16[64,4096]{1,0:T(8,128)(2,1)}, bf16[64,4096]{1,0:T(8,128)(2,1)}, u32[]{:S(2)}, u32[]{:S(2)}) collective-permute-start(bf16[64,4096]{1,0:T(8,128)(2,1)} %collective-permute-done.4.high), channel_id=1, source_target_pairs={{1,0},{3,2},{5,4},{7,6},{9,8},{11,10},{13,12},{15,14},{17,16},{19,... | collective-permute-start | bytes 1572872 | tf_op jit(solution)/shard_map/ppermute | solution.py:312
  68.0 18.7 %collective-permute-start.7 = (bf16[64,4096]{1,0:T(8,128)(2,1)S(1)}, bf16[64,4096]{1,0:T(8,128)(2,1)}, u32[]{:S(2)}, u32[]{:S(2)}) collective-permute-start(bf16[64,4096]{1,0:T(8,128)(2,1)S(1)} %collective-permute-done.1.high.first_high), channel_id=1, source_target_pairs={{241,1},{243,3},{245,5},{247,7},{249,9},{251,11},{253,13},{255,15}... | collective-permute-start | bytes 1572872 | tf_op jit(solution)/shard_map/ppermute | solution.py:312
  69.5 17.3 %collective-permute-start.3 = (bf16[64,4096]{1,0:T(8,128)(2,1)}, bf16[64,4096]{1,0:T(8,128)(2,1)}, u32[]{:S(2)}, u32[]{:S(2)}) collective-permute-start(bf16[64,4096]{1,0:T(8,128)(2,1)} %collective-permute-done.2.low), channel_id=1, source_target_pairs={{1,0},{3,2},{5,4},{7,6},{9,8},{11,10},{13,12},{15,14},{17,16},{19,... | collective-permute-start | bytes 1572872 | tf_op jit(solution)/shard_map/ppermute | solution.py:312
  70.8 16.0 %collective-permute-start.6 = (bf16[64,4096]{1,0:T(8,128)(2,1)}, bf16[64,4096]{1,0:T(8,128)(2,1)}, u32[]{:S(2)}, u32[]{:S(2)}) collective-permute-start(bf16[64,4096]{1,0:T(8,128)(2,1)} %collective-permute-done.low.first_low), channel_id=1, source_target_pairs={{241,1},{243,3},{245,5},{247,7},{249,9},{251,11},{253,13},{255,15}... | collective-permute-start | bytes 1572872 | tf_op jit(solution)/shard_map/ppermute | solution.py:312
  92.3 15.1 %collective-permute-start.11 = (f32[2,64,256]{2,1,0:T(8,128)S(1)}, f32[2,64,256]{2,1,0:T(8,128)S(1)}, u32[]{:S(2)}, u32[]{:S(2)}) collective-permute-start(f32[2,64,256]{2,1,0:T(8,128)S(1)} %get-tuple-element.45), channel_id=1, source_target_pairs={{15,0},{0,1},{1,2},{2,3},{3,4},{4,5},{5,6},{6,7},{7,8},{8,9},{9,10... | collective-permute-start | bytes 393224 | tf_op jit(solution)/shard_map/ppermute | solution.py:312
  107.4 7.0 %collective-permute-start.12 = (f32[64,256]{1,0:T(8,128)S(1)}, f32[64,256]{1,0:T(8,128)S(1)}, u32[]{:S(2)}, u32[]{:S(2)}) collective-permute-start(f32[64,256]{1,0:T(8,128)S(1)} %fusion.1), channel_id=1, source_target_pairs={{240,0},{241,1},{242,2},{243,3},{244,4},{245,5},{246,6},{247,7},{2... | collective-permute-start | bytes 196616 | tf_op jit(solution)/shard_map/ppermute | solution.py:312
  118.8 38.1 %collective-permute-start.30 = (f32[2,64,256]{2,1,0:T(8,128)S(1)}, f32[2,64,256]{2,1,0:T(8,128)S(1)}, u32[]{:S(2)}, u32[]{:S(2)}) collective-permute-start(f32[2,64,256]{2,1,0:T(8,128)S(1)} %pad_maximum_fusion), channel_id=1, source_target_pairs={{1,0},{2,1},{3,2},{4,3},{5,4},{6,5},{7,6},{8,7},{9,8},{10,9},{11,1... | collective-permute-start | bytes 393224 | tf_op jit(solution)/shard_map/ppermute | solution.py:312
  118.9 11.0 %collective-permute-start.13 = (f32[2,256]{1,0:T(2,128)S(1)}, f32[2,256]{1,0:T(2,128)S(1)}, u32[]{:S(2)}, u32[]{:S(2)}) collective-permute-start(f32[2,256]{1,0:T(2,128)S(1)} %get-tuple-element.47), channel_id=1, source_target_pairs={{48,0},{49,1},{50,2},{51,3},{52,4},{53,5},{54,6},{55,7},{56,8},{57... | collective-permute-start | bytes 6152 | tf_op jit(solution)/shard_map/ppermute | solution.py:338
  129.9 4.8 %collective-permute-start.14 = (f32[2,256]{1,0:T(2,128)S(1)}, f32[2,256]{1,0:T(2,128)S(1)}, u32[]{:S(2)}, u32[]{:S(2)}) collective-permute-start(f32[2,256]{1,0:T(2,128)S(1)} %add.62), channel_id=1, source_target_pairs={{50,0},{51,1},{48,2},{49,3},{54,4},{55,5},{52,6},{53,7},{58,8},{59... | collective-permute-start | bytes 6152 | tf_op jit(solution)/shard_map/ppermute | solution.py:338
  141.9 4.8 %collective-permute-start.17 = (f32[2,256]{1,0:T(2,128)S(1)}, f32[2,256]{1,0:T(2,128)S(1)}, u32[]{:S(2)}, u32[]{:S(2)}) collective-permute-start(f32[2,256]{1,0:T(2,128)S(1)} %add.65), channel_id=1, source_target_pairs={{12,0},{13,1},{14,2},{15,3},{8,4},{9,5},{10,6},{11,7},{4,8},{5,9},... | collective-permute-start | bytes 6152 | tf_op jit(solution)/shard_map/ppermute | solution.py:338
  150.3 4.8 %collective-permute-start.19 = (f32[2,256]{1,0:T(2,128)S(1)}, f32[2,256]{1,0:T(2,128)S(1)}, u32[]{:S(2)}, u32[]{:S(2)}) collective-permute-start(f32[2,256]{1,0:T(2,128)S(1)} %add.67), channel_id=1, source_target_pairs={{192,0},{193,1},{194,2},{195,3},{196,4},{197,5},{198,6},{199,7},{2... | collective-permute-start | bytes 6152 | tf_op jit(solution)/shard_map/ppermute | solution.py:338
  158.7 10.6 %collective-permute-start.31 = (f32[2,64,256]{2,1,0:T(8,128)S(1)}, f32[2,64,256]{2,1,0:T(8,128)S(1)}, u32[]{:S(2)}, u32[]{:S(2)}) collective-permute-start(f32[2,64,256]{2,1,0:T(8,128)S(1)} %get-tuple-element.53), channel_id=1, source_target_pairs={{15,0},{0,1},{1,2},{2,3},{3,4},{4,5},{5,6},{6,7},{7,8},{8,9},{9,10... | collective-permute-start | bytes 393224 | tf_op jit(solution)/shard_map/ppermute | solution.py:312
  169.3 31.8 %collective-permute-start.32 = (f32[64,256]{1,0:T(8,128)S(1)}, f32[64,256]{1,0:T(8,128)S(1)}, u32[]{:S(2)}, u32[]{:S(2)}) collective-permute-start(f32[64,256]{1,0:T(8,128)S(1)} %fusion), channel_id=1, source_target_pairs={{240,0},{241,1},{242,2},{243,3},{244,4},{245,5},{246,6},{247,7},{2... | collective-permute-start | bytes 196616 | tf_op jit(solution)/shard_map/ppermute | solution.py:312
  173.1 5.4 %collective-permute-start.22 = (f32[1,256]{1,0:T(1,128)S(1)}, f32[1,256]{1,0:T(1,128)S(1)}, u32[]{:S(2)}, u32[]{:S(2)}) collective-permute-start(f32[1,256]{1,0:T(1,128)S(1)} %add.69), channel_id=1, source_target_pairs={{48,0},{49,1},{50,2},{51,3},{52,4},{53,5},{54,6},{55,7},{56,8},{57... | collective-permute-start | bytes 3080 | tf_op jit(solution)/shard_map/ppermute | solution.py:338
  178.5 4.8 %collective-permute-start.23 = (f32[1,256]{1,0:T(1,128)S(1)}, f32[1,256]{1,0:T(1,128)S(1)}, u32[]{:S(2)}, u32[]{:S(2)}) collective-permute-start(f32[1,256]{1,0:T(1,128)S(1)} %add.70), channel_id=1, source_target_pairs={{50,0},{51,1},{48,2},{49,3},{54,4},{55,5},{52,6},{53,7},{58,8},{59... | collective-permute-start | bytes 3080 | tf_op jit(solution)/shard_map/ppermute | solution.py:338
  186.8 4.8 %collective-permute-start.25 = (f32[1,256]{1,0:T(1,128)S(1)}, f32[1,256]{1,0:T(1,128)S(1)}, u32[]{:S(2)}, u32[]{:S(2)}) collective-permute-start(f32[1,256]{1,0:T(1,128)S(1)} %add.72), channel_id=1, source_target_pairs={{12,0},{13,1},{14,2},{15,3},{8,4},{9,5},{10,6},{11,7},{4,8},{5,9},... | collective-permute-start | bytes 3080 | tf_op jit(solution)/shard_map/ppermute | solution.py:338
  195.2 4.8 %collective-permute-start.27 = (f32[1,256]{1,0:T(1,128)S(1)}, f32[1,256]{1,0:T(1,128)S(1)}, u32[]{:S(2)}, u32[]{:S(2)}) collective-permute-start(f32[1,256]{1,0:T(1,128)S(1)} %add.74), channel_id=1, source_target_pairs={{192,0},{193,1},{194,2},{195,3},{196,4},{197,5},{198,6},{199,7},{2... | collective-permute-start | bytes 3080 | tf_op jit(solution)/shard_map/ppermute | solution.py:338
  (30 other events, 227.7 us)

commit v6 on v4

--- a/solution.py
+++ b/solution.py
@@ -85,18 +85,13 @@
             right = jnp.where(right >= mols, right - mols, right)
         mine = jnp.where(mol == left, factor, 0.0)
         far = jnp.where(mol == right, 1.0, 0.0).astype(BF)
-        high = mine.astype(BF)
-        rest = mine - high.astype(F32)
-        mid = rest.astype(BF)
-        low = (rest - mid.astype(F32)).astype(BF)
         three = dot_nt(
-            jnp.concatenate([high, mid, low], axis=0), jnp.concatenate([far, far], axis=0)
+            jnp.concatenate(split(mine, 3), axis=0), jnp.concatenate([far, far], axis=0)
         )
         return three[:mols] + (three[mols : 2 * mols] + three[2 * mols :])
 
     for own, o in ((own_a, SELF), (own_r, TO_R), (own_u, TO_U), (own_c, TO_UR)):
         own[...] = weight(o)
-    field = y.shape[1]
     for msg, o, q in (
         (msg_r, R_TO_A, R_TO_U),
         (msg_u, U_TO_A, U_TO_R),
@@ -106,11 +101,10 @@
         if q is not None:
             lane = lax.broadcasted_iota(jnp.int32, first.shape, 1)
             first = jnp.where(lane < mols, first, weight(q))
-        msg[:, :field] = y[...].astype(F32)
-        msg[:, field : field + 2 * mols] = first
-        msg[:, field + 2 * mols :] = jnp.concatenate(
-            [e[...], jnp.zeros((mols, 2 * mols - e.shape[1]), F32)], axis=1
-        )
+        energies = split(e[...], 3)
+        used = 3 * e.shape[1]
+        parts = [y[...], *split(first, 2), *energies, jnp.zeros((mols, 2 * mols - used), BF)]
+        msg[...] = jnp.concatenate(parts, axis=1)
 
 
 def choose(core, low, high):
@@ -124,29 +118,51 @@
     c_aa[...] = couple(proj[...], rows, own[...])
 
 
+def stack_two(low, high, states):
+    return jnp.concatenate([stack(low, states // 2), stack(high, states // 2)], axis=0)
+
+
+def note_weights(note, mols, k):
+    base = note.shape[1] - 6 * mols + k * mols
+    high, low = note[:, base : base + mols], note[:, base + 2 * mols : base + 3 * mols]
+    return high.astype(F32) + low.astype(F32)
+
+
+def note_energies(note, states):
+    base = note.shape[1] - 2 * note.shape[0]
+    parts = [note[:, base + k * states : base + (k + 1) * states].astype(F32) for k in range(3)]
+    return parts[0] + (parts[1] + parts[2])
+
+
+def split(value, count):
+    parts = []
+    for _ in range(count):
+        parts.append(value.astype(BF))
+        value = value - parts[-1].astype(F32)
+    return parts
+
+
 def first_body(states, core, rho, proj, back, own_u, own_c, msg_u, msg_c, c):
     mols = rho.shape[0]
-    field = msg_u.shape[1] - 4 * mols
-    part = slice(field, field + mols)
     rows = stack(rho, states)
     c[0] = couple(proj[...], rows, choose(core, own_u[...], own_c[...]))
-    c[1] = couple(rows, back[...], twice(choose(core, msg_u[:, part], msg_c[:, part])))
-
-
-def right_body(states, rho_a, rho_r, metric, proj_a, own, msg_r, proj_r, back_r, c):
+    pair = choose(core, note_weights(msg_u, mols, 0), note_weights(msg_c, mols, 0))
+    c[1] = couple(rows, back[...], twice(pair))
+
+
+def right_body(states, rho_a, low, high, metric, proj_a, own, msg_r, proj_r, back_r, c):
     mols = rho_a.shape[0]
-    field = msg_r.shape[1] - 4 * mols
-    rows = stack(rho_r, states)
+    rows = stack_two(low, high, states)
     proj_r[...] = dot(rows, metric[...]).astype(BF)
     back_r[...] = dot_nt(rows, metric[...]).astype(BF)
     c[0] = couple(proj_a[...], rows, own[...])
-    c[1] = couple(proj_r[...], stack(rho_a, states), twice(msg_r[:, field : field + mols]))
+    c[1] = couple(proj_r[...], stack(rho_a, states), twice(note_weights(msg_r, mols, 0)))
 
 
 def fields(states, core, y_a, msg_r, msg_u, msg_c):
     field = y_a.shape[1]
     f_a = stack(y_a, states)
-    f_r, f_u, f_c = [stack(m[:, :field], states).astype(BF) for m in (msg_r, msg_u, msg_c)]
+    f_r, f_u, f_c = [stack(m[:, :field], states) for m in (msg_r, msg_u, msg_c)]
     return f_a, f_r, f_u, choose(core, f_u, f_c), choose(core, f_c, f_u)
 
 
@@ -162,7 +178,8 @@
     states,
     core,
     rho_f,
-    near,
+    near_low,
+    near_high,
     shifted,
     proj_a,
     back_a,
@@ -187,27 +204,28 @@
 ):
     mols, field = y_a.shape
     width = rho_f.shape[1] // states
-    part = slice(field, field + mols)
-    half = slice(field + mols, field + 2 * mols)
     for a in range(states):
+        near = (near_low, near_high)[a * 2 // states]
+        b = a % (states // 2)
         lanes = slice(a * width, (a + 1) * width)
         place = slice(a * mols, (a + 1) * mols)
         rows[0, place] = rho_f[:, lanes]
-        rows[1, place] = choose(core, near[:, lanes], shifted[:, lanes])
+        rows[1, place] = choose(core, near[:, b * width : (b + 1) * width], shifted[:, lanes])
     upper = rows.at[core[0, 0]]
     last = rows[1]
     c[0] = couple(proj_a[...], last, choose(core, own_c[...], own_u[...]))
-    c[1] = couple(last, back_a[...], twice(choose(core, msg_c[:, part], msg_u[:, part])))
-    c[2] = couple(proj_r[...], upper[...], twice(msg_r[:, half]))
-    c[3] = couple(upper[...], back_r[...], twice(msg_u[:, half]))
+    pair = choose(core, note_weights(msg_c, mols, 0), note_weights(msg_u, mols, 0))
+    c[1] = couple(last, back_a[...], twice(pair))
+    c[2] = couple(proj_r[...], upper[...], twice(note_weights(msg_r, mols, 1)))
+    c[3] = couple(upper[...], back_r[...], twice(note_weights(msg_u, mols, 1)))
     f = fields(states, core, y_a, msg_r, msg_u, msg_c)
     row_a, row_r, row_u, row_c = sums_of(core, c_aa, c_f, c_r, c, *f)
     own_y = y_a[...].astype(F32)
     part_a = unstack(row_a, states) + spread(e_a[...], field // states) * own_y
     part_r, part_u, part_c = [unstack(row, states) for row in (row_r, row_u, row_c)]
     to_a[...], to_r[...], to_uc[0], to_uc[1] = part_a, part_r, part_u, part_c
-    total = part_a * own_y + part_r * msg_r[:, :field]
-    total = total + (part_u * msg_u[:, :field] + part_c * msg_c[:, :field])
+    y_r, y_u, y_c = [m[:, :field].astype(F32) for m in (msg_r, msg_u, msg_c)]
+    total = (part_a * own_y + part_r * y_r) + (part_u * y_u + part_c * y_c)
     sums[0:1] = jnp.sum(total, axis=0, keepdims=True)
     sums[1:2] = jnp.sum(own_y * own_y, axis=0, keepdims=True)
 
@@ -253,12 +271,12 @@
     to_r,
     to_uc,
 ):
-    mols, field = resid.shape
+    _, field = resid.shape
     width = field // states
 
     def other(sigma, msg):
-        e = msg[:, field + 2 * mols : field + 2 * mols + states]
-        value = residual(sigma, msg[:, :field], e, theta[...], width)
+        e = note_energies(msg, states)
+        value = residual(sigma, msg[:, :field].astype(F32), e, theta[...], width)
         return stack(value, states).astype(BF)
 
     f_a = stack(resid[...], states).astype(BF)
@@ -321,8 +339,9 @@
         flip(12, 0),
         flip(0, 1),
     ]
-
-    def butterfly(value):
+    z_far, z_mid, z_near, x_near, x_far, y_near, y_far, chip = steps
+
+    def butterfly(value, steps):
         for k, partner in enumerate(steps):
             table = [(spot(*partner(x, y)), spot(x, y)) for x in range(nx) for y in range(ny)]
             other = lax.ppermute(value, AXES, table)
@@ -336,7 +355,7 @@
     rho_f = lax.ppermute(rho_a, AXES, table)
 
     pair = shape(mols, 2 * mols)
-    note = shape(mols, field + 4 * mols)
+    note = shape(mols, field + 6 * mols, dtype=BF)
     own_a, own_r, own_u, own_c, msg_r, msg_u, msg_c = call(
         functools.partial(weights_body, aux**-0.5),
         (pair, pair, pair, pair, note, note, note),
@@ -347,9 +366,13 @@
     msg_u = take(msg_u, 0, 1)
     msg_c = take(msg_c, 1, 1)
 
-    rho_r = take(rho_a, 1, 0)
-    near = take(rho_r, 0, 1, lambda x, y: y % 2 == 0)
-    shifted = take(rho_f, -1, 0, lambda x, y: y % 2 == 1)
+    half = rho_a.shape[1] // 2
+    even, odd = (lambda x, y: y % 2 == 0), (lambda x, y: y % 2 == 1)
+    right_low = take(rho_a[:, :half], 1, 0)
+    right_high = take(rho_a[:, half:], 1, 0)
+    shifted = take(rho_f, -1, 0, odd)
+    near_low = take(right_low, 0, 1, even)
+    near_high = take(right_high, 0, 1, even)
 
     block = 2 * width * width * aux
     proj = 2 * width * aux * aux
@@ -367,7 +390,7 @@
         (wide, wide, squares_of(2)),
         2 * proj + 2 * block,
         8 * size,
-    )(rho_a, rho_r, metric, proj_a, own_r, msg_r)
+    )(rho_a, right_low, right_high, metric, proj_a, own_r, msg_r)
     one, two = shape(mols, field), shape(2, mols, field)
     c_s, to_a, to_r, to_uc, sums = call(
         functools.partial(corner_body, states),
@@ -379,7 +402,8 @@
     )(
         core,
         rho_f,
-        near,
+        near_low,
+        near_high,
         shifted,
         proj_a,
         back_a,
@@ -402,7 +426,7 @@
         left = take(to_r + below[1], -1, 0)
         return below, left
 
-    sums = butterfly(sums)
+    sums = butterfly(sums, [z_far, chip, z_mid, z_near, x_near, x_far, y_near, y_far])
     below, left = home(to_r, to_uc)
     sigma = (to_a + below[0]) + left
     sig_r = take(sigma, 1, 0)
@@ -420,7 +444,7 @@
         9 * width * width * 2,
         1,
     )(core, theta, resid, sig_r, sig_uc, msg_r, msg_u, msg_c, c_aa, c_f, c_r, c_s)
-    squares = butterfly(squares)
+    squares = butterfly(squares, [x_near, z_far, chip, z_mid, z_near, x_far, y_near, y_far])
     below, left = home(to_r, to_uc)
     corr, sigma2 = call(
         functools.partial(last_body, states, float(width * nx * ny)),

time: 210 us -> 209 us (level)
  starting transfers between devices: 52.3 us -> 88.9 us
  waiting for transfers between devices: 125 us -> 91.2 us
  local copies, waits for them, and re-layouts: 11.3 us -> 7.8 us
    ppermute x12 -> x14, waiting for transfers between devices: 70.5 us -> 31.1 us  [take(): return lax.ppermute(value, AXES, table)]
    ppermute x12 -> x14, starting transfers between devices: 29.7 us -> 56.5 us  [take(): return lax.ppermute(value, AXES, table)]
    ppermute x1, waiting for transfers between devices: 0.01 us -> 8.73 us  [shards(): rho_f = lax.ppermute(rho_a, AXES, table)]
    ppermute x16, starting transfers between devices: 19 us -> 24.7 us  [butterfly(): other = lax.ppermute(value, AXES, table)]
    unnamed x45 -> x25, local copies, waits for them, and re-layouts: 11.3 us -> 6.53 us
    ppermute x1, starting transfers between devices: 3.59 us -> 7.75 us  [shards(): rho_f = lax.ppermute(rho_a, AXES, table)]
    ppermute x16, waiting for transfers between devices: 54.1 us -> 51.4 us  [butterfly(): other = lax.ppermute(value, AXES, table)]
  transfers between devices with their start and end apart: 29 -> 31, of which waited for: 22 -> 21; matrix products, arithmetic and copies ran while one was open for 0% -> 1% of each run, Pallas kernels for 5% -> 5%
where the time goes in v6:
time: 209 us; the launch traced here: 208 us
  waiting for transfers between devices  91.2 us (44%)
  starting transfers between devices  88.9 us (43%)
  Pallas kernels  19.3 us (9%)
  local copies, waits for them, and re-layouts  7.8 us (4%)
    ppermute x14, starting transfers between devices, take(): return lax.ppermute(value, AXES, table)  56.5 us
    ppermute x16, waiting for transfers between devices, butterfly(): other = lax.ppermute(value, AXES, table)  51.4 us
    ppermute x14, waiting for transfers between devices, take(): return lax.ppermute(value, AXES, table)  31.1 us
    ppermute x16, starting transfers between devices, butterfly(): other = lax.ppermute(value, AXES, table)  24.7 us
    pallas_call x8, Pallas kernels, call(): pl.pallas_call(body, out_shape=outs, in_specs=[pl.BlockSpec(memory_space=...  19.3 us
    ppermute x1, waiting for transfers between devices, shards(): rho_f = lax.ppermute(rho_a, AXES, table)  8.73 us
    ppermute x1, starting transfers between devices, shards(): rho_f = lax.ppermute(rho_a, AXES, table)  7.75 us
    unnamed x25, local copies, waits for them, and re-layouts  6.53 us
  transfers between devices with their start and end apart: 31, of which 21 were waited for; matrix products, arithmetic and copies ran while one was open for 1% of the time, Pallas kernels for 5%

profile of v6, /device:TPU:24, one launch (start us, length us, event | category | flops | bytes accessed | tf_op | source)
XLA Modules:
  0.0 208.2 jit_solution(14378098583644265968)
XLA Ops:
  0.7 7.7 %collective-permute-start = (bf16[64,8192]{1,0:T(8,128)(2,1)}, bf16[64,8192]{1,0:T(8,128)(2,1)S(1)}, u32[]{:S(2)}, u32[]{:S(2)}) collective-permute-start(bf16[64,8192]{1,0:T(8,128)(2,1)} %bitcast.27), channel_id=1, source_target_pairs={{1,0},{18,1},{3,2},{20,3},{5,4},{22,5},{7,6},{24,7},{9,8},{26,9},{... | collective-permute-start | bytes 3145736 | tf_op jit(solution)/shard_map/ppermute | solution.py:355
  9.7 2.9 %collective-permute-start.3 = (bf16[64,4096]{1,0:T(8,128)(2,1)S(1)}, bf16[64,4096]{1,0:T(8,128)(2,1)}, u32[]{:S(2)}, u32[]{:S(2)}) collective-permute-start(bf16[64,4096]{1,0:T(8,128)(2,1)S(1)} %get-tuple-element.58), channel_id=1, source_target_pairs={{16,0},{17,1},{18,2},{19,3},{20,4},{21,5},{22,6},{23,7},{24,8},{25... | collective-permute-start | bytes 1572872 | tf_op jit(solution)/shard_map/ppermute | solution.py:320
  13.6 8.7 %collective-permute-done.rho.rho_f = bf16[64,8192]{1,0:T(8,128)(2,1)S(1)} collective-permute-done((bf16[64,8192]{1,0:T(8,128)(2,1)}, bf16[64,8192]{1,0:T(8,128)(2,1)S(1)}, u32[]{:S(2)}, u32[]{:S(2)}) %collective-permute-start) | collective-permute-done | bytes 1048608 | tf_op jit(solution)/shard_map/ppermute | solution.py:355
  25.8 23.4 %collective-permute-start.6 = (bf16[64,640]{1,0:T(8,128)(2,1)}, bf16[64,640]{1,0:T(8,128)(2,1)S(1)}, u32[]{:S(2)}, u32[]{:S(2)}) collective-permute-start(bf16[64,640]{1,0:T(8,128)(2,1)} %get-tuple-element.35), channel_id=1, source_target_pairs={{16,0},{17,1},{18,2},{19,3},{20,4},{21,5},{22,6},{23,7},{24,8},{25... | collective-permute-start | bytes 245768 | tf_op jit(solution)/shard_map/ppermute | solution.py:320
  49.2 20.1 %collective-permute-start.7 = (bf16[64,640]{1,0:T(8,128)(2,1)}, bf16[64,640]{1,0:T(8,128)(2,1)S(1)}, u32[]{:S(2)}, u32[]{:S(2)}) collective-permute-start(bf16[64,640]{1,0:T(8,128)(2,1)} %get-tuple-element.40), channel_id=1, source_target_pairs={{1,0},{2,1},{3,2},{4,3},{5,4},{6,5},{7,6},{8,7},{9,8},{10,9},{11,1... | collective-permute-start | bytes 245768 | tf_op jit(solution)/shard_map/ppermute | solution.py:320
  74.7 2.9 %shard_map.103 = (bf16[512,1024]{1,0:T(8,128)(2,1)S(1)}, bf16[512,1024]{1,0:T(8,128)(2,1)S(1)}, bf16[512,512]{1,0:T(8,128)(2,1)S(1)}) custom-call(bf16[64,8192]{1,0:T(8,128)(2,1)S(1)} %bitcast.29, bf16[1024,1024]{1,0:T(8,128)(2,1)S(1)} %copy-done.6, f32[64,128]{1,0:T(8,128)S(1)} %get-tuple-element.31.own), custom_call_target="tpu_custom_call" | custom-call | flops 2684354560 | bytes 5242880 | tf_op jit(solution)/shard_map/pallas_call | solution.py:23
  82.1 4.6 %shard_map.104 = (bf16[512,1024]{1,0:T(8,128)(2,1)S(1)}, bf16[512,1024]{1,0:T(8,128)(2,1)S(1)}, bf16[2,512,512]{2,1,0:T(8,128)(2,1)S(1)}) custom-call(bf16[64,8192]{1,0:T(8,128)(2,1)S(1)} %bitcast.30, bf16[64,4096]{1,0:T(8,128)(2,1)} %collective-permute-done.1.low, bf16[64,4096]{1,0:T(8,128)(2,1)} %collective-permute-done.3.high, ...), custom_call_target="tpu_custom_call" | custom-call | flops 3221225472 | bytes 8388608 | tf_op jit(solution)/shard_map/pallas_call | solution.py:23
  88.1 5.3 %shard_map.106 = (bf16[4,512,512]{2,1,0:T(8,128)(2,1)S(1)}, f32[64,256]{1,0:T(8,128)S(1)}, f32[64,256]{1,0:T(8,128)S(1)}, f32[2,64,256]{2,1,0:T(8,128)S(1)}, f32[2,256]{1,0:T(2,128)S(1)}) custom-call(s32[1,1]{1,0:T(1,128)} %bitcast.core, bf16[64,8192]{1,0:T(8,128)(2,1)S(1)} %collective-permute-done.rho.rho_f, ...), custom_call_target="tpu_custom_call" | custom-call | flops 2147483648 | bytes 9437184 | tf_op jit(solution)/shard_map/pallas_call | solution.py:23
  95.4 8.6 %collective-permute-done.9 = f32[2,64,256]{2,1,0:T(8,128)S(1)} collective-permute-done((f32[2,64,256]{2,1,0:T(8,128)S(1)}, f32[2,64,256]{2,1,0:T(8,128)S(1)}, u32[]{:S(2)}, u32[]{:S(2)}) %collective-permute-start.9) | collective-permute-done | bytes 131104 | tf_op jit(solution)/shard_map/ppermute | solution.py:320
  105.3 5.7 %collective-permute-done.10 = f32[64,256]{1,0:T(8,128)S(1)} collective-permute-done((f32[64,256]{1,0:T(8,128)S(1)}, f32[64,256]{1,0:T(8,128)S(1)}, u32[]{:S(2)}, u32[]{:S(2)}) %collective-permute-start.10) | collective-permute-done | bytes 65568 | tf_op jit(solution)/shard_map/ppermute | solution.py:320
  111.5 6.3 %collective-permute-done.27.sig_r = f32[64,256]{1,0:T(8,128)S(1)} collective-permute-done((f32[64,256]{1,0:T(8,128)S(1)}, f32[64,256]{1,0:T(8,128)S(1)}, u32[]{:S(2)}, u32[]{:S(2)}) %collective-permute-start.27) | collective-permute-done | bytes 65568 | tf_op jit(solution)/shard_map/ppermute | solution.py:320
  117.9 14.6 %collective-permute-start.11 = (f32[2,256]{1,0:T(2,128)S(1)}, f32[2,256]{1,0:T(2,128)S(1)}, u32[]{:S(2)}, u32[]{:S(2)}) collective-permute-start(f32[2,256]{1,0:T(2,128)S(1)} %get-tuple-element.47), channel_id=1, source_target_pairs={{48,0},{49,1},{50,2},{51,3},{52,4},{53,5},{54,6},{55,7},{56,8},{57... | collective-permute-start | bytes 6152 | tf_op jit(solution)/shard_map/ppermute | solution.py:347
  137.5 3.8 %collective-permute-done.13 = f32[2,256]{1,0:T(2,128)S(1)} collective-permute-done((f32[2,256]{1,0:T(2,128)S(1)}, f32[2,256]{1,0:T(2,128)S(1)}, u32[]{:S(2)}, u32[]{:S(2)}) %collective-permute-start.13) | collective-permute-done | bytes 2080 | tf_op jit(solution)/shard_map/ppermute | solution.py:347
  141.3 3.6 %collective-permute-done.14 = f32[2,256]{1,0:T(2,128)S(1)} collective-permute-done((f32[2,256]{1,0:T(2,128)S(1)}, f32[2,256]{1,0:T(2,128)S(1)}, u32[]{:S(2)}, u32[]{:S(2)}) %collective-permute-start.14) | collective-permute-done | bytes 2080 | tf_op jit(solution)/shard_map/ppermute | solution.py:347
  144.9 3.6 %collective-permute-done.15 = f32[2,256]{1,0:T(2,128)S(1)} collective-permute-done((f32[2,256]{1,0:T(2,128)S(1)}, f32[2,256]{1,0:T(2,128)S(1)}, u32[]{:S(2)}, u32[]{:S(2)}) %collective-permute-start.15) | collective-permute-done | bytes 2080 | tf_op jit(solution)/shard_map/ppermute | solution.py:347
  148.5 4.8 %collective-permute-done.16 = f32[2,256]{1,0:T(2,128)S(1)} collective-permute-done((f32[2,256]{1,0:T(2,128)S(1)}, f32[2,256]{1,0:T(2,128)S(1)}, u32[]{:S(2)}, u32[]{:S(2)}) %collective-permute-start.16) | collective-permute-done | bytes 2080 | tf_op jit(solution)/shard_map/ppermute | solution.py:347
  153.3 3.6 %collective-permute-done.17 = f32[2,256]{1,0:T(2,128)S(1)} collective-permute-done((f32[2,256]{1,0:T(2,128)S(1)}, f32[2,256]{1,0:T(2,128)S(1)}, u32[]{:S(2)}, u32[]{:S(2)}) %collective-permute-start.17) | collective-permute-done | bytes 2080 | tf_op jit(solution)/shard_map/ppermute | solution.py:347
  158.2 3.5 %collective-permute-done.18.rest = f32[2,256]{1,0:T(2,128)S(1)} collective-permute-done((f32[2,256]{1,0:T(2,128)S(1)}, f32[2,256]{1,0:T(2,128)S(1)}, u32[]{:S(2)}, u32[]{:S(2)}) %collective-permute-start.18) | collective-permute-done | bytes 2080 | tf_op jit(solution)/shard_map/ppermute | solution.py:347
  164.4 10.5 %collective-permute-done.29.below = f32[2,64,256]{2,1,0:T(8,128)S(1)} collective-permute-done((f32[2,64,256]{2,1,0:T(8,128)S(1)}, f32[2,64,256]{2,1,0:T(8,128)S(1)}, u32[]{:S(2)}, u32[]{:S(2)}) %collective-permute-start.29) | collective-permute-done | bytes 131104 | tf_op jit(solution)/shard_map/ppermute | solution.py:320
  175.1 3.6 %collective-permute-done.19 = f32[1,256]{1,0:T(1,128)S(1)} collective-permute-done((f32[1,256]{1,0:T(1,128)S(1)}, f32[1,256]{1,0:T(1,128)S(1)}, u32[]{:S(2)}, u32[]{:S(2)}) %collective-permute-start.19) | collective-permute-done | bytes 1056 | tf_op jit(solution)/shard_map/ppermute | solution.py:347
  178.7 4.4 %collective-permute-start.20 = (f32[1,256]{1,0:T(1,128)S(1)}, f32[1,256]{1,0:T(1,128)S(1)}, u32[]{:S(2)}, u32[]{:S(2)}) collective-permute-start(f32[1,256]{1,0:T(1,128)S(1)} %add.69), channel_id=1, source_target_pairs={{48,0},{49,1},{50,2},{51,3},{52,4},{53,5},{54,6},{55,7},{56,8},{57... | collective-permute-start | bytes 3080 | tf_op jit(solution)/shard_map/ppermute | solution.py:347
  186.8 3.8 %collective-permute-done.22 = f32[1,256]{1,0:T(1,128)S(1)} collective-permute-done((f32[1,256]{1,0:T(1,128)S(1)}, f32[1,256]{1,0:T(1,128)S(1)}, u32[]{:S(2)}, u32[]{:S(2)}) %collective-permute-start.22) | collective-permute-done | bytes 1056 | tf_op jit(solution)/shard_map/ppermute | solution.py:347
  194.2 4.8 %collective-permute-done.24 = f32[1,256]{1,0:T(1,128)S(1)} collective-permute-done((f32[1,256]{1,0:T(1,128)S(1)}, f32[1,256]{1,0:T(1,128)S(1)}, u32[]{:S(2)}, u32[]{:S(2)}) %collective-permute-start.24) | collective-permute-done | bytes 1056 | tf_op jit(solution)/shard_map/ppermute | solution.py:347
  203.2 4.1 %collective-permute-done.26.rest = f32[1,256]{1,0:T(1,128)S(1)} collective-permute-done((f32[1,256]{1,0:T(1,128)S(1)}, f32[1,256]{1,0:T(1,128)S(1)}, u32[]{:S(2)}, u32[]{:S(2)}) %collective-permute-start.26) | collective-permute-done | bytes 1056 | tf_op jit(solution)/shard_map/ppermute | solution.py:347
  (90 shorter events, 42.4 us)
Async XLA Ops:
  0.7 21.6 %collective-permute-start = (bf16[64,8192]{1,0:T(8,128)(2,1)}, bf16[64,8192]{1,0:T(8,128)(2,1)S(1)}, u32[]{:S(2)}, u32[]{:S(2)}) collective-permute-start(bf16[64,8192]{1,0:T(8,128)(2,1)} %bitcast.27), channel_id=1, source_target_pairs={{1,0},{18,1},{3,2},{20,3},{5,4},{22,5},{7,6},{24,7},{9,8},{26,9},{... | collective-permute-start | bytes 3145736 | tf_op jit(solution)/shard_map/ppermute | solution.py:355
  9.7 59.6 %collective-permute-start.3 = (bf16[64,4096]{1,0:T(8,128)(2,1)S(1)}, bf16[64,4096]{1,0:T(8,128)(2,1)}, u32[]{:S(2)}, u32[]{:S(2)}) collective-permute-start(bf16[64,4096]{1,0:T(8,128)(2,1)S(1)} %get-tuple-element.58), channel_id=1, source_target_pairs={{16,0},{17,1},{18,2},{19,3},{20,4},{21,5},{22,6},{23,7},{24,8},{25... | collective-permute-start | bytes 1572872 | tf_op jit(solution)/shard_map/ppermute | solution.py:320
  12.6 58.0 %collective-permute-start.1 = (bf16[64,4096]{1,0:T(8,128)(2,1)S(1)}, bf16[64,4096]{1,0:T(8,128)(2,1)}, u32[]{:S(2)}, u32[]{:S(2)}) collective-permute-start(bf16[64,4096]{1,0:T(8,128)(2,1)S(1)} %get-tuple-element.59), channel_id=1, source_target_pairs={{16,0},{17,1},{18,2},{19,3},{20,4},{21,5},{22,6},{23,7},{24,8},{25... | collective-permute-start | bytes 1572872 | tf_op jit(solution)/shard_map/ppermute | solution.py:320
  22.3 65.8 %collective-permute-start.5 = (bf16[64,8192]{1,0:T(8,128)(2,1)S(1)}, bf16[64,8192]{1,0:T(8,128)(2,1)}, u32[]{:S(2)}, u32[]{:S(2)}) collective-permute-start(bf16[64,8192]{1,0:T(8,128)(2,1)S(1)} %collective-permute-done.rho.rho_f), channel_id=1, source_target_pairs={{241,1},{243,3},{245,5},{247,7},{249,9},{251,11},{253,13},{255,15}... | collective-permute-start | bytes 3145736 | tf_op jit(solution)/shard_map/ppermute | solution.py:320
  25.8 52.6 %collective-permute-start.6 = (bf16[64,640]{1,0:T(8,128)(2,1)}, bf16[64,640]{1,0:T(8,128)(2,1)S(1)}, u32[]{:S(2)}, u32[]{:S(2)}) collective-permute-start(bf16[64,640]{1,0:T(8,128)(2,1)} %get-tuple-element.35), channel_id=1, source_target_pairs={{16,0},{17,1},{18,2},{19,3},{20,4},{21,5},{22,6},{23,7},{24,8},{25... | collective-permute-start | bytes 245768 | tf_op jit(solution)/shard_map/ppermute | solution.py:320
  49.2 37.5 %collective-permute-start.7 = (bf16[64,640]{1,0:T(8,128)(2,1)}, bf16[64,640]{1,0:T(8,128)(2,1)S(1)}, u32[]{:S(2)}, u32[]{:S(2)}) collective-permute-start(bf16[64,640]{1,0:T(8,128)(2,1)} %get-tuple-element.40), channel_id=1, source_target_pairs={{1,0},{2,1},{3,2},{4,3},{5,4},{6,5},{7,6},{8,7},{9,8},{10,9},{11,1... | collective-permute-start | bytes 245768 | tf_op jit(solution)/shard_map/ppermute | solution.py:320
  69.3 18.7 %collective-permute-start.4 = (bf16[64,4096]{1,0:T(8,128)(2,1)}, bf16[64,4096]{1,0:T(8,128)(2,1)}, u32[]{:S(2)}, u32[]{:S(2)}) collective-permute-start(bf16[64,4096]{1,0:T(8,128)(2,1)} %collective-permute-done.3.high), channel_id=1, source_target_pairs={{1,0},{3,2},{5,4},{7,6},{9,8},{11,10},{13,12},{15,14},{17,16},{19,... | collective-permute-start | bytes 1572872 | tf_op jit(solution)/shard_map/ppermute | solution.py:320
  70.6 17.4 %collective-permute-start.2 = (bf16[64,4096]{1,0:T(8,128)(2,1)}, bf16[64,4096]{1,0:T(8,128)(2,1)}, u32[]{:S(2)}, u32[]{:S(2)}) collective-permute-start(bf16[64,4096]{1,0:T(8,128)(2,1)} %collective-permute-done.1.low), channel_id=1, source_target_pairs={{1,0},{3,2},{5,4},{7,6},{9,8},{11,10},{13,12},{15,14},{17,16},{19,... | collective-permute-start | bytes 1572872 | tf_op jit(solution)/shard_map/ppermute | solution.py:320
  78.4 8.3 %collective-permute-start.8 = (bf16[64,640]{1,0:T(8,128)(2,1)S(1)}, bf16[64,640]{1,0:T(8,128)(2,1)S(1)}, u32[]{:S(2)}, u32[]{:S(2)}) collective-permute-start(bf16[64,640]{1,0:T(8,128)(2,1)S(1)} %get-tuple-element.41), channel_id=1, source_target_pairs={{17,0},{18,1},{19,2},{20,3},{21,4},{22,5},{23,6},{24,7},{25,8},{26... | collective-permute-start | bytes 245768 | tf_op jit(solution)/shard_map/ppermute | solution.py:320
  93.4 10.5 %collective-permute-start.9 = (f32[2,64,256]{2,1,0:T(8,128)S(1)}, f32[2,64,256]{2,1,0:T(8,128)S(1)}, u32[]{:S(2)}, u32[]{:S(2)}) collective-permute-start(f32[2,64,256]{2,1,0:T(8,128)S(1)} %get-tuple-element.45), channel_id=1, source_target_pairs={{15,0},{0,1},{1,2},{2,3},{3,4},{4,5},{5,6},{6,7},{7,8},{8,9},{9,10... | collective-permute-start | bytes 393224 | tf_op jit(solution)/shard_map/ppermute | solution.py:320
  103.9 7.0 %collective-permute-start.10 = (f32[64,256]{1,0:T(8,128)S(1)}, f32[64,256]{1,0:T(8,128)S(1)}, u32[]{:S(2)}, u32[]{:S(2)}) collective-permute-start(f32[64,256]{1,0:T(8,128)S(1)} %fusion.1), channel_id=1, source_target_pairs={{240,0},{241,1},{242,2},{243,3},{244,4},{245,5},{246,6},{247,7},{2... | collective-permute-start | bytes 196616 | tf_op jit(solution)/shard_map/ppermute | solution.py:320
  111.0 6.8 %collective-permute-start.27 = (f32[64,256]{1,0:T(8,128)S(1)}, f32[64,256]{1,0:T(8,128)S(1)}, u32[]{:S(2)}, u32[]{:S(2)}) collective-permute-start(f32[64,256]{1,0:T(8,128)S(1)} %fusion.3.sigma), channel_id=1, source_target_pairs={{16,0},{17,1},{18,2},{19,3},{20,4},{21,5},{22,6},{23,7},{24,8},{25... | collective-permute-start | bytes 196616 | tf_op jit(solution)/shard_map/ppermute | solution.py:320
  117.8 44.6 %collective-permute-start.28 = (f32[2,64,256]{2,1,0:T(8,128)S(1)}, f32[2,64,256]{2,1,0:T(8,128)S(1)}, u32[]{:S(2)}, u32[]{:S(2)}) collective-permute-start(f32[2,64,256]{2,1,0:T(8,128)S(1)} %pad_maximum_fusion), channel_id=1, source_target_pairs={{1,0},{2,1},{3,2},{4,3},{5,4},{6,5},{7,6},{8,7},{9,8},{10,9},{11,1... | collective-permute-start | bytes 393224 | tf_op jit(solution)/shard_map/ppermute | solution.py:320
  117.9 17.5 %collective-permute-start.11 = (f32[2,256]{1,0:T(2,128)S(1)}, f32[2,256]{1,0:T(2,128)S(1)}, u32[]{:S(2)}, u32[]{:S(2)}) collective-permute-start(f32[2,256]{1,0:T(2,128)S(1)} %get-tuple-element.47), channel_id=1, source_target_pairs={{48,0},{49,1},{50,2},{51,3},{52,4},{53,5},{54,6},{55,7},{56,8},{57... | collective-permute-start | bytes 6152 | tf_op jit(solution)/shard_map/ppermute | solution.py:347
  136.5 4.8 %collective-permute-start.13 = (f32[2,256]{1,0:T(2,128)S(1)}, f32[2,256]{1,0:T(2,128)S(1)}, u32[]{:S(2)}, u32[]{:S(2)}) collective-permute-start(f32[2,256]{1,0:T(2,128)S(1)} %add.63), channel_id=1, source_target_pairs={{50,0},{51,1},{48,2},{49,3},{54,4},{55,5},{52,6},{53,7},{58,8},{59... | collective-permute-start | bytes 6152 | tf_op jit(solution)/shard_map/ppermute | solution.py:347
  148.5 4.8 %collective-permute-start.16 = (f32[2,256]{1,0:T(2,128)S(1)}, f32[2,256]{1,0:T(2,128)S(1)}, u32[]{:S(2)}, u32[]{:S(2)}) collective-permute-start(f32[2,256]{1,0:T(2,128)S(1)} %add.66), channel_id=1, source_target_pairs={{12,0},{13,1},{14,2},{15,3},{8,4},{9,5},{10,6},{11,7},{4,8},{5,9},... | collective-permute-start | bytes 6152 | tf_op jit(solution)/shard_map/ppermute | solution.py:347
  156.9 4.8 %collective-permute-start.18 = (f32[2,256]{1,0:T(2,128)S(1)}, f32[2,256]{1,0:T(2,128)S(1)}, u32[]{:S(2)}, u32[]{:S(2)}) collective-permute-start(f32[2,256]{1,0:T(2,128)S(1)} %add.68.part), channel_id=1, source_target_pairs={{192,0},{193,1},{194,2},{195,3},{196,4},{197,5},{198,6},{199,7},{2... | collective-permute-start | bytes 6152 | tf_op jit(solution)/shard_map/ppermute | solution.py:347
  164.3 10.6 %collective-permute-start.29 = (f32[2,64,256]{2,1,0:T(8,128)S(1)}, f32[2,64,256]{2,1,0:T(8,128)S(1)}, u32[]{:S(2)}, u32[]{:S(2)}) collective-permute-start(f32[2,64,256]{2,1,0:T(8,128)S(1)} %get-tuple-element.53), channel_id=1, source_target_pairs={{15,0},{0,1},{1,2},{2,3},{3,4},{4,5},{5,6},{6,7},{7,8},{8,9},{9,10... | collective-permute-start | bytes 393224 | tf_op jit(solution)/shard_map/ppermute | solution.py:320
  174.9 32.4 %collective-permute-start.30 = (f32[64,256]{1,0:T(8,128)S(1)}, f32[64,256]{1,0:T(8,128)S(1)}, u32[]{:S(2)}, u32[]{:S(2)}) collective-permute-start(f32[64,256]{1,0:T(8,128)S(1)} %fusion), channel_id=1, source_target_pairs={{240,0},{241,1},{242,2},{243,3},{244,4},{245,5},{246,6},{247,7},{2... | collective-permute-start | bytes 196616 | tf_op jit(solution)/shard_map/ppermute | solution.py:320
  175.0 3.7 %collective-permute-start.19 = (f32[1,256]{1,0:T(1,128)S(1)}, f32[1,256]{1,0:T(1,128)S(1)}, u32[]{:S(2)}, u32[]{:S(2)}) collective-permute-start(f32[1,256]{1,0:T(1,128)S(1)} %get-tuple-element.48), channel_id=1, source_target_pairs={{4,0},{5,1},{6,2},{7,3},{0,4},{1,5},{2,6},{3,7},{12,8},{13,9},{14,... | collective-permute-start | bytes 3080 | tf_op jit(solution)/shard_map/ppermute | solution.py:347
  178.7 6.0 %collective-permute-start.20 = (f32[1,256]{1,0:T(1,128)S(1)}, f32[1,256]{1,0:T(1,128)S(1)}, u32[]{:S(2)}, u32[]{:S(2)}) collective-permute-start(f32[1,256]{1,0:T(1,128)S(1)} %add.69), channel_id=1, source_target_pairs={{48,0},{49,1},{50,2},{51,3},{52,4},{53,5},{54,6},{55,7},{56,8},{57... | collective-permute-start | bytes 3080 | tf_op jit(solution)/shard_map/ppermute | solution.py:347
  185.8 4.8 %collective-permute-start.22 = (f32[1,256]{1,0:T(1,128)S(1)}, f32[1,256]{1,0:T(1,128)S(1)}, u32[]{:S(2)}, u32[]{:S(2)}) collective-permute-start(f32[1,256]{1,0:T(1,128)S(1)} %add.71), channel_id=1, source_target_pairs={{50,0},{51,1},{48,2},{49,3},{54,4},{55,5},{52,6},{53,7},{58,8},{59... | collective-permute-start | bytes 3080 | tf_op jit(solution)/shard_map/ppermute | solution.py:347
  194.2 4.8 %collective-permute-start.24 = (f32[1,256]{1,0:T(1,128)S(1)}, f32[1,256]{1,0:T(1,128)S(1)}, u32[]{:S(2)}, u32[]{:S(2)}) collective-permute-start(f32[1,256]{1,0:T(1,128)S(1)} %add.73), channel_id=1, source_target_pairs={{12,0},{13,1},{14,2},{15,3},{8,4},{9,5},{10,6},{11,7},{4,8},{5,9},... | collective-permute-start | bytes 3080 | tf_op jit(solution)/shard_map/ppermute | solution.py:347
  202.6 4.8 %collective-permute-start.26 = (f32[1,256]{1,0:T(1,128)S(1)}, f32[1,256]{1,0:T(1,128)S(1)}, u32[]{:S(2)}, u32[]{:S(2)}) collective-permute-start(f32[1,256]{1,0:T(1,128)S(1)} %add.75.part), channel_id=1, source_target_pairs={{192,0},{193,1},{194,2},{195,3},{196,4},{197,5},{198,6},{199,7},{2... | collective-permute-start | bytes 3080 | tf_op jit(solution)/shard_map/ppermute | solution.py:347
  (19 other events, 198.4 us)

commit v7 on v6

--- a/solution.py
+++ b/solution.py
@@ -142,9 +142,9 @@
     return parts
 
 
-def first_body(states, core, rho, proj, back, own_u, own_c, msg_u, msg_c, c):
-    mols = rho.shape[0]
-    rows = stack(rho, states)
+def first_body(states, core, low, high, proj, back, own_u, own_c, msg_u, msg_c, c):
+    mols = low.shape[0]
+    rows = stack_two(low, high, states)
     c[0] = couple(proj[...], rows, choose(core, own_u[...], own_c[...]))
     pair = choose(core, note_weights(msg_u, mols, 0), note_weights(msg_c, mols, 0))
     c[1] = couple(rows, back[...], twice(pair))
@@ -177,10 +177,12 @@
 def corner_body(
     states,
     core,
-    rho_f,
+    first_low,
+    first_high,
     near_low,
     near_high,
-    shifted,
+    shift_low,
+    shift_high,
     proj_a,
     back_a,
     proj_r,
@@ -203,14 +205,15 @@
     rows,
 ):
     mols, field = y_a.shape
-    width = rho_f.shape[1] // states
+    width = first_low.shape[1] * 2 // states
+    halves = ((first_low, near_low, shift_low), (first_high, near_high, shift_high))
     for a in range(states):
-        near = (near_low, near_high)[a * 2 // states]
+        first, near, shifted = halves[a * 2 // states]
         b = a % (states // 2)
-        lanes = slice(a * width, (a + 1) * width)
+        lanes = slice(b * width, (b + 1) * width)
         place = slice(a * mols, (a + 1) * mols)
-        rows[0, place] = rho_f[:, lanes]
-        rows[1, place] = choose(core, near[:, b * width : (b + 1) * width], shifted[:, lanes])
+        rows[0, place] = first[:, lanes]
+        rows[1, place] = choose(core, near[:, lanes], shifted[:, lanes])
     upper = rows.at[core[0, 0]]
     last = rows[1]
     c[0] = couple(proj_a[...], last, choose(core, own_c[...], own_u[...]))
@@ -352,7 +355,9 @@
     rho_a, y_a, e_a = densities[0, 0], trials[0, 0], energies[0, 0]
     core = (lax.axis_index("gy") % 2).astype(jnp.int32).reshape(1, 1)
     table = [(spot(x + y % 2, y + 1), spot(x, y)) for x in range(nx) for y in range(ny)]
-    rho_f = lax.ppermute(rho_a, AXES, table)
+    half = rho_a.shape[1] // 2
+    first_low = lax.ppermute(rho_a[:, :half], AXES, table)
+    first_high = lax.ppermute(rho_a[:, half:], AXES, table)
 
     pair = shape(mols, 2 * mols)
     note = shape(mols, field + 6 * mols, dtype=BF)
@@ -366,11 +371,11 @@
     msg_u = take(msg_u, 0, 1)
     msg_c = take(msg_c, 1, 1)
 
-    half = rho_a.shape[1] // 2
     even, odd = (lambda x, y: y % 2 == 0), (lambda x, y: y % 2 == 1)
     right_low = take(rho_a[:, :half], 1, 0)
     right_high = take(rho_a[:, half:], 1, 0)
-    shifted = take(rho_f, -1, 0, odd)
+    shift_low = take(first_low, -1, 0, odd)
+    shift_high = take(first_high, -1, 0, odd)
     near_low = take(right_low, 0, 1, even)
     near_high = take(right_high, 0, 1, even)
 
@@ -383,7 +388,7 @@
         functools.partial(self_body, states), (wide, wide, square), 2 * proj + block, 5 * size
     )(rho_a, metric, own_a)
     c_f = call(functools.partial(first_body, states), squares_of(2), 2 * block, 4 * size, 1)(
-        core, rho_f, proj_a, back_a, own_u, own_c, msg_u, msg_c
+        core, first_low, first_high, proj_a, back_a, own_u, own_c, msg_u, msg_c
     )
     proj_r, back_r, c_r = call(
         functools.partial(right_body, states),
@@ -401,10 +406,12 @@
         [pltpu.VMEM((2, width, aux), BF)],
     )(
         core,
-        rho_f,
+        first_low,
+        first_high,
         near_low,
         near_high,
-        shifted,
+        shift_low,
+        shift_high,
         proj_a,
         back_a,
         proj_r,

time: 209 us -> 198 us (0.947)
  starting transfers between devices: 88.9 us -> 56.5 us
  waiting for transfers between devices: 91.2 us -> 115 us
  local copies, waits for them, and re-layouts: 7.8 us -> 4.23 us
    ppermute x14 -> x15, waiting for transfers between devices: 31.1 us -> 67.2 us  [take(): return lax.ppermute(value, AXES, table)]
    ppermute x14 -> x15, starting transfers between devices: 56.5 us -> 32.5 us  [take(): return lax.ppermute(value, AXES, table)]
    ppermute x1 -> x2, waiting for transfers between devices: 8.73 us -> 0.01 us  [the longest x1 0.01 us: shards(): first_high = lax.ppermute(rho_a[:, half:], AXES, table)]
    ppermute x16, starting transfers between devices: 24.7 us -> 20.4 us  [butterfly(): other = lax.ppermute(value, AXES, table)]
    ppermute x1 -> x2, starting transfers between devices: 7.75 us -> 3.6 us  [the longest x1 3.59 us: shards(): first_high = lax.ppermute(rho_a[:, half:], AXES, table)]
    unnamed x25 -> x21, local copies, waits for them, and re-layouts: 6.53 us -> 2.93 us
    ppermute x16, waiting for transfers between devices: 51.4 us -> 48.2 us  [butterfly(): other = lax.ppermute(value, AXES, table)]
  transfers between devices with their start and end apart: 31 -> 33, of which waited for: 21 -> 22; matrix products, arithmetic and copies ran while one was open for 1% -> 0% of each run, Pallas kernels for 5% -> 6%
where the time goes in v7:
time: 198 us
  waiting for transfers between devices  115 us (58%)
  starting transfers between devices  56.5 us (29%)
  Pallas kernels  20.6 us (10%)
  local copies, waits for them, and re-layouts  4.23 us (2%)
    ppermute x15, waiting for transfers between devices, take(): return lax.ppermute(value, AXES, table)  67.2 us
    ppermute x16, waiting for transfers between devices, butterfly(): other = lax.ppermute(value, AXES, table)  48.2 us
    ppermute x15, starting transfers between devices, take(): return lax.ppermute(value, AXES, table)  32.5 us
    pallas_call x8, Pallas kernels, call(): pl.pallas_call(body, out_shape=outs, in_specs=[pl.BlockSpec(memory_space=...  20.6 us
    ppermute x16, starting transfers between devices, butterfly(): other = lax.ppermute(value, AXES, table)  20.4 us
  transfers between devices with their start and end apart: 33, of which 22 were waited for; matrix products, arithmetic and copies ran while one was open for 0% of the time, Pallas kernels for 6%

profile of v7, /device:TPU:24, one launch (start us, length us, event | category | flops | bytes accessed | tf_op | source)
XLA Modules:
  0.0 197.8 jit_solution(2044215869725420802)
XLA Ops:
  2.0 4.9 %collective-permute-start.4 = (bf16[64,4096]{1,0:T(8,128)(2,1)S(1)}, bf16[64,4096]{1,0:T(8,128)(2,1)}, u32[]{:S(2)}, u32[]{:S(2)}) collective-permute-start(bf16[64,4096]{1,0:T(8,128)(2,1)S(1)} %get-tuple-element.58), channel_id=1, source_target_pairs={{16,0},{17,1},{18,2},{19,3},{20,4},{21,5},{22,6},{23,7},{24,8},{25... | collective-permute-start | bytes 1572872 | tf_op jit(solution)/shard_map/ppermute | solution.py:323
  6.9 3.6 %collective-permute-start.1 = (bf16[64,4096]{1,0:T(8,128)(2,1)S(1)}, bf16[64,4096]{1,0:T(8,128)(2,1)S(1)}, u32[]{:S(2)}, u32[]{:S(2)}) collective-permute-start(bf16[64,4096]{1,0:T(8,128)(2,1)S(1)} %get-tuple-element.58), channel_id=1, source_target_pairs={{1,0},{18,1},{3,2},{20,3},{5,4},{22,5},{7,6},{24,7},{9,8},{26,9},{... | collective-permute-start | bytes 1572872 | tf_op jit(solution)/shard_map/ppermute | solution.py:360
  16.5 38.7 %collective-permute-done.9.msg_u = bf16[64,640]{1,0:T(8,128)(2,1)S(1)} collective-permute-done((bf16[64,640]{1,0:T(8,128)(2,1)S(1)}, bf16[64,640]{1,0:T(8,128)(2,1)S(1)}, u32[]{:S(2)}, u32[]{:S(2)}) %collective-permute-start.9) | collective-permute-done | bytes 81952 | tf_op jit(solution)/shard_map/ppermute | solution.py:323
  63.6 2.9 %shard_map.103 = (bf16[512,1024]{1,0:T(8,128)(2,1)S(1)}, bf16[512,1024]{1,0:T(8,128)(2,1)S(1)}, bf16[512,512]{1,0:T(8,128)(2,1)S(1)}) custom-call(bf16[64,8192]{1,0:T(8,128)(2,1)S(1)} %bitcast.28, bf16[1024,1024]{1,0:T(8,128)(2,1)S(1)} %copy-done.4, f32[64,128]{1,0:T(8,128)S(1)} %get-tuple-element.31.own), custom_call_target="tpu_custom_call" | custom-call | flops 2684354560 | bytes 5242880 | tf_op jit(solution)/shard_map/pallas_call | solution.py:23
  66.5 6.2 %collective-permute-start.8 = (bf16[64,640]{1,0:T(8,128)(2,1)S(1)}, bf16[64,640]{1,0:T(8,128)(2,1)S(1)}, u32[]{:S(2)}, u32[]{:S(2)}) collective-permute-start(bf16[64,640]{1,0:T(8,128)(2,1)S(1)} %get-tuple-element.35), channel_id=1, source_target_pairs={{16,0},{17,1},{18,2},{19,3},{20,4},{21,5},{22,6},{23,7},{24,8},{25... | collective-permute-start | bytes 245768 | tf_op jit(solution)/shard_map/ppermute | solution.py:323
  77.9 4.6 %shard_map.104 = (bf16[512,1024]{1,0:T(8,128)(2,1)S(1)}, bf16[512,1024]{1,0:T(8,128)(2,1)S(1)}, bf16[2,512,512]{2,1,0:T(8,128)(2,1)S(1)}) custom-call(bf16[64,8192]{1,0:T(8,128)(2,1)S(1)} %bitcast.29, bf16[64,4096]{1,0:T(8,128)(2,1)} %collective-permute-done.2.low, bf16[64,4096]{1,0:T(8,128)(2,1)} %collective-permute-done.4.high, ...), custom_call_target="tpu_custom_call" | custom-call | flops 3221225472 | bytes 8388608 | tf_op jit(solution)/shard_map/pallas_call | solution.py:23
  82.6 5.5 %shard_map.106 = (bf16[4,512,512]{2,1,0:T(8,128)(2,1)S(1)}, f32[64,256]{1,0:T(8,128)S(1)}, f32[64,256]{1,0:T(8,128)S(1)}, f32[2,64,256]{2,1,0:T(8,128)S(1)}, f32[2,256]{1,0:T(2,128)S(1)}) custom-call(s32[1,1]{1,0:T(1,128)} %bitcast.core, bf16[64,4096]{1,0:T(8,128)(2,1)} %collective-permute-done.low.first_low, ...), custom_call_target="tpu_custom_call" | custom-call | flops 2147483648 | bytes 9437184 | tf_op jit(solution)/shard_map/pallas_call | solution.py:23
  88.0 9.1 %collective-permute-start.11 = (f32[2,64,256]{2,1,0:T(8,128)S(1)}, f32[2,64,256]{2,1,0:T(8,128)S(1)}, u32[]{:S(2)}, u32[]{:S(2)}) collective-permute-start(f32[2,64,256]{2,1,0:T(8,128)S(1)} %get-tuple-element.45), channel_id=1, source_target_pairs={{15,0},{0,1},{1,2},{2,3},{3,4},{4,5},{5,6},{6,7},{7,8},{8,9},{9,10... | collective-permute-start | bytes 393224 | tf_op jit(solution)/shard_map/ppermute | solution.py:323
  97.2 5.5 %collective-permute-done.11 = f32[2,64,256]{2,1,0:T(8,128)S(1)} collective-permute-done((f32[2,64,256]{2,1,0:T(8,128)S(1)}, f32[2,64,256]{2,1,0:T(8,128)S(1)}, u32[]{:S(2)}, u32[]{:S(2)}) %collective-permute-start.11) | collective-permute-done | bytes 131104 | tf_op jit(solution)/shard_map/ppermute | solution.py:323
  103.3 6.4 %collective-permute-done.12 = f32[64,256]{1,0:T(8,128)S(1)} collective-permute-done((f32[64,256]{1,0:T(8,128)S(1)}, f32[64,256]{1,0:T(8,128)S(1)}, u32[]{:S(2)}, u32[]{:S(2)}) %collective-permute-start.12) | collective-permute-done | bytes 65568 | tf_op jit(solution)/shard_map/ppermute | solution.py:323
  114.2 7.1 %collective-permute-start.13 = (f32[2,256]{1,0:T(2,128)S(1)}, f32[2,256]{1,0:T(2,128)S(1)}, u32[]{:S(2)}, u32[]{:S(2)}) collective-permute-start(f32[2,256]{1,0:T(2,128)S(1)} %get-tuple-element.47), channel_id=1, source_target_pairs={{48,0},{49,1},{50,2},{51,3},{52,4},{53,5},{54,6},{55,7},{56,8},{57... | collective-permute-start | bytes 6152 | tf_op jit(solution)/shard_map/ppermute | solution.py:350
  121.3 2.9 %collective-permute-done.13 = f32[2,256]{1,0:T(2,128)S(1)} collective-permute-done((f32[2,256]{1,0:T(2,128)S(1)}, f32[2,256]{1,0:T(2,128)S(1)}, u32[]{:S(2)}, u32[]{:S(2)}) %collective-permute-start.13) | collective-permute-done | bytes 2080 | tf_op jit(solution)/shard_map/ppermute | solution.py:350
  125.3 3.8 %collective-permute-start.15 = (f32[2,256]{1,0:T(2,128)S(1)}, f32[2,256]{1,0:T(2,128)S(1)}, u32[]{:S(2)}, u32[]{:S(2)}) collective-permute-start(f32[2,256]{1,0:T(2,128)S(1)} %add.63), channel_id=1, source_target_pairs={{50,0},{51,1},{48,2},{49,3},{54,4},{55,5},{52,6},{53,7},{58,8},{59... | collective-permute-start | bytes 6152 | tf_op jit(solution)/shard_map/ppermute | solution.py:350
  130.7 3.6 %collective-permute-done.16 = f32[2,256]{1,0:T(2,128)S(1)} collective-permute-done((f32[2,256]{1,0:T(2,128)S(1)}, f32[2,256]{1,0:T(2,128)S(1)}, u32[]{:S(2)}, u32[]{:S(2)}) %collective-permute-start.16) | collective-permute-done | bytes 2080 | tf_op jit(solution)/shard_map/ppermute | solution.py:350
  139.2 3.5 %collective-permute-done.18 = f32[2,256]{1,0:T(2,128)S(1)} collective-permute-done((f32[2,256]{1,0:T(2,128)S(1)}, f32[2,256]{1,0:T(2,128)S(1)}, u32[]{:S(2)}, u32[]{:S(2)}) %collective-permute-start.18) | collective-permute-done | bytes 2080 | tf_op jit(solution)/shard_map/ppermute | solution.py:350
  142.7 3.6 %collective-permute-done.19 = f32[2,256]{1,0:T(2,128)S(1)} collective-permute-done((f32[2,256]{1,0:T(2,128)S(1)}, f32[2,256]{1,0:T(2,128)S(1)}, u32[]{:S(2)}, u32[]{:S(2)}) %collective-permute-start.19) | collective-permute-done | bytes 2080 | tf_op jit(solution)/shard_map/ppermute | solution.py:350
  146.5 4.6 %collective-permute-done.20.rest = f32[2,256]{1,0:T(2,128)S(1)} collective-permute-done((f32[2,256]{1,0:T(2,128)S(1)}, f32[2,256]{1,0:T(2,128)S(1)}, u32[]{:S(2)}, u32[]{:S(2)}) %collective-permute-start.20) | collective-permute-done | bytes 2080 | tf_op jit(solution)/shard_map/ppermute | solution.py:350
  153.8 11.3 %collective-permute-done.31.below = f32[2,64,256]{2,1,0:T(8,128)S(1)} collective-permute-done((f32[2,64,256]{2,1,0:T(8,128)S(1)}, f32[2,64,256]{2,1,0:T(8,128)S(1)}, u32[]{:S(2)}, u32[]{:S(2)}) %collective-permute-start.31) | collective-permute-done | bytes 131104 | tf_op jit(solution)/shard_map/ppermute | solution.py:323
  165.3 3.6 %collective-permute-done.21 = f32[1,256]{1,0:T(1,128)S(1)} collective-permute-done((f32[1,256]{1,0:T(1,128)S(1)}, f32[1,256]{1,0:T(1,128)S(1)}, u32[]{:S(2)}, u32[]{:S(2)}) %collective-permute-start.21) | collective-permute-done | bytes 1056 | tf_op jit(solution)/shard_map/ppermute | solution.py:350
  168.9 3.3 %collective-permute-start.22 = (f32[1,256]{1,0:T(1,128)S(1)}, f32[1,256]{1,0:T(1,128)S(1)}, u32[]{:S(2)}, u32[]{:S(2)}) collective-permute-start(f32[1,256]{1,0:T(1,128)S(1)} %add.69), channel_id=1, source_target_pairs={{48,0},{49,1},{50,2},{51,3},{52,4},{53,5},{54,6},{55,7},{56,8},{57... | collective-permute-start | bytes 3080 | tf_op jit(solution)/shard_map/ppermute | solution.py:350
  176.8 3.4 %collective-permute-done.24 = f32[1,256]{1,0:T(1,128)S(1)} collective-permute-done((f32[1,256]{1,0:T(1,128)S(1)}, f32[1,256]{1,0:T(1,128)S(1)}, u32[]{:S(2)}, u32[]{:S(2)}) %collective-permute-start.24) | collective-permute-done | bytes 1056 | tf_op jit(solution)/shard_map/ppermute | solution.py:350
  180.4 3.4 %collective-permute-done.25 = f32[1,256]{1,0:T(1,128)S(1)} collective-permute-done((f32[1,256]{1,0:T(1,128)S(1)}, f32[1,256]{1,0:T(1,128)S(1)}, u32[]{:S(2)}, u32[]{:S(2)}) %collective-permute-start.25) | collective-permute-done | bytes 1056 | tf_op jit(solution)/shard_map/ppermute | solution.py:350
  184.3 4.2 %collective-permute-done.26 = f32[1,256]{1,0:T(1,128)S(1)} collective-permute-done((f32[1,256]{1,0:T(1,128)S(1)}, f32[1,256]{1,0:T(1,128)S(1)}, u32[]{:S(2)}, u32[]{:S(2)}) %collective-permute-start.26) | collective-permute-done | bytes 1056 | tf_op jit(solution)/shard_map/ppermute | solution.py:350
  192.3 4.6 %collective-permute-done.28.rest = f32[1,256]{1,0:T(1,128)S(1)} collective-permute-done((f32[1,256]{1,0:T(1,128)S(1)}, f32[1,256]{1,0:T(1,128)S(1)}, u32[]{:S(2)}, u32[]{:S(2)}) %collective-permute-start.28) | collective-permute-done | bytes 1056 | tf_op jit(solution)/shard_map/ppermute | solution.py:350
  (90 shorter events, 46.7 us)
Async XLA Ops:
  2.0 53.3 %collective-permute-start.4 = (bf16[64,4096]{1,0:T(8,128)(2,1)S(1)}, bf16[64,4096]{1,0:T(8,128)(2,1)}, u32[]{:S(2)}, u32[]{:S(2)}) collective-permute-start(bf16[64,4096]{1,0:T(8,128)(2,1)S(1)} %get-tuple-element.58), channel_id=1, source_target_pairs={{16,0},{17,1},{18,2},{19,3},{20,4},{21,5},{22,6},{23,7},{24,8},{25... | collective-permute-start | bytes 1572872 | tf_op jit(solution)/shard_map/ppermute | solution.py:323
  6.9 49.7 %collective-permute-start.1 = (bf16[64,4096]{1,0:T(8,128)(2,1)S(1)}, bf16[64,4096]{1,0:T(8,128)(2,1)S(1)}, u32[]{:S(2)}, u32[]{:S(2)}) collective-permute-start(bf16[64,4096]{1,0:T(8,128)(2,1)S(1)} %get-tuple-element.58), channel_id=1, source_target_pairs={{1,0},{18,1},{3,2},{20,3},{5,4},{22,5},{7,6},{24,7},{9,8},{26,9},{... | collective-permute-start | bytes 1572872 | tf_op jit(solution)/shard_map/ppermute | solution.py:360
  10.5 47.6 %collective-permute-start.2 = (bf16[64,4096]{1,0:T(8,128)(2,1)S(1)}, bf16[64,4096]{1,0:T(8,128)(2,1)}, u32[]{:S(2)}, u32[]{:S(2)}) collective-permute-start(bf16[64,4096]{1,0:T(8,128)(2,1)S(1)} %get-tuple-element.59), channel_id=1, source_target_pairs={{16,0},{17,1},{18,2},{19,3},{20,4},{21,5},{22,6},{23,7},{24,8},{25... | collective-permute-start | bytes 1572872 | tf_op jit(solution)/shard_map/ppermute | solution.py:323
  13.3 46.1 %collective-permute-start = (bf16[64,4096]{1,0:T(8,128)(2,1)S(1)}, bf16[64,4096]{1,0:T(8,128)(2,1)}, u32[]{:S(2)}, u32[]{:S(2)}) collective-permute-start(bf16[64,4096]{1,0:T(8,128)(2,1)S(1)} %get-tuple-element.59), channel_id=1, source_target_pairs={{1,0},{18,1},{3,2},{20,3},{5,4},{22,5},{7,6},{24,7},{9,8},{26,9},{... | collective-permute-start | bytes 1572872 | tf_op jit(solution)/shard_map/ppermute | solution.py:359
  15.1 40.1 %collective-permute-start.9 = (bf16[64,640]{1,0:T(8,128)(2,1)S(1)}, bf16[64,640]{1,0:T(8,128)(2,1)S(1)}, u32[]{:S(2)}, u32[]{:S(2)}) collective-permute-start(bf16[64,640]{1,0:T(8,128)(2,1)S(1)} %get-tuple-element.40), channel_id=1, source_target_pairs={{1,0},{2,1},{3,2},{4,3},{5,4},{6,5},{7,6},{8,7},{9,8},{10,9},{11,1... | collective-permute-start | bytes 245768 | tf_op jit(solution)/shard_map/ppermute | solution.py:323
  55.3 11.3 %collective-permute-start.10 = (bf16[64,640]{1,0:T(8,128)(2,1)}, bf16[64,640]{1,0:T(8,128)(2,1)S(1)}, u32[]{:S(2)}, u32[]{:S(2)}) collective-permute-start(bf16[64,640]{1,0:T(8,128)(2,1)} %get-tuple-element.41), channel_id=1, source_target_pairs={{17,0},{18,1},{19,2},{20,3},{21,4},{22,5},{23,6},{24,7},{25,8},{26... | collective-permute-start | bytes 245768 | tf_op jit(solution)/shard_map/ppermute | solution.py:323
  55.3 27.2 %collective-permute-start.5 = (bf16[64,4096]{1,0:T(8,128)(2,1)}, bf16[64,4096]{1,0:T(8,128)(2,1)}, u32[]{:S(2)}, u32[]{:S(2)}) collective-permute-start(bf16[64,4096]{1,0:T(8,128)(2,1)} %collective-permute-done.4.high), channel_id=1, source_target_pairs={{1,0},{3,2},{5,4},{7,6},{9,8},{11,10},{13,12},{15,14},{17,16},{19,... | collective-permute-start | bytes 1572872 | tf_op jit(solution)/shard_map/ppermute | solution.py:323
  56.6 26.0 %collective-permute-start.7 = (bf16[64,4096]{1,0:T(8,128)(2,1)S(1)}, bf16[64,4096]{1,0:T(8,128)(2,1)}, u32[]{:S(2)}, u32[]{:S(2)}) collective-permute-start(bf16[64,4096]{1,0:T(8,128)(2,1)S(1)} %collective-permute-done.1.high.first_high), channel_id=1, source_target_pairs={{241,1},{243,3},{245,5},{247,7},{249,9},{251,11},{253,13},{255,15}... | collective-permute-start | bytes 1572872 | tf_op jit(solution)/shard_map/ppermute | solution.py:323
  58.0 24.5 %collective-permute-start.3 = (bf16[64,4096]{1,0:T(8,128)(2,1)}, bf16[64,4096]{1,0:T(8,128)(2,1)}, u32[]{:S(2)}, u32[]{:S(2)}) collective-permute-start(bf16[64,4096]{1,0:T(8,128)(2,1)} %collective-permute-done.2.low), channel_id=1, source_target_pairs={{1,0},{3,2},{5,4},{7,6},{9,8},{11,10},{13,12},{15,14},{17,16},{19,... | collective-permute-start | bytes 1572872 | tf_op jit(solution)/shard_map/ppermute | solution.py:323
  59.3 23.2 %collective-permute-start.6 = (bf16[64,4096]{1,0:T(8,128)(2,1)}, bf16[64,4096]{1,0:T(8,128)(2,1)}, u32[]{:S(2)}, u32[]{:S(2)}) collective-permute-start(bf16[64,4096]{1,0:T(8,128)(2,1)} %collective-permute-done.low.first_low), channel_id=1, source_target_pairs={{241,1},{243,3},{245,5},{247,7},{249,9},{251,11},{253,13},{255,15}... | collective-permute-start | bytes 1572872 | tf_op jit(solution)/shard_map/ppermute | solution.py:323
  66.5 11.4 %collective-permute-start.8 = (bf16[64,640]{1,0:T(8,128)(2,1)S(1)}, bf16[64,640]{1,0:T(8,128)(2,1)S(1)}, u32[]{:S(2)}, u32[]{:S(2)}) collective-permute-start(bf16[64,640]{1,0:T(8,128)(2,1)S(1)} %get-tuple-element.35), channel_id=1, source_target_pairs={{16,0},{17,1},{18,2},{19,3},{20,4},{21,5},{22,6},{23,7},{24,8},{25... | collective-permute-start | bytes 245768 | tf_op jit(solution)/shard_map/ppermute | solution.py:323
  88.0 14.6 %collective-permute-start.11 = (f32[2,64,256]{2,1,0:T(8,128)S(1)}, f32[2,64,256]{2,1,0:T(8,128)S(1)}, u32[]{:S(2)}, u32[]{:S(2)}) collective-permute-start(f32[2,64,256]{2,1,0:T(8,128)S(1)} %get-tuple-element.45), channel_id=1, source_target_pairs={{15,0},{0,1},{1,2},{2,3},{3,4},{4,5},{5,6},{6,7},{7,8},{8,9},{9,10... | collective-permute-start | bytes 393224 | tf_op jit(solution)/shard_map/ppermute | solution.py:323
  102.6 7.0 %collective-permute-start.12 = (f32[64,256]{1,0:T(8,128)S(1)}, f32[64,256]{1,0:T(8,128)S(1)}, u32[]{:S(2)}, u32[]{:S(2)}) collective-permute-start(f32[64,256]{1,0:T(8,128)S(1)} %fusion.1), channel_id=1, source_target_pairs={{240,0},{241,1},{242,2},{243,3},{244,4},{245,5},{246,6},{247,7},{2... | collective-permute-start | bytes 196616 | tf_op jit(solution)/shard_map/ppermute | solution.py:323
  114.1 37.7 %collective-permute-start.30 = (f32[2,64,256]{2,1,0:T(8,128)S(1)}, f32[2,64,256]{2,1,0:T(8,128)S(1)}, u32[]{:S(2)}, u32[]{:S(2)}) collective-permute-start(f32[2,64,256]{2,1,0:T(8,128)S(1)} %pad_maximum_fusion), channel_id=1, source_target_pairs={{1,0},{2,1},{3,2},{4,3},{5,4},{6,5},{7,6},{8,7},{9,8},{10,9},{11,1... | collective-permute-start | bytes 393224 | tf_op jit(solution)/shard_map/ppermute | solution.py:323
  114.2 10.0 %collective-permute-start.13 = (f32[2,256]{1,0:T(2,128)S(1)}, f32[2,256]{1,0:T(2,128)S(1)}, u32[]{:S(2)}, u32[]{:S(2)}) collective-permute-start(f32[2,256]{1,0:T(2,128)S(1)} %get-tuple-element.47), channel_id=1, source_target_pairs={{48,0},{49,1},{50,2},{51,3},{52,4},{53,5},{54,6},{55,7},{56,8},{57... | collective-permute-start | bytes 6152 | tf_op jit(solution)/shard_map/ppermute | solution.py:350
  125.3 5.4 %collective-permute-start.15 = (f32[2,256]{1,0:T(2,128)S(1)}, f32[2,256]{1,0:T(2,128)S(1)}, u32[]{:S(2)}, u32[]{:S(2)}) collective-permute-start(f32[2,256]{1,0:T(2,128)S(1)} %add.63), channel_id=1, source_target_pairs={{50,0},{51,1},{48,2},{49,3},{54,4},{55,5},{52,6},{53,7},{58,8},{59... | collective-permute-start | bytes 6152 | tf_op jit(solution)/shard_map/ppermute | solution.py:350
  137.9 4.8 %collective-permute-start.18 = (f32[2,256]{1,0:T(2,128)S(1)}, f32[2,256]{1,0:T(2,128)S(1)}, u32[]{:S(2)}, u32[]{:S(2)}) collective-permute-start(f32[2,256]{1,0:T(2,128)S(1)} %add.66), channel_id=1, source_target_pairs={{12,0},{13,1},{14,2},{15,3},{8,4},{9,5},{10,6},{11,7},{4,8},{5,9},... | collective-permute-start | bytes 6152 | tf_op jit(solution)/shard_map/ppermute | solution.py:350
  146.2 4.8 %collective-permute-start.20 = (f32[2,256]{1,0:T(2,128)S(1)}, f32[2,256]{1,0:T(2,128)S(1)}, u32[]{:S(2)}, u32[]{:S(2)}) collective-permute-start(f32[2,256]{1,0:T(2,128)S(1)} %add.68.part), channel_id=1, source_target_pairs={{192,0},{193,1},{194,2},{195,3},{196,4},{197,5},{198,6},{199,7},{2... | collective-permute-start | bytes 6152 | tf_op jit(solution)/shard_map/ppermute | solution.py:350
  153.7 11.4 %collective-permute-start.31 = (f32[2,64,256]{2,1,0:T(8,128)S(1)}, f32[2,64,256]{2,1,0:T(8,128)S(1)}, u32[]{:S(2)}, u32[]{:S(2)}) collective-permute-start(f32[2,64,256]{2,1,0:T(8,128)S(1)} %get-tuple-element.53), channel_id=1, source_target_pairs={{15,0},{0,1},{1,2},{2,3},{3,4},{4,5},{5,6},{6,7},{7,8},{8,9},{9,10... | collective-permute-start | bytes 393224 | tf_op jit(solution)/shard_map/ppermute | solution.py:323
  165.1 31.8 %collective-permute-start.32 = (f32[64,256]{1,0:T(8,128)S(1)}, f32[64,256]{1,0:T(8,128)S(1)}, u32[]{:S(2)}, u32[]{:S(2)}) collective-permute-start(f32[64,256]{1,0:T(8,128)S(1)} %fusion), channel_id=1, source_target_pairs={{240,0},{241,1},{242,2},{243,3},{244,4},{245,5},{246,6},{247,7},{2... | collective-permute-start | bytes 196616 | tf_op jit(solution)/shard_map/ppermute | solution.py:323
  168.9 5.4 %collective-permute-start.22 = (f32[1,256]{1,0:T(1,128)S(1)}, f32[1,256]{1,0:T(1,128)S(1)}, u32[]{:S(2)}, u32[]{:S(2)}) collective-permute-start(f32[1,256]{1,0:T(1,128)S(1)} %add.69), channel_id=1, source_target_pairs={{48,0},{49,1},{50,2},{51,3},{52,4},{53,5},{54,6},{55,7},{56,8},{57... | collective-permute-start | bytes 3080 | tf_op jit(solution)/shard_map/ppermute | solution.py:350
  175.4 4.8 %collective-permute-start.24 = (f32[1,256]{1,0:T(1,128)S(1)}, f32[1,256]{1,0:T(1,128)S(1)}, u32[]{:S(2)}, u32[]{:S(2)}) collective-permute-start(f32[1,256]{1,0:T(1,128)S(1)} %add.71), channel_id=1, source_target_pairs={{50,0},{51,1},{48,2},{49,3},{54,4},{55,5},{52,6},{53,7},{58,8},{59... | collective-permute-start | bytes 3080 | tf_op jit(solution)/shard_map/ppermute | solution.py:350
  183.8 4.8 %collective-permute-start.26 = (f32[1,256]{1,0:T(1,128)S(1)}, f32[1,256]{1,0:T(1,128)S(1)}, u32[]{:S(2)}, u32[]{:S(2)}) collective-permute-start(f32[1,256]{1,0:T(1,128)S(1)} %add.73), channel_id=1, source_target_pairs={{12,0},{13,1},{14,2},{15,3},{8,4},{9,5},{10,6},{11,7},{4,8},{5,9},... | collective-permute-start | bytes 3080 | tf_op jit(solution)/shard_map/ppermute | solution.py:350
  192.1 4.8 %collective-permute-start.28 = (f32[1,256]{1,0:T(1,128)S(1)}, f32[1,256]{1,0:T(1,128)S(1)}, u32[]{:S(2)}, u32[]{:S(2)}) collective-permute-start(f32[1,256]{1,0:T(1,128)S(1)} %add.75.part), channel_id=1, source_target_pairs={{192,0},{193,1},{194,2},{195,3},{196,4},{197,5},{198,6},{199,7},{2... | collective-permute-start | bytes 3080 | tf_op jit(solution)/shard_map/ppermute | solution.py:350
  (19 other events, 148.8 us)

commit v8 on v7

--- a/solution.py
+++ b/solution.py
@@ -120,6 +120,18 @@
 
 def stack_two(low, high, states):
     return jnp.concatenate([stack(low, states // 2), stack(high, states // 2)], axis=0)
+
+
+def cut_body(rho, low, high, sems):
+    half = low.shape[1]
+    copies = [
+        pltpu.make_async_copy(rho.at[:, k * half : (k + 1) * half], out, sems.at[k])
+        for k, out in enumerate((low, high))
+    ]
+    for copy in copies:
+        copy.start()
+    for copy in copies:
+        copy.wait()
 
 
 def note_weights(note, mols, k):
@@ -354,10 +366,18 @@
 
     rho_a, y_a, e_a = densities[0, 0], trials[0, 0], energies[0, 0]
     core = (lax.axis_index("gy") % 2).astype(jnp.int32).reshape(1, 1)
+    piece = shape(mols, rho_a.shape[1] // 2, dtype=BF)
+    own_low, own_high = pl.pallas_call(
+        cut_body,
+        out_shape=(piece, piece),
+        in_specs=[pl.BlockSpec(memory_space=pltpu.HBM)],
+        out_specs=(pl.BlockSpec(memory_space=pltpu.VMEM),) * 2,
+        scratch_shapes=[pltpu.SemaphoreType.DMA((2,))],
+        compiler_params=pltpu.CompilerParams(vmem_limit_bytes=4 * 2**20),
+    )(rho_a)
     table = [(spot(x + y % 2, y + 1), spot(x, y)) for x in range(nx) for y in range(ny)]
-    half = rho_a.shape[1] // 2
-    first_low = lax.ppermute(rho_a[:, :half], AXES, table)
-    first_high = lax.ppermute(rho_a[:, half:], AXES, table)
+    first_low = lax.ppermute(own_low, AXES, table)
+    first_high = lax.ppermute(own_high, AXES, table)
 
     pair = shape(mols, 2 * mols)
     note = shape(mols, field + 6 * mols, dtype=BF)
@@ -372,8 +392,8 @@
     msg_c = take(msg_c, 1, 1)
 
     even, odd = (lambda x, y: y % 2 == 0), (lambda x, y: y % 2 == 1)
-    right_low = take(rho_a[:, :half], 1, 0)
-    right_high = take(rho_a[:, half:], 1, 0)
+    right_low = take(own_low, 1, 0)
+    right_high = take(own_high, 1, 0)
     shift_low = take(first_low, -1, 0, odd)
     shift_high = take(first_high, -1, 0, odd)
     near_low = take(right_low, 0, 1, even)
@@ -451,7 +471,7 @@
         9 * width * width * 2,
         1,
     )(core, theta, resid, sig_r, sig_uc, msg_r, msg_u, msg_c, c_aa, c_f, c_r, c_s)
-    squares = butterfly(squares, [x_near, z_far, chip, z_mid, z_near, x_far, y_near, y_far])
+    squares = butterfly(squares, [x_near, x_far, z_far, chip, z_mid, z_near, y_near, y_far])
     below, left = home(to_r, to_uc)
     corr, sigma2 = call(
         functools.partial(last_body, states, float(width * nx * ny)),

time: 198 us -> 198 us (level)
  local copies, waits for them, and re-layouts: 4.23 us -> 7.81 us
  waiting for transfers between devices: 115 us -> 112 us
    unnamed x21 -> x23, local copies, waits for them, and re-layouts: 2.93 us -> 7.81 us
    ppermute x15, waiting for transfers between devices: 67.2 us -> 63.6 us  [take(): return lax.ppermute(value, AXES, table)]
where the time goes in v8:
time: 198 us
  waiting for transfers between devices  112 us (57%)
  starting transfers between devices  56.5 us (29%)
  Pallas kernels  20.7 us (10%)
  local copies, waits for them, and re-layouts  7.81 us (4%)
    ppermute x15, waiting for transfers between devices, take(): return lax.ppermute(value, AXES, table)  63.6 us
    ppermute x16, waiting for transfers between devices, butterfly(): other = lax.ppermute(value, AXES, table)  48.2 us
    ppermute x15, starting transfers between devices, take(): return lax.ppermute(value, AXES, table)  32.5 us
    pallas_call x8, Pallas kernels, call(): pl.pallas_call(body, out_shape=outs, in_specs=[pl.BlockSpec(memory_space=...  20.6 us
    ppermute x16, starting transfers between devices, butterfly(): other = lax.ppermute(value, AXES, table)  20.4 us
    unnamed x23, local copies, waits for them, and re-layouts  7.81 us
  transfers between devices with their start and end apart: 33, of which 22 were waited for; matrix products, arithmetic and copies ran while one was open for 0% of the time, Pallas kernels for 6%

profile of v8, /device:TPU:24, one launch (start us, length us, event | category | flops | bytes accessed | tf_op | source)
XLA Modules:
  0.0 197.7 jit_solution(11851243816939273558)
XLA Ops:
  2.0 4.9 %collective-permute-start.2 = (bf16[64,4096]{1,0:T(8,128)(2,1)S(1)}, bf16[64,4096]{1,0:T(8,128)(2,1)}, u32[]{:S(2)}, u32[]{:S(2)}) collective-permute-start(bf16[64,4096]{1,0:T(8,128)(2,1)S(1)} %get-tuple-element.33), channel_id=1, source_target_pairs={{16,0},{17,1},{18,2},{19,3},{20,4},{21,5},{22,6},{23,7},{24,8},{25... | collective-permute-start | bytes 1572872 | tf_op jit(solution)/shard_map/ppermute | solution.py:335
  6.8 3.6 %collective-permute-start = (bf16[64,4096]{1,0:T(8,128)(2,1)S(1)}, bf16[64,4096]{1,0:T(8,128)(2,1)S(1)}, u32[]{:S(2)}, u32[]{:S(2)}) collective-permute-start(bf16[64,4096]{1,0:T(8,128)(2,1)S(1)} %get-tuple-element.33), channel_id=1, source_target_pairs={{1,0},{18,1},{3,2},{20,3},{5,4},{22,5},{7,6},{24,7},{9,8},{26,9},{... | collective-permute-start | bytes 1572872 | tf_op jit(solution)/shard_map/ppermute | solution.py:379
  20.2 35.1 %collective-permute-done.9.msg_u = bf16[64,640]{1,0:T(8,128)(2,1)S(1)} collective-permute-done((bf16[64,640]{1,0:T(8,128)(2,1)S(1)}, bf16[64,640]{1,0:T(8,128)(2,1)S(1)}, u32[]{:S(2)}, u32[]{:S(2)}) %collective-permute-start.9) | collective-permute-done | bytes 81952 | tf_op jit(solution)/shard_map/ppermute | solution.py:335
  63.6 2.9 %shard_map.104 = (bf16[512,1024]{1,0:T(8,128)(2,1)S(1)}, bf16[512,1024]{1,0:T(8,128)(2,1)S(1)}, bf16[512,512]{1,0:T(8,128)(2,1)S(1)}) custom-call(bf16[64,8192]{1,0:T(8,128)(2,1)S(1)} %bitcast.28, bf16[1024,1024]{1,0:T(8,128)(2,1)S(1)} %copy-done.6, f32[64,128]{1,0:T(8,128)S(1)} %get-tuple-element.35.own), custom_call_target="tpu_custom_call" | custom-call | flops 2684354560 | bytes 5242880 | tf_op jit(solution)/shard_map/pallas_call | solution.py:23
  66.5 6.2 %collective-permute-start.8 = (bf16[64,640]{1,0:T(8,128)(2,1)S(1)}, bf16[64,640]{1,0:T(8,128)(2,1)S(1)}, u32[]{:S(2)}, u32[]{:S(2)}) collective-permute-start(bf16[64,640]{1,0:T(8,128)(2,1)S(1)} %get-tuple-element.39), channel_id=1, source_target_pairs={{16,0},{17,1},{18,2},{19,3},{20,4},{21,5},{22,6},{23,7},{24,8},{25... | collective-permute-start | bytes 245768 | tf_op jit(solution)/shard_map/ppermute | solution.py:335
  77.9 4.6 %shard_map.105 = (bf16[512,1024]{1,0:T(8,128)(2,1)S(1)}, bf16[512,1024]{1,0:T(8,128)(2,1)S(1)}, bf16[2,512,512]{2,1,0:T(8,128)(2,1)S(1)}) custom-call(bf16[64,8192]{1,0:T(8,128)(2,1)S(1)} %bitcast.29, bf16[64,4096]{1,0:T(8,128)(2,1)} %collective-permute-done.2.low, bf16[64,4096]{1,0:T(8,128)(2,1)} %collective-permute-done.4.high, ...), custom_call_target="tpu_custom_call" | custom-call | flops 3221225472 | bytes 8388608 | tf_op jit(solution)/shard_map/pallas_call | solution.py:23
  82.5 5.5 %shard_map.107 = (bf16[4,512,512]{2,1,0:T(8,128)(2,1)S(1)}, f32[64,256]{1,0:T(8,128)S(1)}, f32[64,256]{1,0:T(8,128)S(1)}, f32[2,64,256]{2,1,0:T(8,128)S(1)}, f32[2,256]{1,0:T(2,128)S(1)}) custom-call(s32[1,1]{1,0:T(1,128)} %bitcast.core, bf16[64,4096]{1,0:T(8,128)(2,1)S(1)} %collective-permute-done.low.first_low, ...), custom_call_target="tpu_custom_call" | custom-call | flops 2147483648 | bytes 9437184 | tf_op jit(solution)/shard_map/pallas_call | solution.py:23
  88.0 9.1 %collective-permute-start.11 = (f32[2,64,256]{2,1,0:T(8,128)S(1)}, f32[2,64,256]{2,1,0:T(8,128)S(1)}, u32[]{:S(2)}, u32[]{:S(2)}) collective-permute-start(f32[2,64,256]{2,1,0:T(8,128)S(1)} %get-tuple-element.49), channel_id=1, source_target_pairs={{15,0},{0,1},{1,2},{2,3},{3,4},{4,5},{5,6},{6,7},{7,8},{8,9},{9,10... | collective-permute-start | bytes 393224 | tf_op jit(solution)/shard_map/ppermute | solution.py:335
  97.2 5.5 %collective-permute-done.11 = f32[2,64,256]{2,1,0:T(8,128)S(1)} collective-permute-done((f32[2,64,256]{2,1,0:T(8,128)S(1)}, f32[2,64,256]{2,1,0:T(8,128)S(1)}, u32[]{:S(2)}, u32[]{:S(2)}) %collective-permute-start.11) | collective-permute-done | bytes 131104 | tf_op jit(solution)/shard_map/ppermute | solution.py:335
  103.3 6.4 %collective-permute-done.12 = f32[64,256]{1,0:T(8,128)S(1)} collective-permute-done((f32[64,256]{1,0:T(8,128)S(1)}, f32[64,256]{1,0:T(8,128)S(1)}, u32[]{:S(2)}, u32[]{:S(2)}) %collective-permute-start.12) | collective-permute-done | bytes 65568 | tf_op jit(solution)/shard_map/ppermute | solution.py:335
  114.1 7.1 %collective-permute-start.13 = (f32[2,256]{1,0:T(2,128)S(1)}, f32[2,256]{1,0:T(2,128)S(1)}, u32[]{:S(2)}, u32[]{:S(2)}) collective-permute-start(f32[2,256]{1,0:T(2,128)S(1)} %get-tuple-element.51), channel_id=1, source_target_pairs={{48,0},{49,1},{50,2},{51,3},{52,4},{53,5},{54,6},{55,7},{56,8},{57... | collective-permute-start | bytes 6152 | tf_op jit(solution)/shard_map/ppermute | solution.py:362
  121.2 2.9 %collective-permute-done.13 = f32[2,256]{1,0:T(2,128)S(1)} collective-permute-done((f32[2,256]{1,0:T(2,128)S(1)}, f32[2,256]{1,0:T(2,128)S(1)}, u32[]{:S(2)}, u32[]{:S(2)}) %collective-permute-start.13) | collective-permute-done | bytes 2080 | tf_op jit(solution)/shard_map/ppermute | solution.py:362
  125.3 3.8 %collective-permute-start.15 = (f32[2,256]{1,0:T(2,128)S(1)}, f32[2,256]{1,0:T(2,128)S(1)}, u32[]{:S(2)}, u32[]{:S(2)}) collective-permute-start(f32[2,256]{1,0:T(2,128)S(1)} %add.63), channel_id=1, source_target_pairs={{50,0},{51,1},{48,2},{49,3},{54,4},{55,5},{52,6},{53,7},{58,8},{59... | collective-permute-start | bytes 6152 | tf_op jit(solution)/shard_map/ppermute | solution.py:362
  130.7 3.6 %collective-permute-done.16 = f32[2,256]{1,0:T(2,128)S(1)} collective-permute-done((f32[2,256]{1,0:T(2,128)S(1)}, f32[2,256]{1,0:T(2,128)S(1)}, u32[]{:S(2)}, u32[]{:S(2)}) %collective-permute-start.16) | collective-permute-done | bytes 2080 | tf_op jit(solution)/shard_map/ppermute | solution.py:362
  139.2 3.5 %collective-permute-done.18 = f32[2,256]{1,0:T(2,128)S(1)} collective-permute-done((f32[2,256]{1,0:T(2,128)S(1)}, f32[2,256]{1,0:T(2,128)S(1)}, u32[]{:S(2)}, u32[]{:S(2)}) %collective-permute-start.18) | collective-permute-done | bytes 2080 | tf_op jit(solution)/shard_map/ppermute | solution.py:362
  142.6 3.6 %collective-permute-done.19 = f32[2,256]{1,0:T(2,128)S(1)} collective-permute-done((f32[2,256]{1,0:T(2,128)S(1)}, f32[2,256]{1,0:T(2,128)S(1)}, u32[]{:S(2)}, u32[]{:S(2)}) %collective-permute-start.19) | collective-permute-done | bytes 2080 | tf_op jit(solution)/shard_map/ppermute | solution.py:362
  146.5 4.5 %collective-permute-done.20.rest = f32[2,256]{1,0:T(2,128)S(1)} collective-permute-done((f32[2,256]{1,0:T(2,128)S(1)}, f32[2,256]{1,0:T(2,128)S(1)}, u32[]{:S(2)}, u32[]{:S(2)}) %collective-permute-start.20) | collective-permute-done | bytes 2080 | tf_op jit(solution)/shard_map/ppermute | solution.py:362
  153.7 11.3 %collective-permute-done.31.below = f32[2,64,256]{2,1,0:T(8,128)S(1)} collective-permute-done((f32[2,64,256]{2,1,0:T(8,128)S(1)}, f32[2,64,256]{2,1,0:T(8,128)S(1)}, u32[]{:S(2)}, u32[]{:S(2)}) %collective-permute-start.31) | collective-permute-done | bytes 131104 | tf_op jit(solution)/shard_map/ppermute | solution.py:335
  165.3 3.6 %collective-permute-done.21 = f32[1,256]{1,0:T(1,128)S(1)} collective-permute-done((f32[1,256]{1,0:T(1,128)S(1)}, f32[1,256]{1,0:T(1,128)S(1)}, u32[]{:S(2)}, u32[]{:S(2)}) %collective-permute-start.21) | collective-permute-done | bytes 1056 | tf_op jit(solution)/shard_map/ppermute | solution.py:362
  169.4 4.2 %collective-permute-done.22 = f32[1,256]{1,0:T(1,128)S(1)} collective-permute-done((f32[1,256]{1,0:T(1,128)S(1)}, f32[1,256]{1,0:T(1,128)S(1)}, u32[]{:S(2)}, u32[]{:S(2)}) %collective-permute-start.22) | collective-permute-done | bytes 1056 | tf_op jit(solution)/shard_map/ppermute | solution.py:362
  173.6 3.3 %collective-permute-start.23 = (f32[1,256]{1,0:T(1,128)S(1)}, f32[1,256]{1,0:T(1,128)S(1)}, u32[]{:S(2)}, u32[]{:S(2)}) collective-permute-start(f32[1,256]{1,0:T(1,128)S(1)} %add.70), channel_id=1, source_target_pairs={{48,0},{49,1},{50,2},{51,3},{52,4},{53,5},{54,6},{55,7},{56,8},{57... | collective-permute-start | bytes 3080 | tf_op jit(solution)/shard_map/ppermute | solution.py:362
  181.6 3.4 %collective-permute-done.25 = f32[1,256]{1,0:T(1,128)S(1)} collective-permute-done((f32[1,256]{1,0:T(1,128)S(1)}, f32[1,256]{1,0:T(1,128)S(1)}, u32[]{:S(2)}, u32[]{:S(2)}) %collective-permute-start.25) | collective-permute-done | bytes 1056 | tf_op jit(solution)/shard_map/ppermute | solution.py:362
  185.2 3.4 %collective-permute-done.26 = f32[1,256]{1,0:T(1,128)S(1)} collective-permute-done((f32[1,256]{1,0:T(1,128)S(1)}, f32[1,256]{1,0:T(1,128)S(1)}, u32[]{:S(2)}, u32[]{:S(2)}) %collective-permute-start.26) | collective-permute-done | bytes 1056 | tf_op jit(solution)/shard_map/ppermute | solution.py:362
  192.3 4.6 %collective-permute-done.28.rest = f32[1,256]{1,0:T(1,128)S(1)} collective-permute-done((f32[1,256]{1,0:T(1,128)S(1)}, f32[1,256]{1,0:T(1,128)S(1)}, u32[]{:S(2)}, u32[]{:S(2)}) %collective-permute-start.28) | collective-permute-done | bytes 1056 | tf_op jit(solution)/shard_map/ppermute | solution.py:362
  (92 shorter events, 50.4 us)
Async XLA Ops:
  2.0 53.3 %collective-permute-start.2 = (bf16[64,4096]{1,0:T(8,128)(2,1)S(1)}, bf16[64,4096]{1,0:T(8,128)(2,1)}, u32[]{:S(2)}, u32[]{:S(2)}) collective-permute-start(bf16[64,4096]{1,0:T(8,128)(2,1)S(1)} %get-tuple-element.33), channel_id=1, source_target_pairs={{16,0},{17,1},{18,2},{19,3},{20,4},{21,5},{22,6},{23,7},{24,8},{25... | collective-permute-start | bytes 1572872 | tf_op jit(solution)/shard_map/ppermute | solution.py:335
  6.8 49.7 %collective-permute-start = (bf16[64,4096]{1,0:T(8,128)(2,1)S(1)}, bf16[64,4096]{1,0:T(8,128)(2,1)S(1)}, u32[]{:S(2)}, u32[]{:S(2)}) collective-permute-start(bf16[64,4096]{1,0:T(8,128)(2,1)S(1)} %get-tuple-element.33), channel_id=1, source_target_pairs={{1,0},{18,1},{3,2},{20,3},{5,4},{22,5},{7,6},{24,7},{9,8},{26,9},{... | collective-permute-start | bytes 1572872 | tf_op jit(solution)/shard_map/ppermute | solution.py:379
  10.4 47.6 %collective-permute-start.4 = (bf16[64,4096]{1,0:T(8,128)(2,1)S(1)}, bf16[64,4096]{1,0:T(8,128)(2,1)}, u32[]{:S(2)}, u32[]{:S(2)}) collective-permute-start(bf16[64,4096]{1,0:T(8,128)(2,1)S(1)} %get-tuple-element.34), channel_id=1, source_target_pairs={{16,0},{17,1},{18,2},{19,3},{20,4},{21,5},{22,6},{23,7},{24,8},{25... | collective-permute-start | bytes 1572872 | tf_op jit(solution)/shard_map/ppermute | solution.py:335
  13.2 46.1 %collective-permute-start.1 = (bf16[64,4096]{1,0:T(8,128)(2,1)S(1)}, bf16[64,4096]{1,0:T(8,128)(2,1)}, u32[]{:S(2)}, u32[]{:S(2)}) collective-permute-start(bf16[64,4096]{1,0:T(8,128)(2,1)S(1)} %get-tuple-element.34), channel_id=1, source_target_pairs={{1,0},{18,1},{3,2},{20,3},{5,4},{22,5},{7,6},{24,7},{9,8},{26,9},{... | collective-permute-start | bytes 1572872 | tf_op jit(solution)/shard_map/ppermute | solution.py:380
  18.8 36.5 %collective-permute-start.9 = (bf16[64,640]{1,0:T(8,128)(2,1)S(1)}, bf16[64,640]{1,0:T(8,128)(2,1)S(1)}, u32[]{:S(2)}, u32[]{:S(2)}) collective-permute-start(bf16[64,640]{1,0:T(8,128)(2,1)S(1)} %get-tuple-element.44), channel_id=1, source_target_pairs={{1,0},{2,1},{3,2},{4,3},{5,4},{6,5},{7,6},{8,7},{9,8},{10,9},{11,1... | collective-permute-start | bytes 245768 | tf_op jit(solution)/shard_map/ppermute | solution.py:335
  55.2 11.2 %collective-permute-start.10 = (bf16[64,640]{1,0:T(8,128)(2,1)}, bf16[64,640]{1,0:T(8,128)(2,1)S(1)}, u32[]{:S(2)}, u32[]{:S(2)}) collective-permute-start(bf16[64,640]{1,0:T(8,128)(2,1)} %get-tuple-element.45), channel_id=1, source_target_pairs={{17,0},{18,1},{19,2},{20,3},{21,4},{22,5},{23,6},{24,7},{25,8},{26... | collective-permute-start | bytes 245768 | tf_op jit(solution)/shard_map/ppermute | solution.py:335
  55.2 27.3 %collective-permute-start.3 = (bf16[64,4096]{1,0:T(8,128)(2,1)}, bf16[64,4096]{1,0:T(8,128)(2,1)}, u32[]{:S(2)}, u32[]{:S(2)}) collective-permute-start(bf16[64,4096]{1,0:T(8,128)(2,1)} %collective-permute-done.2.low), channel_id=1, source_target_pairs={{1,0},{3,2},{5,4},{7,6},{9,8},{11,10},{13,12},{15,14},{17,16},{19,... | collective-permute-start | bytes 1572872 | tf_op jit(solution)/shard_map/ppermute | solution.py:335
  56.5 26.0 %collective-permute-start.6 = (bf16[64,4096]{1,0:T(8,128)(2,1)S(1)}, bf16[64,4096]{1,0:T(8,128)(2,1)}, u32[]{:S(2)}, u32[]{:S(2)}) collective-permute-start(bf16[64,4096]{1,0:T(8,128)(2,1)S(1)} %collective-permute-done.low.first_low), channel_id=1, source_target_pairs={{241,1},{243,3},{245,5},{247,7},{249,9},{251,11},{253,13},{255,15}... | collective-permute-start | bytes 1572872 | tf_op jit(solution)/shard_map/ppermute | solution.py:335
  58.0 24.5 %collective-permute-start.5 = (bf16[64,4096]{1,0:T(8,128)(2,1)}, bf16[64,4096]{1,0:T(8,128)(2,1)}, u32[]{:S(2)}, u32[]{:S(2)}) collective-permute-start(bf16[64,4096]{1,0:T(8,128)(2,1)} %collective-permute-done.4.high), channel_id=1, source_target_pairs={{1,0},{3,2},{5,4},{7,6},{9,8},{11,10},{13,12},{15,14},{17,16},{19,... | collective-permute-start | bytes 1572872 | tf_op jit(solution)/shard_map/ppermute | solution.py:335
  59.3 23.2 %collective-permute-start.7 = (bf16[64,4096]{1,0:T(8,128)(2,1)}, bf16[64,4096]{1,0:T(8,128)(2,1)}, u32[]{:S(2)}, u32[]{:S(2)}) collective-permute-start(bf16[64,4096]{1,0:T(8,128)(2,1)} %collective-permute-done.1.high.first_high), channel_id=1, source_target_pairs={{241,1},{243,3},{245,5},{247,7},{249,9},{251,11},{253,13},{255,15}... | collective-permute-start | bytes 1572872 | tf_op jit(solution)/shard_map/ppermute | solution.py:335
  66.5 11.4 %collective-permute-start.8 = (bf16[64,640]{1,0:T(8,128)(2,1)S(1)}, bf16[64,640]{1,0:T(8,128)(2,1)S(1)}, u32[]{:S(2)}, u32[]{:S(2)}) collective-permute-start(bf16[64,640]{1,0:T(8,128)(2,1)S(1)} %get-tuple-element.39), channel_id=1, source_target_pairs={{16,0},{17,1},{18,2},{19,3},{20,4},{21,5},{22,6},{23,7},{24,8},{25... | collective-permute-start | bytes 245768 | tf_op jit(solution)/shard_map/ppermute | solution.py:335
  88.0 14.6 %collective-permute-start.11 = (f32[2,64,256]{2,1,0:T(8,128)S(1)}, f32[2,64,256]{2,1,0:T(8,128)S(1)}, u32[]{:S(2)}, u32[]{:S(2)}) collective-permute-start(f32[2,64,256]{2,1,0:T(8,128)S(1)} %get-tuple-element.49), channel_id=1, source_target_pairs={{15,0},{0,1},{1,2},{2,3},{3,4},{4,5},{5,6},{6,7},{7,8},{8,9},{9,10... | collective-permute-start | bytes 393224 | tf_op jit(solution)/shard_map/ppermute | solution.py:335
  102.6 7.0 %collective-permute-start.12 = (f32[64,256]{1,0:T(8,128)S(1)}, f32[64,256]{1,0:T(8,128)S(1)}, u32[]{:S(2)}, u32[]{:S(2)}) collective-permute-start(f32[64,256]{1,0:T(8,128)S(1)} %fusion.1), channel_id=1, source_target_pairs={{240,0},{241,1},{242,2},{243,3},{244,4},{245,5},{246,6},{247,7},{2... | collective-permute-start | bytes 196616 | tf_op jit(solution)/shard_map/ppermute | solution.py:335
  114.1 37.6 %collective-permute-start.30 = (f32[2,64,256]{2,1,0:T(8,128)S(1)}, f32[2,64,256]{2,1,0:T(8,128)S(1)}, u32[]{:S(2)}, u32[]{:S(2)}) collective-permute-start(f32[2,64,256]{2,1,0:T(8,128)S(1)} %pad_maximum_fusion), channel_id=1, source_target_pairs={{1,0},{2,1},{3,2},{4,3},{5,4},{6,5},{7,6},{8,7},{9,8},{10,9},{11,1... | collective-permute-start | bytes 393224 | tf_op jit(solution)/shard_map/ppermute | solution.py:335
  114.1 10.0 %collective-permute-start.13 = (f32[2,256]{1,0:T(2,128)S(1)}, f32[2,256]{1,0:T(2,128)S(1)}, u32[]{:S(2)}, u32[]{:S(2)}) collective-permute-start(f32[2,256]{1,0:T(2,128)S(1)} %get-tuple-element.51), channel_id=1, source_target_pairs={{48,0},{49,1},{50,2},{51,3},{52,4},{53,5},{54,6},{55,7},{56,8},{57... | collective-permute-start | bytes 6152 | tf_op jit(solution)/shard_map/ppermute | solution.py:362
  125.3 5.4 %collective-permute-start.15 = (f32[2,256]{1,0:T(2,128)S(1)}, f32[2,256]{1,0:T(2,128)S(1)}, u32[]{:S(2)}, u32[]{:S(2)}) collective-permute-start(f32[2,256]{1,0:T(2,128)S(1)} %add.63), channel_id=1, source_target_pairs={{50,0},{51,1},{48,2},{49,3},{54,4},{55,5},{52,6},{53,7},{58,8},{59... | collective-permute-start | bytes 6152 | tf_op jit(solution)/shard_map/ppermute | solution.py:362
  137.8 4.8 %collective-permute-start.18 = (f32[2,256]{1,0:T(2,128)S(1)}, f32[2,256]{1,0:T(2,128)S(1)}, u32[]{:S(2)}, u32[]{:S(2)}) collective-permute-start(f32[2,256]{1,0:T(2,128)S(1)} %add.66), channel_id=1, source_target_pairs={{12,0},{13,1},{14,2},{15,3},{8,4},{9,5},{10,6},{11,7},{4,8},{5,9},... | collective-permute-start | bytes 6152 | tf_op jit(solution)/shard_map/ppermute | solution.py:362
  146.2 4.8 %collective-permute-start.20 = (f32[2,256]{1,0:T(2,128)S(1)}, f32[2,256]{1,0:T(2,128)S(1)}, u32[]{:S(2)}, u32[]{:S(2)}) collective-permute-start(f32[2,256]{1,0:T(2,128)S(1)} %add.68.part), channel_id=1, source_target_pairs={{192,0},{193,1},{194,2},{195,3},{196,4},{197,5},{198,6},{199,7},{2... | collective-permute-start | bytes 6152 | tf_op jit(solution)/shard_map/ppermute | solution.py:362
  153.7 11.4 %collective-permute-start.31 = (f32[2,64,256]{2,1,0:T(8,128)S(1)}, f32[2,64,256]{2,1,0:T(8,128)S(1)}, u32[]{:S(2)}, u32[]{:S(2)}) collective-permute-start(f32[2,64,256]{2,1,0:T(8,128)S(1)} %get-tuple-element.57), channel_id=1, source_target_pairs={{15,0},{0,1},{1,2},{2,3},{3,4},{4,5},{5,6},{6,7},{7,8},{8,9},{9,10... | collective-permute-start | bytes 393224 | tf_op jit(solution)/shard_map/ppermute | solution.py:335
  165.1 31.8 %collective-permute-start.32 = (f32[64,256]{1,0:T(8,128)S(1)}, f32[64,256]{1,0:T(8,128)S(1)}, u32[]{:S(2)}, u32[]{:S(2)}) collective-permute-start(f32[64,256]{1,0:T(8,128)S(1)} %fusion), channel_id=1, source_target_pairs={{240,0},{241,1},{242,2},{243,3},{244,4},{245,5},{246,6},{247,7},{2... | collective-permute-start | bytes 196616 | tf_op jit(solution)/shard_map/ppermute | solution.py:335
  168.9 4.8 %collective-permute-start.22 = (f32[1,256]{1,0:T(1,128)S(1)}, f32[1,256]{1,0:T(1,128)S(1)}, u32[]{:S(2)}, u32[]{:S(2)}) collective-permute-start(f32[1,256]{1,0:T(1,128)S(1)} %add.69), channel_id=1, source_target_pairs={{12,0},{13,1},{14,2},{15,3},{8,4},{9,5},{10,6},{11,7},{4,8},{5,9},... | collective-permute-start | bytes 3080 | tf_op jit(solution)/shard_map/ppermute | solution.py:362
  173.6 5.4 %collective-permute-start.23 = (f32[1,256]{1,0:T(1,128)S(1)}, f32[1,256]{1,0:T(1,128)S(1)}, u32[]{:S(2)}, u32[]{:S(2)}) collective-permute-start(f32[1,256]{1,0:T(1,128)S(1)} %add.70), channel_id=1, source_target_pairs={{48,0},{49,1},{50,2},{51,3},{52,4},{53,5},{54,6},{55,7},{56,8},{57... | collective-permute-start | bytes 3080 | tf_op jit(solution)/shard_map/ppermute | solution.py:362
  180.2 4.8 %collective-permute-start.25 = (f32[1,256]{1,0:T(1,128)S(1)}, f32[1,256]{1,0:T(1,128)S(1)}, u32[]{:S(2)}, u32[]{:S(2)}) collective-permute-start(f32[1,256]{1,0:T(1,128)S(1)} %add.72), channel_id=1, source_target_pairs={{50,0},{51,1},{48,2},{49,3},{54,4},{55,5},{52,6},{53,7},{58,8},{59... | collective-permute-start | bytes 3080 | tf_op jit(solution)/shard_map/ppermute | solution.py:362
  192.1 4.8 %collective-permute-start.28 = (f32[1,256]{1,0:T(1,128)S(1)}, f32[1,256]{1,0:T(1,128)S(1)}, u32[]{:S(2)}, u32[]{:S(2)}) collective-permute-start(f32[1,256]{1,0:T(1,128)S(1)} %add.75.part), channel_id=1, source_target_pairs={{192,0},{193,1},{194,2},{195,3},{196,4},{197,5},{198,6},{199,7},{2... | collective-permute-start | bytes 3080 | tf_op jit(solution)/shard_map/ppermute | solution.py:362
  (20 other events, 94.3 us)

commit v9 on v7

--- a/solution.py
+++ b/solution.py
@@ -119,7 +119,11 @@
 
 
 def stack_two(low, high, states):
-    return jnp.concatenate([stack(low, states // 2), stack(high, states // 2)], axis=0)
+    width = low.shape[1] // states
+    return jnp.concatenate(
+        [half[:, a * width : (a + 1) * width] for a in range(states) for half in (low, high)],
+        axis=0,
+    )
 
 
 def note_weights(note, mols, k):
@@ -143,7 +147,7 @@
 
 
 def first_body(states, core, low, high, proj, back, own_u, own_c, msg_u, msg_c, c):
-    mols = low.shape[0]
+    mols = 2 * low.shape[0]
     rows = stack_two(low, high, states)
     c[0] = couple(proj[...], rows, choose(core, own_u[...], own_c[...]))
     pair = choose(core, note_weights(msg_u, mols, 0), note_weights(msg_c, mols, 0))
@@ -205,15 +209,15 @@
     rows,
 ):
     mols, field = y_a.shape
-    width = first_low.shape[1] * 2 // states
+    width = first_low.shape[1] // states
     halves = ((first_low, near_low, shift_low), (first_high, near_high, shift_high))
     for a in range(states):
-        first, near, shifted = halves[a * 2 // states]
-        b = a % (states // 2)
-        lanes = slice(b * width, (b + 1) * width)
-        place = slice(a * mols, (a + 1) * mols)
-        rows[0, place] = first[:, lanes]
-        rows[1, place] = choose(core, near[:, lanes], shifted[:, lanes])
+        for k, (first, near, shifted) in enumerate(halves):
+            lanes = slice(a * width, (a + 1) * width)
+            start = a * mols + k * mols // 2
+            place = slice(start, start + mols // 2)
+            rows[0, place] = first[:, lanes]
+            rows[1, place] = choose(core, near[:, lanes], shifted[:, lanes])
     upper = rows.at[core[0, 0]]
     last = rows[1]
     c[0] = couple(proj_a[...], last, choose(core, own_c[...], own_u[...]))
@@ -354,10 +358,10 @@
 
     rho_a, y_a, e_a = densities[0, 0], trials[0, 0], energies[0, 0]
     core = (lax.axis_index("gy") % 2).astype(jnp.int32).reshape(1, 1)
+    own_low, own_high = rho_a[: mols // 2], rho_a[mols // 2 :]
     table = [(spot(x + y % 2, y + 1), spot(x, y)) for x in range(nx) for y in range(ny)]
-    half = rho_a.shape[1] // 2
-    first_low = lax.ppermute(rho_a[:, :half], AXES, table)
-    first_high = lax.ppermute(rho_a[:, half:], AXES, table)
+    first_low = lax.ppermute(own_low, AXES, table)
+    first_high = lax.ppermute(own_high, AXES, table)
 
     pair = shape(mols, 2 * mols)
     note = shape(mols, field + 6 * mols, dtype=BF)
@@ -372,8 +376,8 @@
     msg_c = take(msg_c, 1, 1)
 
     even, odd = (lambda x, y: y % 2 == 0), (lambda x, y: y % 2 == 1)
-    right_low = take(rho_a[:, :half], 1, 0)
-    right_high = take(rho_a[:, half:], 1, 0)
+    right_low = take(own_low, 1, 0)
+    right_high = take(own_high, 1, 0)
     shift_low = take(first_low, -1, 0, odd)
     shift_high = take(first_high, -1, 0, odd)
     near_low = take(right_low, 0, 1, even)
@@ -451,7 +455,7 @@
         9 * width * width * 2,
         1,
     )(core, theta, resid, sig_r, sig_uc, msg_r, msg_u, msg_c, c_aa, c_f, c_r, c_s)
-    squares = butterfly(squares, [x_near, z_far, chip, z_mid, z_near, x_far, y_near, y_far])
+    squares = butterfly(squares, [x_near, x_far, z_far, chip, z_mid, z_near, y_near, y_far])
     below, left = home(to_r, to_uc)
     corr, sigma2 = call(
         functools.partial(last_body, states, float(width * nx * ny)),

time: 198 us -> 198 us (level)
  no operation moved by 1% of the time
where the time goes in v9:
time: 198 us
  waiting for transfers between devices  115 us (58%)
  starting transfers between devices  56.5 us (29%)
  Pallas kernels  20.6 us (10%)
  local copies, waits for them, and re-layouts  4.23 us (2%)
    ppermute x15, waiting for transfers between devices, take(): return lax.ppermute(value, AXES, table)  67.2 us
    ppermute x16, waiting for transfers between devices, butterfly(): other = lax.ppermute(value, AXES, table)  48.2 us
    ppermute x15, starting transfers between devices, take(): return lax.ppermute(value, AXES, table)  32.5 us
    pallas_call x8, Pallas kernels, call(): pl.pallas_call(body, out_shape=outs, in_specs=[pl.BlockSpec(memory_space=...  20.6 us
    ppermute x16, starting transfers between devices, butterfly(): other = lax.ppermute(value, AXES, table)  20.4 us
  transfers between devices with their start and end apart: 33, of which 22 were waited for; matrix products, arithmetic and copies ran while one was open for 0% of the time, Pallas kernels for 6%

profile of v9, /device:TPU:24, one launch (start us, length us, event | category | flops | bytes accessed | tf_op | source)
XLA Modules:
  0.0 197.7 jit_solution(34511094677230711)
XLA Ops:
  2.0 4.9 %collective-permute-start.4 = (bf16[32,8192]{1,0:T(8,128)(2,1)S(1)}, bf16[32,8192]{1,0:T(8,128)(2,1)}, u32[]{:S(2)}, u32[]{:S(2)}) collective-permute-start(bf16[32,8192]{1,0:T(8,128)(2,1)S(1)} %get-tuple-element.58), channel_id=1, source_target_pairs={{16,0},{17,1},{18,2},{19,3},{20,4},{21,5},{22,6},{23,7},{24,8},{25... | collective-permute-start | bytes 1572872 | tf_op jit(solution)/shard_map/ppermute | solution.py:327
  6.9 3.6 %collective-permute-start.1 = (bf16[32,8192]{1,0:T(8,128)(2,1)S(1)}, bf16[32,8192]{1,0:T(8,128)(2,1)S(1)}, u32[]{:S(2)}, u32[]{:S(2)}) collective-permute-start(bf16[32,8192]{1,0:T(8,128)(2,1)S(1)} %get-tuple-element.58), channel_id=1, source_target_pairs={{1,0},{18,1},{3,2},{20,3},{5,4},{22,5},{7,6},{24,7},{9,8},{26,9},{... | collective-permute-start | bytes 1572872 | tf_op jit(solution)/shard_map/ppermute | solution.py:364
  16.6 38.7 %collective-permute-done.9.msg_u = bf16[64,640]{1,0:T(8,128)(2,1)S(1)} collective-permute-done((bf16[64,640]{1,0:T(8,128)(2,1)S(1)}, bf16[64,640]{1,0:T(8,128)(2,1)S(1)}, u32[]{:S(2)}, u32[]{:S(2)}) %collective-permute-start.9) | collective-permute-done | bytes 81952 | tf_op jit(solution)/shard_map/ppermute | solution.py:327
  63.6 2.9 %shard_map.103 = (bf16[512,1024]{1,0:T(8,128)(2,1)S(1)}, bf16[512,1024]{1,0:T(8,128)(2,1)S(1)}, bf16[512,512]{1,0:T(8,128)(2,1)S(1)}) custom-call(bf16[64,8192]{1,0:T(8,128)(2,1)S(1)} %bitcast.31, bf16[1024,1024]{1,0:T(8,128)(2,1)S(1)} %copy-done.4, f32[64,128]{1,0:T(8,128)S(1)} %get-tuple-element.31.own), custom_call_target="tpu_custom_call" | custom-call | flops 2684354560 | bytes 5242880 | tf_op jit(solution)/shard_map/pallas_call | solution.py:23
  66.5 6.2 %collective-permute-start.8 = (bf16[64,640]{1,0:T(8,128)(2,1)S(1)}, bf16[64,640]{1,0:T(8,128)(2,1)S(1)}, u32[]{:S(2)}, u32[]{:S(2)}) collective-permute-start(bf16[64,640]{1,0:T(8,128)(2,1)S(1)} %get-tuple-element.35), channel_id=1, source_target_pairs={{16,0},{17,1},{18,2},{19,3},{20,4},{21,5},{22,6},{23,7},{24,8},{25... | collective-permute-start | bytes 245768 | tf_op jit(solution)/shard_map/ppermute | solution.py:327
  77.9 4.6 %shard_map.104 = (bf16[512,1024]{1,0:T(8,128)(2,1)S(1)}, bf16[512,1024]{1,0:T(8,128)(2,1)S(1)}, bf16[2,512,512]{2,1,0:T(8,128)(2,1)S(1)}) custom-call(bf16[64,8192]{1,0:T(8,128)(2,1)S(1)} %bitcast.32, bf16[32,8192]{1,0:T(8,128)(2,1)} %collective-permute-done.2.low, bf16[32,8192]{1,0:T(8,128)(2,1)} %collective-permute-done.4.high, ...), custom_call_target="tpu_custom_call" | custom-call | flops 3221225472 | bytes 8388608 | tf_op jit(solution)/shard_map/pallas_call | solution.py:23
  82.6 5.5 %shard_map.106 = (bf16[4,512,512]{2,1,0:T(8,128)(2,1)S(1)}, f32[64,256]{1,0:T(8,128)S(1)}, f32[64,256]{1,0:T(8,128)S(1)}, f32[2,64,256]{2,1,0:T(8,128)S(1)}, f32[2,256]{1,0:T(2,128)S(1)}) custom-call(s32[1,1]{1,0:T(1,128)} %bitcast.core, bf16[32,8192]{1,0:T(8,128)(2,1)} %collective-permute-done.low.first_low, ...), custom_call_target="tpu_custom_call" | custom-call | flops 2147483648 | bytes 9437184 | tf_op jit(solution)/shard_map/pallas_call | solution.py:23
  88.0 9.1 %collective-permute-start.11 = (f32[2,64,256]{2,1,0:T(8,128)S(1)}, f32[2,64,256]{2,1,0:T(8,128)S(1)}, u32[]{:S(2)}, u32[]{:S(2)}) collective-permute-start(f32[2,64,256]{2,1,0:T(8,128)S(1)} %get-tuple-element.45), channel_id=1, source_target_pairs={{15,0},{0,1},{1,2},{2,3},{3,4},{4,5},{5,6},{6,7},{7,8},{8,9},{9,10... | collective-permute-start | bytes 393224 | tf_op jit(solution)/shard_map/ppermute | solution.py:327
  97.2 5.4 %collective-permute-done.11 = f32[2,64,256]{2,1,0:T(8,128)S(1)} collective-permute-done((f32[2,64,256]{2,1,0:T(8,128)S(1)}, f32[2,64,256]{2,1,0:T(8,128)S(1)}, u32[]{:S(2)}, u32[]{:S(2)}) %collective-permute-start.11) | collective-permute-done | bytes 131104 | tf_op jit(solution)/shard_map/ppermute | solution.py:327
  103.3 6.4 %collective-permute-done.12 = f32[64,256]{1,0:T(8,128)S(1)} collective-permute-done((f32[64,256]{1,0:T(8,128)S(1)}, f32[64,256]{1,0:T(8,128)S(1)}, u32[]{:S(2)}, u32[]{:S(2)}) %collective-permute-start.12) | collective-permute-done | bytes 65568 | tf_op jit(solution)/shard_map/ppermute | solution.py:327
  114.2 7.1 %collective-permute-start.13 = (f32[2,256]{1,0:T(2,128)S(1)}, f32[2,256]{1,0:T(2,128)S(1)}, u32[]{:S(2)}, u32[]{:S(2)}) collective-permute-start(f32[2,256]{1,0:T(2,128)S(1)} %get-tuple-element.47), channel_id=1, source_target_pairs={{48,0},{49,1},{50,2},{51,3},{52,4},{53,5},{54,6},{55,7},{56,8},{57... | collective-permute-start | bytes 6152 | tf_op jit(solution)/shard_map/ppermute | solution.py:354
  121.3 2.9 %collective-permute-done.13 = f32[2,256]{1,0:T(2,128)S(1)} collective-permute-done((f32[2,256]{1,0:T(2,128)S(1)}, f32[2,256]{1,0:T(2,128)S(1)}, u32[]{:S(2)}, u32[]{:S(2)}) %collective-permute-start.13) | collective-permute-done | bytes 2080 | tf_op jit(solution)/shard_map/ppermute | solution.py:354
  125.3 3.8 %collective-permute-start.15 = (f32[2,256]{1,0:T(2,128)S(1)}, f32[2,256]{1,0:T(2,128)S(1)}, u32[]{:S(2)}, u32[]{:S(2)}) collective-permute-start(f32[2,256]{1,0:T(2,128)S(1)} %add.63), channel_id=1, source_target_pairs={{50,0},{51,1},{48,2},{49,3},{54,4},{55,5},{52,6},{53,7},{58,8},{59... | collective-permute-start | bytes 6152 | tf_op jit(solution)/shard_map/ppermute | solution.py:354
  130.7 3.6 %collective-permute-done.16 = f32[2,256]{1,0:T(2,128)S(1)} collective-permute-done((f32[2,256]{1,0:T(2,128)S(1)}, f32[2,256]{1,0:T(2,128)S(1)}, u32[]{:S(2)}, u32[]{:S(2)}) %collective-permute-start.16) | collective-permute-done | bytes 2080 | tf_op jit(solution)/shard_map/ppermute | solution.py:354
  139.2 3.5 %collective-permute-done.18 = f32[2,256]{1,0:T(2,128)S(1)} collective-permute-done((f32[2,256]{1,0:T(2,128)S(1)}, f32[2,256]{1,0:T(2,128)S(1)}, u32[]{:S(2)}, u32[]{:S(2)}) %collective-permute-start.18) | collective-permute-done | bytes 2080 | tf_op jit(solution)/shard_map/ppermute | solution.py:354
  142.7 3.6 %collective-permute-done.19 = f32[2,256]{1,0:T(2,128)S(1)} collective-permute-done((f32[2,256]{1,0:T(2,128)S(1)}, f32[2,256]{1,0:T(2,128)S(1)}, u32[]{:S(2)}, u32[]{:S(2)}) %collective-permute-start.19) | collective-permute-done | bytes 2080 | tf_op jit(solution)/shard_map/ppermute | solution.py:354
  146.5 4.5 %collective-permute-done.20.rest = f32[2,256]{1,0:T(2,128)S(1)} collective-permute-done((f32[2,256]{1,0:T(2,128)S(1)}, f32[2,256]{1,0:T(2,128)S(1)}, u32[]{:S(2)}, u32[]{:S(2)}) %collective-permute-start.20) | collective-permute-done | bytes 2080 | tf_op jit(solution)/shard_map/ppermute | solution.py:354
  153.8 11.3 %collective-permute-done.31.below = f32[2,64,256]{2,1,0:T(8,128)S(1)} collective-permute-done((f32[2,64,256]{2,1,0:T(8,128)S(1)}, f32[2,64,256]{2,1,0:T(8,128)S(1)}, u32[]{:S(2)}, u32[]{:S(2)}) %collective-permute-start.31) | collective-permute-done | bytes 131104 | tf_op jit(solution)/shard_map/ppermute | solution.py:327
  165.3 3.6 %collective-permute-done.21 = f32[1,256]{1,0:T(1,128)S(1)} collective-permute-done((f32[1,256]{1,0:T(1,128)S(1)}, f32[1,256]{1,0:T(1,128)S(1)}, u32[]{:S(2)}, u32[]{:S(2)}) %collective-permute-start.21) | collective-permute-done | bytes 1056 | tf_op jit(solution)/shard_map/ppermute | solution.py:354
  169.4 4.2 %collective-permute-done.22 = f32[1,256]{1,0:T(1,128)S(1)} collective-permute-done((f32[1,256]{1,0:T(1,128)S(1)}, f32[1,256]{1,0:T(1,128)S(1)}, u32[]{:S(2)}, u32[]{:S(2)}) %collective-permute-start.22) | collective-permute-done | bytes 1056 | tf_op jit(solution)/shard_map/ppermute | solution.py:354
  173.7 3.3 %collective-permute-start.23 = (f32[1,256]{1,0:T(1,128)S(1)}, f32[1,256]{1,0:T(1,128)S(1)}, u32[]{:S(2)}, u32[]{:S(2)}) collective-permute-start(f32[1,256]{1,0:T(1,128)S(1)} %add.70), channel_id=1, source_target_pairs={{48,0},{49,1},{50,2},{51,3},{52,4},{53,5},{54,6},{55,7},{56,8},{57... | collective-permute-start | bytes 3080 | tf_op jit(solution)/shard_map/ppermute | solution.py:354
  181.6 3.4 %collective-permute-done.25 = f32[1,256]{1,0:T(1,128)S(1)} collective-permute-done((f32[1,256]{1,0:T(1,128)S(1)}, f32[1,256]{1,0:T(1,128)S(1)}, u32[]{:S(2)}, u32[]{:S(2)}) %collective-permute-start.25) | collective-permute-done | bytes 1056 | tf_op jit(solution)/shard_map/ppermute | solution.py:354
  185.2 3.4 %collective-permute-done.26 = f32[1,256]{1,0:T(1,128)S(1)} collective-permute-done((f32[1,256]{1,0:T(1,128)S(1)}, f32[1,256]{1,0:T(1,128)S(1)}, u32[]{:S(2)}, u32[]{:S(2)}) %collective-permute-start.26) | collective-permute-done | bytes 1056 | tf_op jit(solution)/shard_map/ppermute | solution.py:354
  192.3 4.6 %collective-permute-done.28.rest = f32[1,256]{1,0:T(1,128)S(1)} collective-permute-done((f32[1,256]{1,0:T(1,128)S(1)}, f32[1,256]{1,0:T(1,128)S(1)}, u32[]{:S(2)}, u32[]{:S(2)}) %collective-permute-start.28) | collective-permute-done | bytes 1056 | tf_op jit(solution)/shard_map/ppermute | solution.py:354
  (90 shorter events, 46.7 us)
Async XLA Ops:
  2.0 53.3 %collective-permute-start.4 = (bf16[32,8192]{1,0:T(8,128)(2,1)S(1)}, bf16[32,8192]{1,0:T(8,128)(2,1)}, u32[]{:S(2)}, u32[]{:S(2)}) collective-permute-start(bf16[32,8192]{1,0:T(8,128)(2,1)S(1)} %get-tuple-element.58), channel_id=1, source_target_pairs={{16,0},{17,1},{18,2},{19,3},{20,4},{21,5},{22,6},{23,7},{24,8},{25... | collective-permute-start | bytes 1572872 | tf_op jit(solution)/shard_map/ppermute | solution.py:327
  6.9 49.7 %collective-permute-start.1 = (bf16[32,8192]{1,0:T(8,128)(2,1)S(1)}, bf16[32,8192]{1,0:T(8,128)(2,1)S(1)}, u32[]{:S(2)}, u32[]{:S(2)}) collective-permute-start(bf16[32,8192]{1,0:T(8,128)(2,1)S(1)} %get-tuple-element.58), channel_id=1, source_target_pairs={{1,0},{18,1},{3,2},{20,3},{5,4},{22,5},{7,6},{24,7},{9,8},{26,9},{... | collective-permute-start | bytes 1572872 | tf_op jit(solution)/shard_map/ppermute | solution.py:364
  10.5 47.6 %collective-permute-start.2 = (bf16[32,8192]{1,0:T(8,128)(2,1)S(1)}, bf16[32,8192]{1,0:T(8,128)(2,1)}, u32[]{:S(2)}, u32[]{:S(2)}) collective-permute-start(bf16[32,8192]{1,0:T(8,128)(2,1)S(1)} %get-tuple-element.59), channel_id=1, source_target_pairs={{16,0},{17,1},{18,2},{19,3},{20,4},{21,5},{22,6},{23,7},{24,8},{25... | collective-permute-start | bytes 1572872 | tf_op jit(solution)/shard_map/ppermute | solution.py:327
  13.3 46.1 %collective-permute-start = (bf16[32,8192]{1,0:T(8,128)(2,1)S(1)}, bf16[32,8192]{1,0:T(8,128)(2,1)}, u32[]{:S(2)}, u32[]{:S(2)}) collective-permute-start(bf16[32,8192]{1,0:T(8,128)(2,1)S(1)} %get-tuple-element.59), channel_id=1, source_target_pairs={{1,0},{18,1},{3,2},{20,3},{5,4},{22,5},{7,6},{24,7},{9,8},{26,9},{... | collective-permute-start | bytes 1572872 | tf_op jit(solution)/shard_map/ppermute | solution.py:363
  15.1 40.1 %collective-permute-start.9 = (bf16[64,640]{1,0:T(8,128)(2,1)S(1)}, bf16[64,640]{1,0:T(8,128)(2,1)S(1)}, u32[]{:S(2)}, u32[]{:S(2)}) collective-permute-start(bf16[64,640]{1,0:T(8,128)(2,1)S(1)} %get-tuple-element.40), channel_id=1, source_target_pairs={{1,0},{2,1},{3,2},{4,3},{5,4},{6,5},{7,6},{8,7},{9,8},{10,9},{11,1... | collective-permute-start | bytes 245768 | tf_op jit(solution)/shard_map/ppermute | solution.py:327
  55.3 11.3 %collective-permute-start.10 = (bf16[64,640]{1,0:T(8,128)(2,1)}, bf16[64,640]{1,0:T(8,128)(2,1)S(1)}, u32[]{:S(2)}, u32[]{:S(2)}) collective-permute-start(bf16[64,640]{1,0:T(8,128)(2,1)} %get-tuple-element.41), channel_id=1, source_target_pairs={{17,0},{18,1},{19,2},{20,3},{21,4},{22,5},{23,6},{24,7},{25,8},{26... | collective-permute-start | bytes 245768 | tf_op jit(solution)/shard_map/ppermute | solution.py:327
  55.3 27.2 %collective-permute-start.5 = (bf16[32,8192]{1,0:T(8,128)(2,1)}, bf16[32,8192]{1,0:T(8,128)(2,1)}, u32[]{:S(2)}, u32[]{:S(2)}) collective-permute-start(bf16[32,8192]{1,0:T(8,128)(2,1)} %collective-permute-done.4.high), channel_id=1, source_target_pairs={{1,0},{3,2},{5,4},{7,6},{9,8},{11,10},{13,12},{15,14},{17,16},{19,... | collective-permute-start | bytes 1572872 | tf_op jit(solution)/shard_map/ppermute | solution.py:327
  56.6 26.0 %collective-permute-start.7 = (bf16[32,8192]{1,0:T(8,128)(2,1)S(1)}, bf16[32,8192]{1,0:T(8,128)(2,1)}, u32[]{:S(2)}, u32[]{:S(2)}) collective-permute-start(bf16[32,8192]{1,0:T(8,128)(2,1)S(1)} %collective-permute-done.1.high.first_high), channel_id=1, source_target_pairs={{241,1},{243,3},{245,5},{247,7},{249,9},{251,11},{253,13},{255,15}... | collective-permute-start | bytes 1572872 | tf_op jit(solution)/shard_map/ppermute | solution.py:327
  58.0 24.5 %collective-permute-start.3 = (bf16[32,8192]{1,0:T(8,128)(2,1)}, bf16[32,8192]{1,0:T(8,128)(2,1)}, u32[]{:S(2)}, u32[]{:S(2)}) collective-permute-start(bf16[32,8192]{1,0:T(8,128)(2,1)} %collective-permute-done.2.low), channel_id=1, source_target_pairs={{1,0},{3,2},{5,4},{7,6},{9,8},{11,10},{13,12},{15,14},{17,16},{19,... | collective-permute-start | bytes 1572872 | tf_op jit(solution)/shard_map/ppermute | solution.py:327
  59.3 23.2 %collective-permute-start.6 = (bf16[32,8192]{1,0:T(8,128)(2,1)}, bf16[32,8192]{1,0:T(8,128)(2,1)}, u32[]{:S(2)}, u32[]{:S(2)}) collective-permute-start(bf16[32,8192]{1,0:T(8,128)(2,1)} %collective-permute-done.low.first_low), channel_id=1, source_target_pairs={{241,1},{243,3},{245,5},{247,7},{249,9},{251,11},{253,13},{255,15}... | collective-permute-start | bytes 1572872 | tf_op jit(solution)/shard_map/ppermute | solution.py:327
  66.5 11.4 %collective-permute-start.8 = (bf16[64,640]{1,0:T(8,128)(2,1)S(1)}, bf16[64,640]{1,0:T(8,128)(2,1)S(1)}, u32[]{:S(2)}, u32[]{:S(2)}) collective-permute-start(bf16[64,640]{1,0:T(8,128)(2,1)S(1)} %get-tuple-element.35), channel_id=1, source_target_pairs={{16,0},{17,1},{18,2},{19,3},{20,4},{21,5},{22,6},{23,7},{24,8},{25... | collective-permute-start | bytes 245768 | tf_op jit(solution)/shard_map/ppermute | solution.py:327
  88.0 14.6 %collective-permute-start.11 = (f32[2,64,256]{2,1,0:T(8,128)S(1)}, f32[2,64,256]{2,1,0:T(8,128)S(1)}, u32[]{:S(2)}, u32[]{:S(2)}) collective-permute-start(f32[2,64,256]{2,1,0:T(8,128)S(1)} %get-tuple-element.45), channel_id=1, source_target_pairs={{15,0},{0,1},{1,2},{2,3},{3,4},{4,5},{5,6},{6,7},{7,8},{8,9},{9,10... | collective-permute-start | bytes 393224 | tf_op jit(solution)/shard_map/ppermute | solution.py:327
  102.6 7.0 %collective-permute-start.12 = (f32[64,256]{1,0:T(8,128)S(1)}, f32[64,256]{1,0:T(8,128)S(1)}, u32[]{:S(2)}, u32[]{:S(2)}) collective-permute-start(f32[64,256]{1,0:T(8,128)S(1)} %fusion.1), channel_id=1, source_target_pairs={{240,0},{241,1},{242,2},{243,3},{244,4},{245,5},{246,6},{247,7},{2... | collective-permute-start | bytes 196616 | tf_op jit(solution)/shard_map/ppermute | solution.py:327
  114.1 37.6 %collective-permute-start.30 = (f32[2,64,256]{2,1,0:T(8,128)S(1)}, f32[2,64,256]{2,1,0:T(8,128)S(1)}, u32[]{:S(2)}, u32[]{:S(2)}) collective-permute-start(f32[2,64,256]{2,1,0:T(8,128)S(1)} %pad_maximum_fusion), channel_id=1, source_target_pairs={{1,0},{2,1},{3,2},{4,3},{5,4},{6,5},{7,6},{8,7},{9,8},{10,9},{11,1... | collective-permute-start | bytes 393224 | tf_op jit(solution)/shard_map/ppermute | solution.py:327
  114.2 10.0 %collective-permute-start.13 = (f32[2,256]{1,0:T(2,128)S(1)}, f32[2,256]{1,0:T(2,128)S(1)}, u32[]{:S(2)}, u32[]{:S(2)}) collective-permute-start(f32[2,256]{1,0:T(2,128)S(1)} %get-tuple-element.47), channel_id=1, source_target_pairs={{48,0},{49,1},{50,2},{51,3},{52,4},{53,5},{54,6},{55,7},{56,8},{57... | collective-permute-start | bytes 6152 | tf_op jit(solution)/shard_map/ppermute | solution.py:354
  125.3 5.4 %collective-permute-start.15 = (f32[2,256]{1,0:T(2,128)S(1)}, f32[2,256]{1,0:T(2,128)S(1)}, u32[]{:S(2)}, u32[]{:S(2)}) collective-permute-start(f32[2,256]{1,0:T(2,128)S(1)} %add.63), channel_id=1, source_target_pairs={{50,0},{51,1},{48,2},{49,3},{54,4},{55,5},{52,6},{53,7},{58,8},{59... | collective-permute-start | bytes 6152 | tf_op jit(solution)/shard_map/ppermute | solution.py:354
  137.9 4.8 %collective-permute-start.18 = (f32[2,256]{1,0:T(2,128)S(1)}, f32[2,256]{1,0:T(2,128)S(1)}, u32[]{:S(2)}, u32[]{:S(2)}) collective-permute-start(f32[2,256]{1,0:T(2,128)S(1)} %add.66), channel_id=1, source_target_pairs={{12,0},{13,1},{14,2},{15,3},{8,4},{9,5},{10,6},{11,7},{4,8},{5,9},... | collective-permute-start | bytes 6152 | tf_op jit(solution)/shard_map/ppermute | solution.py:354
  146.2 4.8 %collective-permute-start.20 = (f32[2,256]{1,0:T(2,128)S(1)}, f32[2,256]{1,0:T(2,128)S(1)}, u32[]{:S(2)}, u32[]{:S(2)}) collective-permute-start(f32[2,256]{1,0:T(2,128)S(1)} %add.68.part), channel_id=1, source_target_pairs={{192,0},{193,1},{194,2},{195,3},{196,4},{197,5},{198,6},{199,7},{2... | collective-permute-start | bytes 6152 | tf_op jit(solution)/shard_map/ppermute | solution.py:354
  153.7 11.4 %collective-permute-start.31 = (f32[2,64,256]{2,1,0:T(8,128)S(1)}, f32[2,64,256]{2,1,0:T(8,128)S(1)}, u32[]{:S(2)}, u32[]{:S(2)}) collective-permute-start(f32[2,64,256]{2,1,0:T(8,128)S(1)} %get-tuple-element.53), channel_id=1, source_target_pairs={{15,0},{0,1},{1,2},{2,3},{3,4},{4,5},{5,6},{6,7},{7,8},{8,9},{9,10... | collective-permute-start | bytes 393224 | tf_op jit(solution)/shard_map/ppermute | solution.py:327
  165.1 31.8 %collective-permute-start.32 = (f32[64,256]{1,0:T(8,128)S(1)}, f32[64,256]{1,0:T(8,128)S(1)}, u32[]{:S(2)}, u32[]{:S(2)}) collective-permute-start(f32[64,256]{1,0:T(8,128)S(1)} %fusion), channel_id=1, source_target_pairs={{240,0},{241,1},{242,2},{243,3},{244,4},{245,5},{246,6},{247,7},{2... | collective-permute-start | bytes 196616 | tf_op jit(solution)/shard_map/ppermute | solution.py:327
  168.9 4.8 %collective-permute-start.22 = (f32[1,256]{1,0:T(1,128)S(1)}, f32[1,256]{1,0:T(1,128)S(1)}, u32[]{:S(2)}, u32[]{:S(2)}) collective-permute-start(f32[1,256]{1,0:T(1,128)S(1)} %add.69), channel_id=1, source_target_pairs={{12,0},{13,1},{14,2},{15,3},{8,4},{9,5},{10,6},{11,7},{4,8},{5,9},... | collective-permute-start | bytes 3080 | tf_op jit(solution)/shard_map/ppermute | solution.py:354
  173.7 5.4 %collective-permute-start.23 = (f32[1,256]{1,0:T(1,128)S(1)}, f32[1,256]{1,0:T(1,128)S(1)}, u32[]{:S(2)}, u32[]{:S(2)}) collective-permute-start(f32[1,256]{1,0:T(1,128)S(1)} %add.70), channel_id=1, source_target_pairs={{48,0},{49,1},{50,2},{51,3},{52,4},{53,5},{54,6},{55,7},{56,8},{57... | collective-permute-start | bytes 3080 | tf_op jit(solution)/shard_map/ppermute | solution.py:354
  180.2 4.8 %collective-permute-start.25 = (f32[1,256]{1,0:T(1,128)S(1)}, f32[1,256]{1,0:T(1,128)S(1)}, u32[]{:S(2)}, u32[]{:S(2)}) collective-permute-start(f32[1,256]{1,0:T(1,128)S(1)} %add.72), channel_id=1, source_target_pairs={{50,0},{51,1},{48,2},{49,3},{54,4},{55,5},{52,6},{53,7},{58,8},{59... | collective-permute-start | bytes 3080 | tf_op jit(solution)/shard_map/ppermute | solution.py:354
  192.1 4.8 %collective-permute-start.28 = (f32[1,256]{1,0:T(1,128)S(1)}, f32[1,256]{1,0:T(1,128)S(1)}, u32[]{:S(2)}, u32[]{:S(2)}) collective-permute-start(f32[1,256]{1,0:T(1,128)S(1)} %add.75.part), channel_id=1, source_target_pairs={{192,0},{193,1},{194,2},{195,3},{196,4},{197,5},{198,6},{199,7},{2... | collective-permute-start | bytes 3080 | tf_op jit(solution)/shard_map/ppermute | solution.py:354
  (19 other events, 148.8 us)
